TPU v7x, 32 devices: a whole 2x2x4 slice. The times are simulated.
32 devices in a mesh: seq: 4 (over x, core), fsdp: 8 (over z, y).
Axes of the slice: x: 2, y: 2, z: 4, core: 2. Of those that a mesh axis runs over, the one named last changes fastest.
Arguments:
- tokens: bfloat16 [8, 1536, 1536], P('fsdp', 'seq'), may hold values from -6 to 6
- out_grad: bfloat16 [8, 1536, 1536], P('fsdp', 'seq'), may hold values from -6 to 6
- attn_gain: bfloat16 [1536], P('fsdp'), may hold values from 0.5 to 1.5
- w_query: bfloat16 [1536, 768], P('fsdp'), may hold values from -0.0390625 to 0.0390625
- w_key: bfloat16 [1536, 768], P('fsdp'), may hold values from -0.15625 to 0.15625
- w_value: bfloat16 [1536, 768], P('fsdp'), may hold values from -0.15625 to 0.15625
- w_out: bfloat16 [768, 1536], P('fsdp'), may hold values from -0.875 to 0.875
- mix_gain: bfloat16 [1536], P('fsdp'), may hold values from 0.5 to 1.5
- w_gate: bfloat16 [1536, 3968], P('fsdp'), may hold values from -0.15625 to 0.15625
- w_up: bfloat16 [1536, 3968], P('fsdp'), may hold values from -0.15625 to 0.15625
- w_down: bfloat16 [3968, 1536], P('fsdp'), may hold values from -0.09375 to 0.09375
- rel_table: float32 [32, 12], replicated, may hold values from -4 to 4
- bucket_ids: int32 [3071], replicated, may hold values from 0 to 31
- cont_start: int32 [8, 2], P('fsdp'), may hold values from 1024 to 1279
Outputs:
- block_out: bfloat16 [8, 1536, 1536], P('fsdp', 'seq')
- in_grad: bfloat16 [8, 1536, 1536], P('fsdp', 'seq')
- attn_gain_grad: float32 [1536], P('fsdp')
- w_query_grad: float32 [1536, 768], P('fsdp')
- w_key_grad: float32 [1536, 768], P('fsdp')
- w_value_grad: float32 [1536, 768], P('fsdp')
- w_out_grad: float32 [768, 1536], P('fsdp')
- mix_gain_grad: float32 [1536], P('fsdp')
- w_gate_grad: float32 [1536, 3968], P('fsdp')
- w_up_grad: float32 [1536, 3968], P('fsdp')
- w_down_grad: float32 [3968, 1536], P('fsdp')
- rel_table_grad: float32 [32, 12], replicated
Inputs may be any that keep to these rules, and one draw needn't show every extreme that they name: `cont_start`: a continuation's positions lie after all 1024 positions of the prompt.
All inputs are finite; a program needn't handle non-finite values.
Results may differ from a plain program's by a relative error of at most 0.018.
Values may be sent and summed in bfloat16 or wider, within the bound.
A program may use at most 320 MiB of HBM per device.

v0:
```python
import jax
import jax.numpy as jnp
from jax import lax
from jax.sharding import PartitionSpec as P

HEAD_DIM = 64
PROMPT = 1024
CL = 256


precise = lax.Precision.HIGHEST
epsilon = 1e-06


def rms_scaled(v, gain):
    return v * lax.rsqrt(jnp.mean(v * v, axis=-1, keepdims=True) + epsilon) * gain


def gelu_tanh(v):
    return 0.5 * v * (1.0 + jnp.tanh(0.7978845608028654 * (v + 0.044715 * v * v * v)))


def skew_bias(by_offset, base, count, cols):
    heads = by_offset.shape[0]
    length = count + cols - 1
    piece = lax.dynamic_slice_in_dim(by_offset, base, length, 1)
    tiled = jnp.tile(piece, (1, count))
    flat = tiled[:, count - 1 : count - 1 + count * (length - 1)]
    return flat.reshape(heads, count, length - 1)[:, :, :cols]


def skew_grad(grad, count, cols):
    heads = grad.shape[0]
    length = count + cols - 1
    padded = jnp.pad(grad, ((0, 0), (0, 0), (0, length - 1 - cols)))
    flat = padded.reshape(heads, count * (length - 1))
    placed = jnp.pad(flat, ((0, 0), (count - 1, 1)))
    return jnp.sum(placed.reshape(heads, count, length), axis=1)


def add_at(total, part, base):
    current = lax.dynamic_slice_in_dim(total, base, part.shape[1], 1)
    return lax.dynamic_update_slice_in_dim(total, current + part, base, 1)


def prompt_forward(query, keys, values, bias):
    scores = jnp.einsum("rhe,she->hrs", query, keys, preferred_element_type=jnp.float32) + bias
    top = jnp.max(scores, axis=-1, keepdims=True)
    expd = jnp.exp(scores - top)
    total = jnp.sum(expd, axis=-1, keepdims=True)
    weights = (expd / total).astype(jnp.bfloat16)
    result = jnp.einsum("hrs,she->rhe", weights, values, preferred_element_type=jnp.float32)
    return (result, top + jnp.log(total))


def prompt_backward(query, keys, values, bias, logsum, result_grad):
    scores = jnp.einsum("rhe,she->hrs", query, keys, preferred_element_type=jnp.float32) + bias
    probs = jnp.exp(scores - logsum)
    value_grad = jnp.einsum(
        "hrs,rhe->she", probs.astype(jnp.bfloat16), result_grad, preferred_element_type=jnp.float32
    )
    prob_grad = jnp.einsum("rhe,she->hrs", result_grad, values, preferred_element_type=jnp.float32)
    score_grad = probs * (prob_grad - jnp.sum(prob_grad * probs, axis=-1, keepdims=True))
    score_low = score_grad.astype(jnp.bfloat16)
    query_grad = jnp.einsum("hrs,she->rhe", score_low, keys, preferred_element_type=jnp.float32)
    key_grad = jnp.einsum("hrs,rhe->she", score_low, query, preferred_element_type=jnp.float32)
    return (query_grad, key_grad, value_grad, score_low.astype(jnp.float32))


def cont_scores(query, keys, prompt_keys, bias_far, bias_near):
    far = (
        jnp.einsum("crhe,she->hcrs", query, prompt_keys, preferred_element_type=jnp.float32)
        + bias_far
    )
    near = (
        jnp.einsum("crhe,cshe->hcrs", query, keys, preferred_element_type=jnp.float32)
        + bias_near[:, None]
    )
    return (far, near)


def cont_forward(query, keys, values, prompt_keys, prompt_values, bias_far, bias_near):
    far, near = cont_scores(query, keys, prompt_keys, bias_far, bias_near)
    top = jnp.maximum(jnp.max(far, axis=-1, keepdims=True), jnp.max(near, axis=-1, keepdims=True))
    exp_far = jnp.exp(far - top)
    exp_near = jnp.exp(near - top)
    total = jnp.sum(exp_far, axis=-1, keepdims=True) + jnp.sum(exp_near, axis=-1, keepdims=True)
    weight_far = (exp_far / total).astype(jnp.bfloat16)
    weight_near = (exp_near / total).astype(jnp.bfloat16)
    result = jnp.einsum(
        "hcrs,she->crhe", weight_far, prompt_values, preferred_element_type=jnp.float32
    )
    result = result + jnp.einsum(
        "hcrs,cshe->crhe", weight_near, values, preferred_element_type=jnp.float32
    )
    return (result, top + jnp.log(total))


def cont_backward(
    query, keys, values, prompt_keys, prompt_values, bias_far, bias_near, logsum, result_grad
):
    far, near = cont_scores(query, keys, prompt_keys, bias_far, bias_near)
    prob_far = jnp.exp(far - logsum)
    prob_near = jnp.exp(near - logsum)
    grad_far = jnp.einsum(
        "crhe,she->hcrs", result_grad, prompt_values, preferred_element_type=jnp.float32
    )
    grad_near = jnp.einsum(
        "crhe,cshe->hcrs", result_grad, values, preferred_element_type=jnp.float32
    )
    inner_sum = jnp.sum(grad_far * prob_far, axis=-1, keepdims=True) + jnp.sum(
        grad_near * prob_near, axis=-1, keepdims=True
    )
    score_far = (prob_far * (grad_far - inner_sum)).astype(jnp.bfloat16)
    score_near = (prob_near * (grad_near - inner_sum)).astype(jnp.bfloat16)
    query_grad = jnp.einsum(
        "hcrs,she->crhe", score_far, prompt_keys, preferred_element_type=jnp.float32
    )
    query_grad = query_grad + jnp.einsum(
        "hcrs,cshe->crhe", score_near, keys, preferred_element_type=jnp.float32
    )
    prompt_key_grad = jnp.einsum(
        "hcrs,crhe->she", score_far, query, preferred_element_type=jnp.float32
    )
    prompt_value_grad = jnp.einsum(
        "hcrs,crhe->she",
        prob_far.astype(jnp.bfloat16),
        result_grad,
        preferred_element_type=jnp.float32,
    )
    key_grad = jnp.einsum("hcrs,crhe->cshe", score_near, query, preferred_element_type=jnp.float32)
    value_grad = jnp.einsum(
        "hcrs,crhe->cshe",
        prob_near.astype(jnp.bfloat16),
        result_grad,
        preferred_element_type=jnp.float32,
    )
    return (
        query_grad,
        key_grad,
        value_grad,
        prompt_key_grad,
        prompt_value_grad,
        score_far.astype(jnp.float32),
        score_near.astype(jnp.float32),
    )


def body(
    tokens,
    out_grad,
    attn_gain,
    w_query,
    w_key,
    w_value,
    w_out,
    mix_gain,
    w_gate,
    w_up,
    w_down,
    rel_table,
    bucket_ids,
    cont_start,
):
    block = tokens[0].astype(jnp.float32)
    rows, width = block.shape
    nseq = lax.axis_size("seq")
    nfsdp = lax.axis_size("fsdp")
    gain_one, query_w, key_w, value_w, out_w = (
        lax.all_gather(attn_gain, "fsdp", axis=0, tiled=True),
        lax.all_gather(w_query, "fsdp", axis=0, tiled=True),
        lax.all_gather(w_key, "fsdp", axis=0, tiled=True),
        lax.all_gather(w_value, "fsdp", axis=0, tiled=True),
        lax.all_gather(w_out, "fsdp", axis=0, tiled=True),
    )
    inner = query_w.shape[1]
    piece_w = inner // nseq
    heads_dev = piece_w // HEAD_DIM
    gain_one_f = gain_one.astype(jnp.float32)
    normed = rms_scaled(block, gain_one_f).astype(jnp.bfloat16)
    query = jnp.dot(normed, query_w, preferred_element_type=jnp.float32).astype(jnp.bfloat16)
    keys = jnp.dot(normed, key_w, preferred_element_type=jnp.float32).astype(jnp.bfloat16)
    values = jnp.dot(normed, value_w, preferred_element_type=jnp.float32).astype(jnp.bfloat16)
    packed = jnp.stack((query, keys, values), axis=1).reshape(rows, 3, nseq, piece_w)
    by_head = lax.all_to_all(packed, "seq", split_axis=2, concat_axis=0, tiled=True)
    group_rows = by_head.shape[0]
    by_head = by_head.reshape(group_rows, 3, heads_dev, HEAD_DIM)
    query_h = by_head[:, 0]
    keys_h = by_head[:, 1]
    values_h = by_head[:, 2]
    mine = lax.axis_index("seq")
    buckets = rel_table.shape[0]
    span_len = bucket_ids.shape[0]
    table_mine = lax.dynamic_slice_in_dim(rel_table, mine * heads_dev, heads_dev, 1)
    bucket_hot = (bucket_ids[:, None] == jnp.arange(buckets, dtype=jnp.int32)[None, :]).astype(
        jnp.float32
    )
    by_offset = jnp.dot(table_mine.T, bucket_hot.T, precision=precise)
    maxpos = (span_len + 1) // 2
    cont_count = cont_start.shape[1]
    starts = cont_start[0]
    block_rows = min(512, PROMPT)
    prompt_blocks = PROMPT // block_rows
    q_prompt = query_h[:PROMPT]
    k_prompt = keys_h[:PROMPT]
    v_prompt = values_h[:PROMPT]
    q_cont = query_h[PROMPT:].reshape(cont_count, CL, heads_dev, HEAD_DIM)
    k_cont = keys_h[PROMPT:].reshape(cont_count, CL, heads_dev, HEAD_DIM)
    v_cont = values_h[PROMPT:].reshape(cont_count, CL, heads_dev, HEAD_DIM)
    bias_near = skew_bias(by_offset, maxpos - CL, CL, CL)

    def prompt_bias_of(index):
        return skew_bias(
            by_offset, maxpos - 1 - index * block_rows - (block_rows - 1), block_rows, PROMPT
        )

    def far_base(which):
        return maxpos - 1 - starts[which] - (CL - 1)

    def far_bias_of(first):
        return jnp.stack(
            [skew_bias(by_offset, far_base(first + j), CL, PROMPT) for j in range(2)], axis=1
        )

    prompt_outs = []
    prompt_lse = []
    for index in range(prompt_blocks):
        first = index * block_rows
        result, logsum = prompt_forward(
            q_prompt[first : first + block_rows], k_prompt, v_prompt, prompt_bias_of(index)
        )
        prompt_outs.append(result)
        prompt_lse.append(logsum)
    index = 0
    first = 2 * index
    result, logsum = cont_forward(
        q_cont, k_cont, v_cont, k_prompt, v_prompt, far_bias_of(first), bias_near
    )
    cont_outs = result
    cont_lse = [logsum]
    out_prompt = jnp.concatenate(prompt_outs, axis=0).reshape(PROMPT, piece_w)
    out_cont = cont_outs.reshape(cont_count * CL, piece_w)
    out_heads = jnp.concatenate([out_prompt, out_cont], axis=0)
    out_heads = out_heads.astype(jnp.bfloat16).reshape(group_rows, 1, piece_w)
    mixed = lax.all_to_all(out_heads, "seq", split_axis=0, concat_axis=1, tiled=True).reshape(
        rows, inner
    )
    resid = block + jnp.dot(mixed, out_w, preferred_element_type=jnp.float32)
    gain_two, gate_w, up_w, down_w = (
        lax.all_gather(mix_gain, "fsdp", axis=0, tiled=True),
        lax.all_gather(w_gate, "fsdp", axis=0, tiled=True),
        lax.all_gather(w_up, "fsdp", axis=0, tiled=True),
        lax.all_gather(w_down, "fsdp", axis=0, tiled=True),
    )
    gain_two_f = gain_two.astype(jnp.float32)
    normed_two = rms_scaled(resid, gain_two_f).astype(jnp.bfloat16)
    gate = jnp.dot(normed_two, gate_w, preferred_element_type=jnp.float32)
    upward = jnp.dot(normed_two, up_w, preferred_element_type=jnp.float32)
    active = gelu_tanh(gate)
    hidden = (active * upward).astype(jnp.bfloat16)
    result = resid + jnp.dot(hidden, down_w, preferred_element_type=jnp.float32)
    block_out = result.astype(jnp.bfloat16)[None]
    cot = out_grad[0]
    cot_f = cot.astype(jnp.float32)
    down_grad = jnp.dot(hidden.T, cot, preferred_element_type=jnp.float32)
    hidden_grad = jnp.dot(cot, down_w.T, preferred_element_type=jnp.float32)
    _, gelu_pull = jax.vjp(gelu_tanh, gate)
    gate_grad = gelu_pull(hidden_grad * upward)[0].astype(jnp.bfloat16)
    up_grad = (hidden_grad * active).astype(jnp.bfloat16)
    gate_w_grad = jnp.dot(normed_two.T, gate_grad, preferred_element_type=jnp.float32)
    up_w_grad = jnp.dot(normed_two.T, up_grad, preferred_element_type=jnp.float32)
    normed_two_grad = jnp.dot(gate_grad, gate_w.T, preferred_element_type=jnp.float32) + jnp.dot(
        up_grad, up_w.T, preferred_element_type=jnp.float32
    )
    _, norm_two_pull = jax.vjp(rms_scaled, resid, gain_two_f)
    resid_norm_grad, gain_two_grad = norm_two_pull(normed_two_grad)
    resid_grad = cot_f + resid_norm_grad
    attn_grad = resid_grad.astype(jnp.bfloat16)
    out_w_grad = jnp.dot(mixed.T, attn_grad, preferred_element_type=jnp.float32)
    mixed_grad = jnp.dot(attn_grad, out_w.T, preferred_element_type=jnp.float32).astype(
        jnp.bfloat16
    )
    grad_heads = lax.all_to_all(
        mixed_grad.reshape(rows, 1, nseq, piece_w), "seq", split_axis=2, concat_axis=0, tiled=True
    )
    grad_heads = grad_heads.reshape(group_rows, heads_dev, HEAD_DIM)
    grad_prompt = grad_heads[:PROMPT]
    grad_cont = grad_heads[PROMPT:].reshape(cont_count, CL, heads_dev, HEAD_DIM)
    offset_grad = jnp.zeros((heads_dev, span_len), jnp.float32)
    dk_prompt = jnp.zeros((PROMPT, heads_dev, HEAD_DIM), jnp.float32)
    dv_prompt = jnp.zeros((PROMPT, heads_dev, HEAD_DIM), jnp.float32)
    dq_blocks = []
    for index in range(prompt_blocks):
        first = index * block_rows
        dq_part, dk_part, dv_part, score_part = prompt_backward(
            q_prompt[first : first + block_rows],
            k_prompt,
            v_prompt,
            prompt_bias_of(index),
            prompt_lse[index],
            grad_prompt[first : first + block_rows],
        )
        dq_blocks.append(dq_part)
        dk_prompt = dk_prompt + dk_part
        dv_prompt = dv_prompt + dv_part
        offset_grad = add_at(
            offset_grad,
            skew_grad(score_part, block_rows, PROMPT),
            maxpos - 1 - first - (block_rows - 1),
        )
    index = 0
    first = 2 * index
    dq_part, dk_part, dv_part, pk_part, pv_part, far_part, near_part = cont_backward(
        q_cont,
        k_cont,
        v_cont,
        k_prompt,
        v_prompt,
        far_bias_of(first),
        bias_near,
        cont_lse[index],
        grad_cont,
    )
    dq_pairs = [dq_part]
    dk_pairs = [dk_part]
    dv_pairs = [dv_part]
    dk_prompt = dk_prompt + pk_part
    dv_prompt = dv_prompt + pv_part
    near_total = jnp.sum(near_part, axis=1)
    for j in range(2):
        offset_grad = add_at(
            offset_grad, skew_grad(far_part[:, j], CL, PROMPT), far_base(first + j)
        )
    offset_grad = add_at(offset_grad, skew_grad(near_total, CL, CL), maxpos - CL)

    def join(prompt_part, cont_parts):
        return jnp.concatenate(
            [prompt_part.reshape(PROMPT, piece_w), cont_parts[0].reshape(cont_count * CL, piece_w)],
            axis=0,
        )

    dq_prompt = jnp.concatenate(dq_blocks, axis=0)
    qkv_grad = jnp.stack(
        (join(dq_prompt, dq_pairs), join(dk_prompt, dk_pairs), join(dv_prompt, dv_pairs)), axis=1
    )
    qkv_grad = qkv_grad.astype(jnp.bfloat16).reshape(group_rows, 3, 1, piece_w)
    qkv_tok = lax.all_to_all(qkv_grad, "seq", split_axis=0, concat_axis=2, tiled=True).reshape(
        rows, 3, inner
    )
    query_grad = qkv_tok[:, 0]
    key_grad = qkv_tok[:, 1]
    value_grad = qkv_tok[:, 2]
    query_w_grad = jnp.dot(normed.T, query_grad, preferred_element_type=jnp.float32)
    key_w_grad = jnp.dot(normed.T, key_grad, preferred_element_type=jnp.float32)
    value_w_grad = jnp.dot(normed.T, value_grad, preferred_element_type=jnp.float32)
    normed_grad = jnp.dot(query_grad, query_w.T, preferred_element_type=jnp.float32)
    normed_grad = normed_grad + jnp.dot(key_grad, key_w.T, preferred_element_type=jnp.float32)
    normed_grad = normed_grad + jnp.dot(value_grad, value_w.T, preferred_element_type=jnp.float32)
    _, norm_one_pull = jax.vjp(rms_scaled, block, gain_one_f)
    block_norm_grad, gain_one_grad = norm_one_pull(normed_grad)
    in_grad = (resid_grad + block_norm_grad).astype(jnp.bfloat16)[None]
    table_part = jnp.dot(bucket_hot.T, offset_grad.T, precision=precise)
    table_full = jnp.zeros((buckets, nseq, heads_dev), jnp.float32)
    table_full = lax.dynamic_update_slice(
        table_full, table_part[:, None, :], (jnp.int32(0), mine, jnp.int32(0))
    )
    table_grad, gain_one_all, gain_two_all = lax.psum(
        (table_full.reshape(buckets, nseq * heads_dev), gain_one_grad, gain_two_grad),
        ("seq", "fsdp"),
    )
    share = width // nfsdp
    findex = lax.axis_index("fsdp")
    gain_one_share = lax.dynamic_slice_in_dim(gain_one_all, findex * share, share)
    gain_two_share = lax.dynamic_slice_in_dim(gain_two_all, findex * share, share)
    shares = (
        lax.psum_scatter(query_w_grad, "fsdp", scatter_dimension=0, tiled=True),
        lax.psum_scatter(key_w_grad, "fsdp", scatter_dimension=0, tiled=True),
        lax.psum_scatter(value_w_grad, "fsdp", scatter_dimension=0, tiled=True),
        lax.psum_scatter(out_w_grad, "fsdp", scatter_dimension=0, tiled=True),
        lax.psum_scatter(gate_w_grad, "fsdp", scatter_dimension=0, tiled=True),
        lax.psum_scatter(up_w_grad, "fsdp", scatter_dimension=0, tiled=True),
        lax.psum_scatter(down_grad, "fsdp", scatter_dimension=0, tiled=True),
    )
    summed = (
        lax.psum(shares[0].astype(jnp.bfloat16), "seq").astype(jnp.float32),
        lax.psum(shares[1].astype(jnp.bfloat16), "seq").astype(jnp.float32),
        lax.psum(shares[2].astype(jnp.bfloat16), "seq").astype(jnp.float32),
        lax.psum(shares[3].astype(jnp.bfloat16), "seq").astype(jnp.float32),
        lax.psum(shares[4].astype(jnp.bfloat16), "seq").astype(jnp.float32),
        lax.psum(shares[5].astype(jnp.bfloat16), "seq").astype(jnp.float32),
        lax.psum(shares[6].astype(jnp.bfloat16), "seq").astype(jnp.float32),
    )
    return (
        block_out,
        in_grad,
        gain_one_share,
        summed[0],
        summed[1],
        summed[2],
        summed[3],
        gain_two_share,
        summed[4],
        summed[5],
        summed[6],
        table_grad,
    )


def solution(mesh):
    placed = (
        P("fsdp", "seq", None),
        P("fsdp", "seq", None),
        P("fsdp"),
        P("fsdp", None),
        P("fsdp", None),
        P("fsdp", None),
        P("fsdp", None),
        P("fsdp"),
        P("fsdp", None),
        P("fsdp", None),
        P("fsdp", None),
        P(),
        P(),
        P("fsdp", None),
    )
    return jax.shard_map(
        body,
        mesh=mesh,
        in_specs=placed,
        out_specs=(
            P("fsdp", "seq", None),
            P("fsdp", "seq", None),
            P("fsdp"),
            P("fsdp", None),
            P("fsdp", None),
            P("fsdp", None),
            P("fsdp", None),
            P("fsdp"),
            P("fsdp", None),
            P("fsdp", None),
            P("fsdp", None),
            P(),
        ),
        check_vma=False,
    )
```

profile of v0, /device:TPU:0, one launch (start us, length us, event | category | flops | bytes accessed | tf_op | source)
XLA Modules:
  0.0 2506.5 jit_solution(9280838060224856793)
XLA Ops:
  13.7 23.8 all-reduce.14
  38.8 26.5 %all-gather.10.cloned.1.call-done = bf16[1536,768]{1,0:T(8,128)(2,1)} async-done(((bf16[192,768]{1,0:T(8,128)(2,1)}), bf16[1536,768]{1,0:T(8,128)(2,1)}) %all-gather.10.cloned.1.call-update) | async-done | bytes 2359312 | tf_op jit(solution)/shard_map/all_gather | solution.py:172
  68.4 49.7 %all-gather.12.cloned.1.call-done = bf16[1536,768]{1,0:T(8,128)(2,1)} async-done(((bf16[192,768]{1,0:T(8,128)(2,1)}), bf16[1536,768]{1,0:T(8,128)(2,1)}) %all-gather.12.cloned.1.call-update) | async-done | bytes 2359312 | tf_op jit(solution)/shard_map/all_gather | solution.py:173
  121.2 49.7 %all-gather.8.cloned.1.call-done = bf16[1536,768]{1,0:T(8,128)(2,1)} async-done(((bf16[192,768]{1,0:T(8,128)(2,1)}), bf16[1536,768]{1,0:T(8,128)(2,1)}) %all-gather.8.cloned.1.call-update) | async-done | bytes 2359312 | tf_op jit(solution)/shard_map/all_gather | solution.py:171
  198.7 9.2 tile.25
  215.5 10.0 reshape.413
  227.7 9.1 tile.27
  243.9 10.0 reshape.414
  258.7 15.4 reshape.467
  274.2 13.2 tile.21
  287.3 13.9 slice.162
  301.2 13.3 reshape.469
  314.5 11.0 reshape.410
  330.2 15.6 reshape.463
  345.8 13.2 tile.23
  359.0 13.5 slice.165
  372.5 13.2 reshape.465
  385.7 11.0 reshape.411
  473.6 11.6 fusion.157
  485.3 82.5 %all-gather.16.cloned.1.call-done = bf16[1536,3968]{1,0:T(8,128)(2,1)} async-done(((bf16[192,3968]{1,0:T(8,128)(2,1)}), bf16[1536,3968]{1,0:T(8,128)(2,1)}) %all-gather.16.cloned.1.call-update) | async-done | bytes 12189712 | tf_op jit(solution)/shard_map/all_gather | solution.py:251
  567.8 11.6 fusion.156
  579.4 160.4 %all-gather.20.cloned.1.call-done = bf16[3968,1536]{1,0:T(8,128)(2,1)} async-done(((bf16[496,1536]{1,0:T(8,128)(2,1)}), bf16[3968,1536]{1,0:T(8,128)(2,1)}) %all-gather.20.cloned.1.call-update) | async-done | bytes 12189712 | tf_op jit(solution)/shard_map/all_gather | solution.py:253
  739.8 17.2 multiply_convert_fusion.3
  757.1 9.2 fusion.158
  766.4 9.2 multiply_reduce_fusion.3
  840.4 42.3 %all_to_all.60 = bf16[1536,3,1,192]{3,1,2,0:T(4,128)(2,1)} all-to-all(bf16[1536,3,1,192]{3,1,2,0:T(4,128)(2,1)} %copy.265), channel_id=1, replica_groups=mesh['seq'=4,'fsdp'=8] {'seq'}, dimensions={0} | all-to-all | bytes 3538944 | tf_op jit(solution)/shard_map/all_to_all | solution.py:347
  903.6 13.1 fusion.62
  918.0 13.6 fusion.160
  931.7 13.4 fusion.159
  946.8 10.1 fusion.31
  979.8 9.1 reshape.437
  996.4 9.9 reshape.438
  1010.9 9.1 reshape.435
  1027.5 9.6 reshape.436
  1042.8 9.7 reshape.475
  1062.0 10.2 reshape.471
  1079.2 9.8 pad_convert_fusion.1
  1089.0 13.2 reshape.473
  1102.2 15.6 reshape.444
  1122.2 10.0 pad_convert_fusion
  1132.2 13.3 reshape.477
  1145.5 15.7 reshape.446
  1172.6 11.8 reduce-scatter.8.cloned.1.call-done
  1186.2 394.1 %reduce-scatter.20.cloned.1.call-done = f32[496,1536]{1,0:T(8,128)} async-done(((f32[3968,1536]{1,0:T(8,128)}), f32[496,1536]{1,0:T(8,128)}) %reduce-scatter.20.cloned.1.call-update) | async-done | bytes 3047440 | tf_op jit(solution)/shard_map/reduce_scatter | solution.py:382
  1583.5 392.2 %reduce-scatter.18.cloned.1.call-done = f32[192,3968]{1,0:T(8,128)} async-done(((f32[1536,3968]{1,0:T(8,128)}), f32[192,3968]{1,0:T(8,128)}) %reduce-scatter.18.cloned.1.call-update) | async-done | bytes 3047440 | tf_op jit(solution)/shard_map/reduce_scatter | solution.py:381
  1978.9 392.1 %reduce-scatter.16.cloned.1.call-done = f32[192,3968]{1,0:T(8,128)} async-done(((f32[1536,3968]{1,0:T(8,128)}), f32[192,3968]{1,0:T(8,128)}) %reduce-scatter.16.cloned.1.call-update) | async-done | bytes 3047440 | tf_op jit(solution)/shard_map/reduce_scatter | solution.py:380
  2386.6 41.0 %all-reduce.13 = (f32[1536]{0:T(1024)}, f32[1536]{0:T(1024)}, f32[32,12]{0,1:T(8,128)}) all-reduce(f32[1536]{0:T(1024)} %get-tuple-element.14, f32[1536]{0:T(1024)} %get-tuple-element.12, f32[32,12]{0,1:T(8,128)} %reshape.441), channel_id=1, replica_groups=mesh['seq'=4,'fsdp'=8] {'seq','fsdp'}, use_global_device_ids=true, to_apply=%region_17.18 | all-reduce | flops 3456 | bytes 27648 | tf_op jit(solution)/shard_map/psum | solution.py:367
  2434.2 53.3 %all-reduce.18.cloned.1.call-done = (bf16[192,768]{1,0:T(8,128)(2,1)}, bf16[192,768]{1,0:T(8,128)(2,1)}, bf16[192,768]{1,0:T(8,128)(2,1)}, bf16[96,1536]{1,0:T(8...) async-done(((bf16[192,768]{1,0:T(8,128)(2,1)}, bf16[192,768]{1,0:T(8,128)(2,1)}, bf16[192,768]{1,0:T(8,128)(2,1)}, ...) | async-done | bytes 5750800 | tf_op jit(solution)/shard_map/psum | solution.py:385
  (357 shorter events, 352.5 us)
Async XLA Ops:
  7.2 30.7 %copy-start = (f32[32,12]{0,1:T(8,128)S(1)}, f32[32,12]{0,1:T(8,128)}, u32[]{:S(2)}) copy-start(f32[32,12]{0,1:T(8,128)} %param.25) | copy-start | bytes 4612
  7.2 58.1 %all-gather.10.cloned.1.call-start = ((), (), s32[]{:S(2)}) async-start(), calls=%async_computation.12 | async-start | bytes 2654208 | tf_op jit(solution)/shard_map/all_gather | solution.py:172
  7.9 110.2 %all-gather.12.cloned.1.call-start = ((), (), s32[]{:S(2)}) async-start(), calls=%async_computation.13 | async-start | bytes 2654208 | tf_op jit(solution)/shard_map/all_gather | solution.py:173
  8.7 162.3 %all-gather.8.cloned.1.call-start = ((), (), s32[]{:S(2)}) async-start(), calls=%async_computation.11 | async-start | bytes 2654208 | tf_op jit(solution)/shard_map/all_gather | solution.py:171
  9.4 458.6 %all-gather.14.cloned.1.call-start = ((), (), s32[]{:S(2)}) async-start(), calls=%async_computation.14 | async-start | bytes 2654208 | tf_op jit(solution)/shard_map/all_gather | solution.py:174
  10.0 27.6 %copy-start.5 = (bf16[1,384,1536]{2,1,0:T(8,128)(2,1)S(1)}, bf16[1,384,1536]{2,1,0:T(8,128)(2,1)}, u32[]{:S(2)}) copy-start(bf16[1,384,1536]{2,1,0:T(8,128)(2,1)} %param.14) | copy-start | bytes 3538948
  10.0 463.6 %all-gather.18.cloned.1.call-start = ((), (), s32[]{:S(2)}) async-start(), calls=%async_computation.16 | async-start | bytes 13713408 | tf_op jit(solution)/shard_map/all_gather | solution.py:252
  10.6 27.3 %copy-start.60 = (s32[3071]{0:T(1024)S(1)}, s32[3071]{0:T(1024)}, u32[]{:S(2)}) copy-start(s32[3071]{0:T(1024)} %param.26) | copy-start | bytes 36856
  10.6 557.1 %all-gather.16.cloned.1.call-start = ((), (), s32[]{:S(2)}) async-start(), calls=%async_computation.15 | async-start | bytes 13713408 | tf_op jit(solution)/shard_map/all_gather | solution.py:251
  11.2 728.6 %all-gather.20.cloned.1.call-start = ((), (), s32[]{:S(2)}) async-start(), calls=%async_computation.17 | async-start | bytes 13713408 | tf_op jit(solution)/shard_map/all_gather | solution.py:253
  37.6 133.4 %copy-start.35 = (f32[1536]{0:T(1024)}, f32[1536]{0:T(1024)S(1)}, u32[]{:S(2)}) copy-start(f32[1536]{0:T(1024)S(1)} %convert_element_type.184) | copy-start | bytes 18436
  37.9 30.2 %copy-start.54 = (f32[384]{0:T(512)}, f32[384]{0:T(512)S(1)}, u32[]{:S(2)}) copy-start(f32[384]{0:T(512)S(1)} %fusion.34) | copy-start | bytes 4612
  37.9 133.0 %copy-start.43 = (f32[384]{0:T(512)}, f32[384]{0:T(512)S(1)}, u32[]{:S(2)}) copy-start(f32[384]{0:T(512)S(1)} %fusion.139) | copy-start | bytes 4612
  175.7 7.9 slice-start.6
  175.7 227.7 %all-to-all-start = ((bf16[384,3,4,192]{0,3,1,2:T(8,128)(2,1)}), bf16[384,3,4,192]{0,3,1,2:T(8,128)(2,1)}, u32[]{:S(2)}, u32[]{:S(2)}) async-start(bf16[384,3,4,192]{0,3,1,2:T(8,128)(2,1)} %copy.236), calls=%async_computation | async-start | bytes 3538944 | tf_op jit(solution)/shard_map/all_to_all | solution.py:185
  243.9 10.0 copy-start.41
  411.7 6.3 copy-start.23
  411.7 6.3 copy-start.30
  413.4 9.4 copy-start.11
  428.2 7.7 copy-start.3
  428.2 7.7 copy-start.47
  429.7 6.2 copy-start.51
  446.6 13.4 all-to-all-start.1
  757.1 9.3 copy-start.14
  757.1 9.3 copy-start.27
  757.1 9.3 copy-start.49
  757.1 9.3 copy-start.53
  766.4 9.2 copy-start.57
  766.4 9.2 copy-start.22
  781.7 13.8 all-to-all-start.2
  785.8 381.3 %reduce-scatter.14.cloned.1.call-start = ((), (), s32[]{:S(2)}) async-start(), calls=%async_computation.21 | async-start | bytes 5308416 | tf_op jit(solution)/shard_map/reduce_scatter | solution.py:379
  792.4 376.5 %reduce-scatter.12.cloned.1.call-start = ((), (), s32[]{:S(2)}) async-start(), calls=%async_computation.20 | async-start | bytes 5308416 | tf_op jit(solution)/shard_map/reduce_scatter | solution.py:378
  799.6 8.3 slice-start
  801.7 6.2 slice-start.1
  813.8 8.5 slice-start.2
  821.3 14.0 copy-start.7
  890.3 7.6 copy-start.19
  894.1 276.7 %reduce-scatter.10.cloned.1.call-start = ((), (), s32[]{:S(2)}) async-start(), calls=%async_computation.19 | async-start | bytes 5308416 | tf_op jit(solution)/shard_map/reduce_scatter | solution.py:377
  897.9 286.5 %reduce-scatter.8.cloned.1.call-start = ((), (), s32[]{:S(2)}) async-start(), calls=%async_computation.18 | async-start | bytes 5308416 | tf_op jit(solution)/shard_map/reduce_scatter | solution.py:376
  901.7 678.6 %reduce-scatter.20.cloned.1.call-start = ((), (), s32[]{:S(2)}) async-start(), calls=%async_computation.24 | async-start | bytes 27426816 | tf_op jit(solution)/shard_map/reduce_scatter | solution.py:382
  916.7 1059.1 %reduce-scatter.18.cloned.1.call-start = ((), (), s32[]{:S(2)}) async-start(), calls=%async_computation.23 | async-start | bytes 27426816 | tf_op jit(solution)/shard_map/reduce_scatter | solution.py:381
  931.6 1439.4 %reduce-scatter.16.cloned.1.call-start = ((), (), s32[]{:S(2)}) async-start(), calls=%async_computation.22 | async-start | bytes 27426816 | tf_op jit(solution)/shard_map/reduce_scatter | solution.py:380
  945.1 11.7 copy-start.25
  945.1 1542.4 %all-reduce.18.cloned.1.call-start = ((), (), s32[]{:S(2)}) async-start(), calls=%async_computation.25 | async-start | bytes 11501568 | tf_op jit(solution)/shard_map/psum | solution.py:385
  1052.4 7.1 copy-start.10
  2381.8 48.5 %copy-start.55 = (f32[384]{0:T(512)S(1)}, f32[384]{0:T(512)}, u32[]{:S(2)}) copy-start(f32[384]{0:T(512)} %copy-done.54) | copy-start | bytes 4612
  2381.8 49.1 %copy-start.17 = (f32[384,1536]{1,0:T(8,128)S(1)}, f32[384,1536]{1,0:T(8,128)}, u32[]{:S(2)}) copy-start(f32[384,1536]{1,0:T(8,128)} %copy-done.16) | copy-start | bytes 7077892
  2487.5 6.5 copy-start.34
  (42 other events, 108.5 us)
Sparse Core Ops, SparseCore 0:
  10.2 55.0 all-gather.9
  67.5 50.6 all-gather.11
  120.3 50.6 all-gather.7
  173.0 50.6 all-gather.13
  225.7 170.1 all-gather.17
  397.9 169.8 all-gather.15
  570.0 169.8 all-gather.19
  792.5 93.8 reduce-scatter.13
  894.2 92.7 reduce-scatter.11
  990.5 94.9 reduce-scatter.9
  1089.2 95.1 reduce-scatter.7
  1188.2 392.0 reduce-scatter.19
  1584.3 391.4 reduce-scatter.17
  1979.6 391.4 reduce-scatter.15
  2374.9 112.5 all-reduce.17
where the time goes:
time: 2510 us
  waiting for transfers between devices  1630 us (65%)
  local copies, waits for them, and re-layouts  454 us (18%)
  matrix products  192 us (8%)
  blocking collectives  107 us (4%)
  other arithmetic  93.3 us (4%)
    reduce_scatter x1, waiting for transfers between devices, body(): lax.psum_scatter(down_grad, 'fsdp', scatter_dimension=0, tiled=True)  394 us
    reduce_scatter x1, waiting for transfers between devices, body(): lax.psum_scatter(up_w_grad, 'fsdp', scatter_dimension=0, tiled=True)  392 us
    reduce_scatter x1, waiting for transfers between devices, body(): lax.psum_scatter(gate_w_grad, 'fsdp', scatter_dimension=0, tiled=True)  392 us
    all_gather x1, waiting for transfers between devices, body(): lax.all_gather(w_down, 'fsdp', axis=0, tiled=True)  160 us
    unnamed x162, local copies, waits for them, and re-layouts  125 us
    all_gather x1, waiting for transfers between devices, body(): lax.all_gather(w_gate, 'fsdp', axis=0, tiled=True)  82.5 us
    another operation x10, local copies, waits for them, and re-layouts, skew_bias(): tiled = jnp.tile(piece, (1, count))  63.2 us
    reshape x5, local copies, waits for them, and re-layouts, skew_grad(): return jnp.sum(placed.reshape(heads, count, length), axis=1)  55.3 us
  transfers between devices with their start and end apart: 18, of which 12 were waited for; matrix products, arithmetic and copies ran while one was open for 27% of the time, Pallas kernels for 0%

commit v1 on v0

v1 whole, which is shorter than its diff:
```python
import functools
import jax
import jax.numpy as jnp
from jax import lax
from jax.experimental import pallas as pl
from jax.experimental.pallas import tpu as pltpu
from jax.sharding import PartitionSpec as P

HEAD_DIM = 64
PROMPT = 1024
CL = 256
F32 = jnp.float32
BF16 = jnp.bfloat16
epsilon = 1e-06
STRIP = 2 * PROMPT - 128
FARW = PROMPT - 128 + CL
KC = 256


def nt(a, b):
    return lax.dot_general(a, b, (((1,), (1,)), ((), ())), preferred_element_type=F32)


def nn(a, b):
    return lax.dot_general(a, b, (((1,), (0,)), ((), ())), preferred_element_type=F32)


def build_strips(heads, starts, table, ids, strip, far):
    length = ids.shape[1]
    half = 2 * PROMPT
    for h in range(heads):
        row = jnp.zeros(ids.shape, F32)
        for b in range(table.shape[0]):
            row = jnp.where(ids[...] == b, table[b, h], row)
        base = jnp.broadcast_to(row[:1, PROMPT // 2 : PROMPT // 2 + half], (128, half))
        strip[h] = pltpu.roll(base, 1, 1, stride=1, stride_axis=0)[:, 128:]
        for c in range(2):
            moved = pltpu.roll(row, length - PROMPT // 2 - starts[c], 1)
            base = jnp.broadcast_to(moved[:1, : FARW + 128], (128, FARW + 128))
            far[h, c] = pltpu.roll(base, 1, 1, stride=1, stride_axis=0)[:, 128:]


def head_masks(width, heads):
    lane = lax.broadcasted_iota(jnp.int32, (1, width), 1)
    return [(lane >= h * HEAD_DIM) & (lane < (h + 1) * HEAD_DIM) for h in range(heads)]


def masked_copies(src, dst, heads):
    masks = head_masks(src.shape[1], heads)
    for h in range(heads):
        dst[h] = jnp.where(masks[h], src[...], jnp.zeros((), src.dtype))


def bias_chunk(strip, far, h, first_q, kstart, kind, c):
    parts = []
    for r in range(KC // 128):
        m = PROMPT - 128 - (kstart + 128 * r)
        if kind == "far":
            parts.append(far[h, c, :, m : m + CL])
        else:
            parts.append(strip[h, :, pl.ds(pl.multiple_of(first_q + m, 128), CL)])
    return jnp.concatenate(parts, axis=0)


def attn_fwd_kernel(heads, starts, table, ids, q, k, v, o, lse, strip, far, kh, vt, ot, s, p):
    build_strips(heads, starts, table, ids, strip, far)
    masked_copies(k, kh, heads)
    vt[...] = v[...].astype(F32).T.astype(BF16)
    lse[...] = jnp.zeros(lse.shape, F32)

    def block(h, q0, bias_q0, chunks, c):
        qb = q[pl.ds(q0, CL), :]
        top = None
        for n, (k0, kind, kstart) in enumerate(chunks):
            sc = nt(kh[h, pl.ds(k0, KC), :], qb) + bias_chunk(strip, far, h, bias_q0, kstart, kind, c)
            s[n * KC : (n + 1) * KC, :] = sc
            m = jnp.max(sc, axis=0, keepdims=True)
            top = m if top is None else jnp.maximum(top, m)
        total = jnp.zeros((1, CL), F32)
        acc = jnp.zeros((HEAD_DIM, CL), F32)
        for n, (k0, kind, kstart) in enumerate(chunks):
            e = jnp.exp(s[n * KC : (n + 1) * KC, :] - top)
            total = total + jnp.sum(e, axis=0, keepdims=True)
            acc = acc + nn(vt[pl.ds(pl.multiple_of(h * HEAD_DIM, HEAD_DIM), HEAD_DIM), pl.ds(k0, KC)], e.astype(BF16))
        ot[pl.ds(pl.multiple_of(h * HEAD_DIM, HEAD_DIM), HEAD_DIM), pl.ds(q0, CL)] = acc / total
        lse[pl.ds(h, 1), pl.ds(q0, CL)] = top + jnp.log(total)

    nblk = PROMPT // CL

    def prompt_body(i, carry):
        h, blk = i // nblk, i % nblk
        q0 = pl.multiple_of(blk * CL, CL)
        block(h, q0, q0, [(j * KC, "strip", j * KC) for j in range(PROMPT // KC)], None)
        return carry

    lax.fori_loop(0, heads * nblk, prompt_body, 0)

    def cont_body(i, carry):
        h, c = i // 2, i % 2
        q0 = pl.multiple_of(PROMPT + c * CL, CL)
        chunks = [(j * KC, "far", j * KC) for j in range(PROMPT // KC)]
        chunks += [(q0 + j * KC, "strip", j * KC) for j in range(CL // KC)]
        block(h, q0, 0, chunks, c)
        return carry

    lax.fori_loop(0, heads * 2, cont_body, 0)
    o[...] = ot[...].T.astype(BF16)


def attn_fwd(starts, table, ids, q, k, v):
    rows, width = q.shape
    heads = width // HEAD_DIM
    smem = pl.BlockSpec(memory_space=pltpu.SMEM)
    vm = pl.BlockSpec(memory_space=pltpu.VMEM)
    return pl.pallas_call(
        functools.partial(attn_fwd_kernel, heads),
        out_shape=(
            jax.ShapeDtypeStruct((rows, width), BF16),
            jax.ShapeDtypeStruct((8, rows), F32),
        ),
        in_specs=[smem, smem, vm, vm, vm, vm],
        out_specs=(vm, vm),
        scratch_shapes=[
            pltpu.VMEM((heads, 128, STRIP), F32),
            pltpu.VMEM((heads, 2, 128, FARW), F32),
            pltpu.VMEM((heads, rows, width), BF16),
            pltpu.VMEM((width, rows), BF16),
            pltpu.VMEM((width, rows), F32),
            pltpu.VMEM((PROMPT + CL, CL), F32),
            pltpu.VMEM((PROMPT + CL, CL), BF16),
        ],
        compiler_params=pltpu.CompilerParams(vmem_limit_bytes=56 << 20),
        name="attend_forward",
    )(starts, table, ids, q, k, v)


def attn_bwd_kernel(
    heads, starts, table, ids, q, k, v, o, do, lse,
    dq, dk, dv, tgrad,
    strip, far, kh, vh, qh, doh, kt, delta, dqt, gstrip, gfar,
):
    build_strips(heads, starts, table, ids, strip, far)
    for src, dst in ((k, kh), (v, vh), (q, qh), (do, doh)):
        masked_copies(src, dst, heads)
    kt[...] = k[...].astype(F32).T.astype(BF16)
    prod = (o[...].astype(F32) * do[...].astype(F32)).T
    for h in range(heads):
        delta[h : h + 1, :] = jnp.sum(prod[h * HEAD_DIM : (h + 1) * HEAD_DIM, :], axis=0, keepdims=True)
    dk[...] = jnp.zeros(dk.shape, F32)
    dv[...] = jnp.zeros(dv.shape, F32)
    gstrip[...] = jnp.zeros(gstrip.shape, F32)
    gfar[...] = jnp.zeros(gfar.shape, F32)

    def block(h, q0, bias_q0, chunks, c):
        qb = q[pl.ds(q0, CL), :]
        dob = do[pl.ds(q0, CL), :]
        qhb = qh[h, pl.ds(q0, CL), :]
        dohb = doh[h, pl.ds(q0, CL), :]
        lrow = lse[pl.ds(h, 1), pl.ds(q0, CL)]
        drow = delta[pl.ds(h, 1), pl.ds(q0, CL)]
        acc = jnp.zeros((HEAD_DIM, CL), F32)
        for n, (k0, kind, kstart) in enumerate(chunks):
            ks = pl.ds(k0, KC)
            sc = nt(kh[h, ks, :], qb) + bias_chunk(strip, far, h, bias_q0, kstart, kind, c)
            pr = jnp.exp(sc - lrow)
            dp = nt(vh[h, ks, :], dob)
            ds = pr * (dp - drow)
            pl_ = pr.astype(BF16)
            dsl = ds.astype(BF16)
            dv[ks, :] += nn(pl_, dohb)
            dk[ks, :] += nn(dsl, qhb)
            acc = acc + nn(kt[pl.ds(pl.multiple_of(h * HEAD_DIM, HEAD_DIM), HEAD_DIM), ks], dsl)
            for r in range(KC // 128):
                m = PROMPT - 128 - (kstart + 128 * r)
                piece = ds[128 * r : 128 * (r + 1), :]
                if kind == "far":
                    gfar[h, c, :, m : m + CL] += piece
                else:
                    gstrip[h, :, pl.ds(pl.multiple_of(bias_q0 + m, 128), CL)] += piece
        dqt[pl.ds(pl.multiple_of(h * HEAD_DIM, HEAD_DIM), HEAD_DIM), pl.ds(q0, CL)] = acc

    nblk = PROMPT // CL

    def prompt_body(i, carry):
        h, blk = i // nblk, i % nblk
        q0 = pl.multiple_of(blk * CL, CL)
        block(h, q0, q0, [(j * KC, "strip", j * KC) for j in range(PROMPT // KC)], None)
        return carry

    lax.fori_loop(0, heads * nblk, prompt_body, 0)

    def cont_body(i, carry):
        h, c = i // 2, i % 2
        q0 = pl.multiple_of(PROMPT + c * CL, CL)
        chunks = [(j * KC, "far", j * KC) for j in range(PROMPT // KC)]
        chunks += [(q0 + j * KC, "strip", j * KC) for j in range(CL // KC)]
        block(h, q0, 0, chunks, c)
        return carry

    lax.fori_loop(0, heads * 2, cont_body, 0)
    dq[...] = dqt[...].T

    length = ids.shape[1]
    half = 2 * PROMPT
    lane8 = lax.broadcasted_iota(jnp.int32, (table.shape[0], length), 0)
    hot = ids[:1, :] == lane8
    for h in range(heads):
        def unskew(g, width):
            full = jnp.concatenate([jnp.zeros((128, 128), F32), g], axis=1)
            eight = full[:8]
            for a in range(1, 16):
                eight = eight + pltpu.roll(full[8 * a : 8 * a + 8], width - 8 * a, 1)
            vec = pltpu.roll(eight, width - 1, 1)[:1]
            for b in range(1, 8):
                vec = vec + pltpu.roll(eight, width - 1 - b, 1)[b : b + 1]
            return jnp.concatenate([vec, jnp.zeros((1, length - width), F32)], axis=1)

        total = jnp.broadcast_to(unskew(gstrip[h], half), (8, length))
        total = pltpu.roll(total, PROMPT // 2, 1)
        for c in range(2):
            piece = jnp.broadcast_to(unskew(gfar[h, c], FARW + 128), (8, length))
            total = total + pltpu.roll(piece, PROMPT // 2 + starts[c], 1)
        picked = jnp.where(hot, total[:1, :], 0.0)
        tgrad[h] = jnp.broadcast_to(jnp.sum(picked, axis=1, keepdims=True), tgrad.shape[1:])


def attn_bwd(starts, table, ids, q, k, v, o, do, lse):
    rows, width = q.shape
    heads = width // HEAD_DIM
    smem = pl.BlockSpec(memory_space=pltpu.SMEM)
    vm = pl.BlockSpec(memory_space=pltpu.VMEM)
    wide = jax.ShapeDtypeStruct((rows, width), F32)
    return pl.pallas_call(
        functools.partial(attn_bwd_kernel, heads),
        out_shape=(wide, wide, wide, jax.ShapeDtypeStruct((heads, table.shape[0], 128), F32)),
        in_specs=[smem, smem] + [vm] * 7,
        out_specs=(vm,) * 4,
        scratch_shapes=[
            pltpu.VMEM((heads, 128, STRIP), F32),
            pltpu.VMEM((heads, 2, 128, FARW), F32),
        ]
        + [pltpu.VMEM((heads, rows, width), BF16)] * 4
        + [
            pltpu.VMEM((width, rows), BF16),
            pltpu.VMEM((8, rows), F32),
            pltpu.VMEM((width, rows), F32),
            pltpu.VMEM((heads, 128, STRIP), F32),
            pltpu.VMEM((heads, 2, 128, FARW), F32),
        ],
        compiler_params=pltpu.CompilerParams(vmem_limit_bytes=60 << 20),
        name="attend_backward",
    )(starts, table, ids, q, k, v, o, do, lse)


def reversed_ids(bucket_ids):
    span = bucket_ids.shape[0]
    ids = jnp.concatenate([bucket_ids[::-1], jnp.full((1,), -1, jnp.int32)])
    return jnp.broadcast_to(ids[None, :], (8, span + 1))


def pack_columns(w, nseq, nfsdp, mine):
    depth, total = w.shape
    block = total // nfsdp
    piece = -(-block // (16 * nseq)) * 16
    w = jnp.pad(w.reshape(depth, nfsdp, block), ((0, 0), (0, 0), (0, nseq * piece - block)))
    w = w.reshape(depth, nfsdp, nseq, piece)
    w = lax.dynamic_index_in_dim(w, mine, 2, keepdims=False)
    return w.reshape(depth, nfsdp * piece)


def unpack_columns(parts, total, nfsdp):
    nseq, depth, width = parts.shape
    piece = width // nfsdp
    block = total // nfsdp
    w = parts.reshape(nseq, depth, nfsdp, piece).transpose(1, 2, 0, 3)
    return w.reshape(depth, nfsdp, nseq * piece)[:, :, :block].reshape(depth, total)


def pack_rows(w, nseq, mine):
    block, depth = w.shape
    piece = -(-block // (16 * nseq)) * 16
    w = jnp.pad(w, ((0, nseq * piece - block), (0, 0)))
    return lax.dynamic_slice_in_dim(w, mine * piece, piece, 0)


def dot32(a, b):
    return jnp.dot(a, b, preferred_element_type=F32)


def dot_tn(a, b):
    return lax.dot_general(a, b, (((0,), (0,)), ((), ())), preferred_element_type=F32)


def inverse_rms(v):
    return lax.rsqrt(jnp.mean(v * v, axis=-1, keepdims=True) + epsilon)


def gelu_both(u):
    inner = 0.7978845608028654 * (u + 0.044715 * u * u * u)
    t = jnp.tanh(inner)
    value = 0.5 * u * (1.0 + t)
    slope = 0.5 * (1.0 + t) + 0.5 * u * (1.0 - t * t) * 0.7978845608028654 * (1.0 + 3 * 0.044715 * u * u)
    return value, slope


def norm_back(grad, v, r, gain):
    scaled = grad * gain
    return r * scaled - v * (r * r * r) * jnp.mean(v * scaled, axis=-1, keepdims=True)


def body(
    tokens,
    out_grad,
    attn_gain,
    w_query,
    w_key,
    w_value,
    w_out,
    mix_gain,
    w_gate,
    w_up,
    w_down,
    rel_table,
    bucket_ids,
    cont_start,
):
    nseq = lax.axis_size("seq")
    nfsdp = lax.axis_size("fsdp")
    mine = lax.axis_index("seq")
    where = lax.axis_index("fsdp")
    rows, width = tokens.shape[1:]
    inner = w_query.shape[1]
    piece = inner // nseq
    heads = piece // HEAD_DIM
    hidden_all = w_gate.shape[1]

    def gather_f(a):
        return lax.all_gather(a, "fsdp", axis=0, tiled=True)

    def gather_s(a):
        return lax.all_gather(a, "seq", axis=0, tiled=True)

    def scatter_s(a):
        return lax.psum_scatter(a.astype(BF16), "seq", scatter_dimension=0, tiled=True).astype(F32)

    def scatter_f(a):
        return lax.psum_scatter(a.astype(BF16), "fsdp", scatter_dimension=0, tiled=True)

    local = [lax.dynamic_slice_in_dim(w, mine * piece, piece, 1) for w in (w_query, w_key, w_value)]
    gains = jnp.pad(jnp.stack([attn_gain, mix_gain], axis=1), ((0, 0), (0, 62)))
    first = gather_f(jnp.concatenate(local + [gains], axis=1))
    query_w, key_w, value_w = (first[:, i * piece : (i + 1) * piece] for i in range(3))
    gain_one = first[:, 3 * piece].astype(F32)
    gain_two = first[:, 3 * piece + 1].astype(F32)
    out_cols = width // nseq
    out_local = lax.dynamic_slice_in_dim(w_out, mine * out_cols, out_cols, 1)
    out_w = lax.all_to_all(gather_f(out_local), "seq", split_axis=0, concat_axis=1, tiled=True)
    gate_w = gather_f(pack_columns(w_gate, nseq, nfsdp, mine))
    up_w = gather_f(pack_columns(w_up, nseq, nfsdp, mine))
    down_w = gather_f(pack_rows(w_down, nseq, mine))

    block = tokens[0].astype(F32)
    r_one = inverse_rms(block)
    group = gather_s(tokens[0]).astype(F32)
    normed = (group * inverse_rms(group) * gain_one).astype(BF16)
    query = dot32(normed, query_w).astype(BF16)
    keys = dot32(normed, key_w).astype(BF16)
    values = dot32(normed, value_w).astype(BF16)
    table = lax.dynamic_slice_in_dim(rel_table, mine * heads, heads, 1)
    ids = reversed_ids(bucket_ids)
    starts = cont_start[0]
    mixed, lse = attn_fwd(starts, table, ids, query, keys, values)
    resid = block + scatter_s(dot32(mixed, out_w))
    r_two = inverse_rms(resid)
    normed_two = gather_s((resid * r_two * gain_two).astype(BF16))
    gate = dot32(normed_two, gate_w)
    upward = dot32(normed_two, up_w)
    active, slope = gelu_both(gate)
    hidden = (active * upward).astype(BF16)
    result = resid + scatter_s(dot32(hidden, down_w))
    cot = gather_s(out_grad[0])
    down_grad = scatter_f(dot_tn(hidden, cot))
    hidden_grad = lax.dot_general(cot, down_w, (((1,), (1,)), ((), ())), preferred_element_type=F32)
    gate_grad = (hidden_grad * upward * slope).astype(BF16)
    up_grad = (hidden_grad * active).astype(BF16)
    normed_two_grad = scatter_s(nt(gate_grad, gate_w) + nt(up_grad, up_w))
    gate_w_grad = scatter_f(dot_tn(normed_two, gate_grad))
    up_w_grad = scatter_f(dot_tn(normed_two, up_grad))
    gain_two_grad = jnp.sum(normed_two_grad * resid * r_two, axis=0)
    resid_grad = out_grad[0].astype(F32) + norm_back(normed_two_grad, resid, r_two, gain_two)
    attn_grad = gather_s(resid_grad.astype(BF16))
    out_w_grad = dot_tn(mixed, attn_grad).astype(BF16)
    mixed_grad = nt(attn_grad, out_w).astype(BF16)
    dq, dk, dv, tgrad = attn_bwd(starts, table, ids, query, keys, values, mixed, mixed_grad, lse)
    dq, dk, dv = (a.astype(BF16) for a in (dq, dk, dv))
    normed_grad = scatter_s(nt(dq, query_w) + nt(dk, key_w) + nt(dv, value_w))
    qkv_grad = scatter_f(dot_tn(normed, jnp.concatenate([dq, dk, dv], axis=1)))
    gain_one_grad = jnp.sum(normed_grad * block * r_one, axis=0)
    in_grad = resid_grad + norm_back(normed_grad, block, r_one, gain_one)

    out_grad_cols = lax.all_to_all(out_w_grad, "seq", split_axis=1, concat_axis=0, tiled=True)
    out_w_grad = lax.all_gather(scatter_f(out_grad_cols), "seq", axis=1, tiled=True)
    qkv_grad = lax.all_gather(qkv_grad, "seq", axis=0).reshape(nseq, -1, 3, piece)
    qkv_grad = qkv_grad.transpose(1, 2, 0, 3).reshape(-1, 3, inner).astype(F32)
    gate_w_grad = unpack_columns(lax.all_gather(gate_w_grad, "seq", axis=0), hidden_all, nfsdp)
    up_w_grad = unpack_columns(lax.all_gather(up_w_grad, "seq", axis=0), hidden_all, nfsdp)
    down_grad = gather_s(down_grad)[: w_down.shape[0]]

    buckets = rel_table.shape[0]
    table_full = jnp.zeros((nseq, heads, buckets), F32)
    table_full = lax.dynamic_update_slice(table_full, tgrad[None, :, :, 0], (mine, jnp.int32(0), jnp.int32(0)))
    table_grad, gain_one_all, gain_two_all = lax.psum((table_full, gain_one_grad, gain_two_grad), ("seq", "fsdp"))
    share = width // nfsdp
    gain_one_share = lax.dynamic_slice_in_dim(gain_one_all, where * share, share)
    gain_two_share = lax.dynamic_slice_in_dim(gain_two_all, where * share, share)
    return (
        result.astype(BF16)[None],
        in_grad.astype(BF16)[None],
        gain_one_share,
        qkv_grad[:, 0],
        qkv_grad[:, 1],
        qkv_grad[:, 2],
        out_w_grad.astype(F32),
        gain_two_share,
        gate_w_grad.astype(F32),
        up_w_grad.astype(F32),
        down_grad.astype(F32),
        table_grad.reshape(nseq * heads, buckets).T,
    )


def solution(mesh):
    placed = (
        P("fsdp", "seq", None),
        P("fsdp", "seq", None),
        P("fsdp"),
        P("fsdp", None),
        P("fsdp", None),
        P("fsdp", None),
        P("fsdp", None),
        P("fsdp"),
        P("fsdp", None),
        P("fsdp", None),
        P("fsdp", None),
        P(),
        P(),
        P("fsdp", None),
    )
    results = placed[:1] * 2 + placed[2:11] + (P(),)
    return jax.shard_map(body, mesh=mesh, in_specs=placed, out_specs=results, check_vma=False)
```

time: 2510 us -> 1130 us (0.45)
  waiting for transfers between devices: 1630 us -> 715 us
  local copies, waits for them, and re-layouts: 454 us -> 55.8 us
  matrix products: 192 us -> 124 us
  other arithmetic: 93.3 us -> 34.9 us
  Pallas kernels: 0 us -> 53.4 us
    reduce_scatter x7 -> x9, waiting for transfers between devices: 1190 us -> 391 us  [the longest x5 307 us: scatter_f(): lax.psum_scatter(a.astype(BF16), 'fsdp', scatter_dimension=0, tiled=True)]
    reshape x21 -> x7, local copies, waits for them, and re-layouts: 144 us -> 11.5 us  [the longest x2 10 us: pack_columns(): w.reshape(depth, nfsdp, block)]
    unnamed x162 -> x74, local copies, waits for them, and re-layouts: 125 us -> 9.33 us
    another operation x15 -> x2, local copies, waits for them, and re-layouts: 75.3 us -> 1.35 us  [body(): gains = jnp.pad(jnp.stack([attn_gain, mix_gain], axis=1), ((0, 0), (0, 62)))]
    dot_general x47 -> x19, matrix products: 192 us -> 124 us  [the longest x7 43.4 us: dot32(): return jnp.dot(a, b, preferred_element_type=F32)]
    all_gather x7 -> x11, waiting for transfers between devices: 369 us -> 314 us  [the longest x4 163 us: gather_f(): return lax.all_gather(a, 'fsdp', axis=0, tiled=True)]
    pallas_call x0 -> x2, Pallas kernels: none -> 53.4 us  [the longest x1 34.2 us: attn_bwd(): pl.pallas_call(functools.partial(attn_bwd_kernel, heads), out_shape=(wide...]
    psum x1 -> x0, waiting for transfers between devices: 53.3 us -> none  [body(): lax.psum(shares[0].astype(jnp.bfloat16), 'seq').astype(jnp.float32)]
  transfers between devices with their start and end apart: 18 -> 21, of which waited for: 12 -> 18; matrix products, arithmetic and copies ran while one was open for 27% -> 14% of each run, Pallas kernels for 0% -> 3%
where the time goes in v1:
time: 1130 us; the launch traced here: 1110 us
  waiting for transfers between devices  715 us (63%)
  matrix products  124 us (11%)
  blocking collectives  111 us (10%)
  local copies, waits for them, and re-layouts  55.8 us (5%)
  Pallas kernels  53.4 us (5%)
  other arithmetic  34.9 us (3%)
  between operations  15.1 us (1%)
    reduce_scatter x5, waiting for transfers between devices, scatter_f(): lax.psum_scatter(a.astype(BF16), 'fsdp', scatter_dimension=0, tiled=True)  307 us
    all_gather x4, waiting for transfers between devices, gather_f(): return lax.all_gather(a, 'fsdp', axis=0, tiled=True)  163 us
    all_gather x5, waiting for transfers between devices, gather_s(): return lax.all_gather(a, 'seq', axis=0, tiled=True)  151 us
    reduce_scatter x4, waiting for transfers between devices, scatter_s(): lax.psum_scatter(a.astype(BF16), 'seq', scatter_dimension=0, tiled=True)  84.3 us
    dot_general x7, matrix products, dot32(): return jnp.dot(a, b, preferred_element_type=F32)  43.4 us
    psum x1, blocking collectives, body(): lax.psum((table_full, gain_one_grad, gain_two_grad), ('seq', 'fsdp'))  40.2 us
    dot_general x5, matrix products, dot_tn(): lax.dot_general(a, b, (((0,), (0,)), ((), ())), preferred_element_type=F32)  40.1 us
    all_gather x1, blocking collectives, gather_f(): return lax.all_gather(a, 'fsdp', axis=0, tiled=True)  36.3 us
  transfers between devices with their start and end apart: 21, of which 18 were waited for; matrix products, arithmetic and copies ran while one was open for 14% of the time, Pallas kernels for 3%

profile of v1, /device:TPU:0, one launch (start us, length us, event | category | flops | bytes accessed | tf_op | source)
XLA Modules:
  0.0 1114.8 jit_solution(7252659662682458300)
XLA Ops:
  12.5 36.3 %all_gather.53 = bf16[768,384]{1,0:T(8,128)(2,1)} all-gather(bf16[96,384]{1,0:T(8,128)(2,1)S(1)} %constant_dynamic-slice_fusion.2), channel_id=1, replica_groups=mesh['seq'=4,'fsdp'=8] {'fsdp'}, dimensions={0}, use_global_device_ids=true | all-gather | bytes 663552 | tf_op jit(solution)/shard_map/all_gather | solution.py:338
  48.8 3.5 all-to-all-start
  54.0 7.8 all-to-all-done
  64.7 36.7 %all-gather.31.cloned.1.call-done = bf16[1,1536,1536]{2,1,0:T(8,128)(2,1)} async-done(((bf16[1,384,1536]{2,1,0:T(8,128)(2,1)}), bf16[1,1536,1536]{2,1,0:T(8,128)(2,1)}) %all-gather.31.cloned.1.call-update) | async-done | bytes 4718608 | tf_op jit(solution)/shard_map/all_gather | solution.py:341
  104.9 4.9 convolution_convert_fusion.5.v
  115.5 19.3 %attend_forward.1 = (bf16[1536,192]{1,0:T(8,128)(2,1)}, f32[8,1536]{1,0:T(8,128)}) custom-call(s32[2]{0:T(128)} %bitcast.161, f32[32,3]{1,0:T(8,128)} %copy.112.table, s32[8,3072]{1,0:T(8,128)} %broadcast_in_dim.8.ids, bf16[1536,192]{1,0:T(8,128)(2,1)} %convolution_convert_fusion.7.q, bf16[1536,192]{1,0:T(8,128)(2,1)} %convolution_convert_fusion.6.k, ...), custom_call_target="tpu_custom_call" | custom-call | tf_op jit(solution)/shard_map/attend_forward/pallas_call | solution.py:115
  134.8 4.7 convolution_convert_fusion.1
  139.9 4.6 reshape.139
  144.5 5.5 reshape.136
  152.7 34.8 %reduce-scatter.12.cloned.1.call-done = bf16[384,1536]{1,0:T(8,128)(2,1)} async-done(((bf16[1536,1536]{1,0:T(8,128)(2,1)}), bf16[384,1536]{1,0:T(8,128)(2,1)}) %reduce-scatter.12.cloned.1.call-update) | async-done | bytes 1179664 | tf_op jit(solution)/shard_map/reduce_scatter | solution.py:344
  194.4 56.5 %all-gather.23.cloned.1.call-done = bf16[1536,1024]{1,0:T(8,128)(2,1)} async-done(((bf16[192,1024]{1,0:T(8,128)(2,1)}), bf16[1536,1024]{1,0:T(8,128)(2,1)}) %all-gather.23.cloned.1.call-update) | async-done | bytes 3145744 | tf_op jit(solution)/shard_map/all_gather | solution.py:338
  250.8 38.2 %all-gather.19.cloned.1.call-done = bf16[1536,1536]{1,0:T(8,128)(2,1)} async-done(((bf16[384,1536]{1,0:T(8,128)(2,1)}), bf16[1536,1536]{1,0:T(8,128)(2,1)}) %all-gather.19.cloned.1.call-update) | async-done | bytes 4718608 | tf_op jit(solution)/shard_map/all_gather | solution.py:341
  289.0 9.8 fusion.58
  298.8 53.5 %all-gather.21.cloned.1.call-done = bf16[1536,1024]{1,0:T(8,128)(2,1)} async-done(((bf16[192,1024]{1,0:T(8,128)(2,1)}), bf16[1536,1024]{1,0:T(8,128)(2,1)}) %all-gather.21.cloned.1.call-update) | async-done | bytes 3145744 | tf_op jit(solution)/shard_map/all_gather | solution.py:338
  352.4 9.8 fusion.57
  362.2 52.3 %all-gather.25.cloned.1.call-done = bf16[1024,1536]{1,0:T(8,128)(2,1)} async-done(((bf16[128,1536]{1,0:T(8,128)(2,1)}), bf16[1024,1536]{1,0:T(8,128)(2,1)}) %all-gather.25.cloned.1.call-update) | async-done | bytes 3145744 | tf_op jit(solution)/shard_map/all_gather | solution.py:338
  414.5 37.7 %all-gather.33.cloned.1.call-done = bf16[1,1536,1536]{2,1,0:T(8,128)(2,1)} async-done(((bf16[1,384,1536]{2,1,0:T(8,128)(2,1)}), bf16[1,1536,1536]{2,1,0:T(8,128)(2,1)}) %all-gather.33.cloned.1.call-update) | async-done | bytes 4718608 | tf_op jit(solution)/shard_map/all_gather | solution.py:341
  452.2 16.2 %fusion.11 = (bf16[1536,1024]{1,0:T(8,128)(2,1)}, bf16[1536,1024]{1,0:T(8,128)(2,1)S(1)}, bf16[1536,1024]{1,0:T(8,128)(2,1)}) fusion(f32[1536,1024]{1,0:T(8,128)} %fusion.57, f32[1536,1024]{1,0:T(8,128)} %fusion.58, bf16[1024,1536]{1,0:T(8,128)(2,1)} %all-gather.25.cloned.1.call-done, bf16[1,1536,1536]{2,1,0:T(8,128)(2,1)} %all-gather.33.cloned.1.call-done), kind=kOutput, calls=%fused_computation.22 | convolution fusion | flops 4871159808 | bytes 29884416 | tf_op jit(solution)/shard_map/dot_general | solution.py:383
  468.5 5.2 fusion.59
  473.7 7.2 add_convert_fusion
  481.0 9.4 convolution_convert_fusion.3
  490.4 9.8 convolution_convert_fusion.2
  500.3 9.5 fusion.16
  509.8 19.1 %reduce-scatter.16.cloned.1.call-done = bf16[384,1536]{1,0:T(8,128)(2,1)} async-done(((bf16[1536,1536]{1,0:T(8,128)(2,1)}), bf16[384,1536]{1,0:T(8,128)(2,1)}) %reduce-scatter.16.cloned.1.call-update) | async-done | bytes 1179664 | tf_op jit(solution)/shard_map/reduce_scatter | solution.py:344
  535.4 71.3 %reduce-scatter.22.cloned.1.call-done = bf16[192,1024]{1,0:T(8,128)(2,1)} async-done(((bf16[1536,1024]{1,0:T(8,128)(2,1)}), bf16[192,1024]{1,0:T(8,128)(2,1)}) %reduce-scatter.22.cloned.1.call-update) | async-done | bytes 393232 | tf_op jit(solution)/shard_map/reduce_scatter | solution.py:347
  606.8 76.9 %reduce-scatter.24.cloned.1.call-done = bf16[192,1024]{1,0:T(8,128)(2,1)} async-done(((bf16[1536,1024]{1,0:T(8,128)(2,1)}), bf16[192,1024]{1,0:T(8,128)(2,1)}) %reduce-scatter.24.cloned.1.call-update) | async-done | bytes 393232 | tf_op jit(solution)/shard_map/reduce_scatter | solution.py:347
  683.8 76.9 %reduce-scatter.26.cloned.1.call-done = bf16[128,1536]{1,0:T(8,128)(2,1)} async-done(((bf16[1024,1536]{1,0:T(8,128)(2,1)}), bf16[128,1536]{1,0:T(8,128)(2,1)}) %reduce-scatter.26.cloned.1.call-update) | async-done | bytes 393232 | tf_op jit(solution)/shard_map/reduce_scatter | solution.py:347
  761.0 38.4 %all-gather.27.cloned.1.call-done = bf16[1536,1536]{1,0:T(8,128)(2,1)} async-done(((bf16[384,1536]{1,0:T(8,128)(2,1)}), bf16[1536,1536]{1,0:T(8,128)(2,1)}) %all-gather.27.cloned.1.call-update) | async-done | bytes 4718608 | tf_op jit(solution)/shard_map/all_gather | solution.py:341
  799.4 3.5 convolution_convert_fusion.9
  802.9 18.0 %all_to_all.38 = bf16[192,4,384]{2,0,1:T(8,128)(2,1)} all-to-all(bf16[192,4,384]{2,0,1:T(8,128)(2,1)S(1)} %bitcast.151), channel_id=1, replica_groups=mesh['seq'=4,'fsdp'=8] {'seq'}, dimensions={1} | all-to-all | bytes 1179648 | tf_op jit(solution)/shard_map/all_to_all | solution.py:401
  821.0 4.2 convolution_convert_fusion.8
  826.4 34.2 %attend_backward.1 = (f32[1536,192]{1,0:T(8,128)}, f32[1536,192]{1,0:T(8,128)}, f32[1536,192]{1,0:T(8,128)}, f32[3,32,128]{2,1,0:T(8,128)}) custom-call(s32[2]{0:T(128)} %bitcast.162, f32[32,3]{1,0:T(8,128)} %copy.112.table, s32[8,3072]{1,0:T(8,128)} %broadcast_in_dim.8.ids, bf16[1536,192]{1,0:T(8,128)(2,1)} %convolution_convert_fusion.7.q, ...), custom_call_target="tpu_custom_call" | custom-call | tf_op jit(solution)/shard_map/attend_backward/pallas_call | solution.py:233
  865.4 8.1 convolution_convert_fusion.4
  878.1 3.7 fusion.3
  881.8 9.1 convolution_convert_fusion
  895.3 4.8 reshape.150
  904.3 4.8 reshape.151
  909.1 3.4 slice_convert_fusion.2
  913.9 19.0 %reduce-scatter.20.cloned.1.call-done = bf16[96,384]{1,0:T(8,128)(2,1)} async-done(((bf16[768,384]{1,0:T(8,128)(2,1)}), bf16[96,384]{1,0:T(8,128)(2,1)}) %reduce-scatter.20.cloned.1.call-update) | async-done | bytes 73744 | tf_op jit(solution)/shard_map/reduce_scatter | solution.py:347
  932.9 6.1 all_gather.62
  939.8 62.6 %reduce-scatter.28.cloned.1.call-done = bf16[192,576]{1,0:T(8,128)(2,1)} async-done(((bf16[1536,576]{1,0:T(8,128)(2,1)}), bf16[192,576]{1,0:T(8,128)(2,1)}) %reduce-scatter.28.cloned.1.call-update) | async-done | bytes 221200 | tf_op jit(solution)/shard_map/reduce_scatter | solution.py:347
  1002.5 10.5 all-gather.2
  1017.9 4.4 copy.101
  1022.2 4.0 reshape.149
  1029.0 22.8 %reduce-scatter.18.cloned.1.call-done = bf16[384,1536]{1,0:T(8,128)(2,1)} async-done(((bf16[1536,1536]{1,0:T(8,128)(2,1)}), bf16[384,1536]{1,0:T(8,128)(2,1)}) %reduce-scatter.18.cloned.1.call-update) | async-done | bytes 1179664 | tf_op jit(solution)/shard_map/reduce_scatter | solution.py:344
  1053.9 40.2 %all-reduce.4 = (f32[1536]{0:T(1024)S(1)}, f32[1536]{0:T(1024)S(1)}, f32[32,12]{0,1:T(8,128)}) all-reduce(f32[1536]{0:T(1024)S(1)} %get-tuple-element.26, f32[1536]{0:T(1024)S(1)} %copy-done.18, f32[32,12]{0,1:T(8,128)S(1)} %bitcast.159), channel_id=1, replica_groups=mesh['seq'=4,'fsdp'=8] {'seq','fsdp'}, use_global_device_ids=true, to_apply=%region_10.11 | all-reduce | flops 3456 | bytes 27648 | tf_op jit(solution)/shard_map/psum | solution.py:412
  1095.4 7.6 reduce-scatter.14.cloned.1.call-done
  1103.0 4.7 fusion.41
  (169 shorter events, 68.1 us)
Async XLA Ops:
  7.2 46.6 %copy-start.25 = (s32[3071]{0:T(1024)S(1)}, s32[3071]{0:T(1024)}, u32[]{:S(2)}) copy-start(s32[3071]{0:T(1024)} %param.26) | copy-start | bytes 36856
  7.2 55.7 %all-gather.17.cloned.1.call-start = ((), (), s32[]{:S(2)}) async-start(), calls=%async_computation.11 | async-start | bytes 2211840 | tf_op jit(solution)/shard_map/all_gather | solution.py:338
  10.9 90.6 %all-gather.31.cloned.1.call-start = ((), (), s32[]{:S(2)}) async-start(), calls=%async_computation.26 | async-start | bytes 5898240 | tf_op jit(solution)/shard_map/all_gather | solution.py:341
  48.8 13.0 %all-to-all-start = ((bf16[4,192,384]{2,1,0:T(8,128)(2,1)}), bf16[4,192,384]{2,1,0:T(8,128)(2,1)S(1)}, u32[]{:S(2)}, u32[]{:S(2)}) async-start(bf16[4,192,384]{2,1,0:T(8,128)(2,1)} %bitcast.4), calls=%async_computation | async-start | bytes 1179648 | tf_op jit(solution)/shard_map/all_to_all | solution.py:357
  52.3 135.2 %reduce-scatter.12.cloned.1.call-start = ((), (), s32[]{:S(2)}) async-start(), calls=%async_computation.12 | async-start | bytes 5898240 | tf_op jit(solution)/shard_map/reduce_scatter | solution.py:344
  61.9 72.9 %copy-start.13 = (bf16[4,24,8,384]{3,2,0,1:T(8,128)(2,1)}, bf16[4,24,8,384]{3,2,0,1:T(8,128)(2,1)S(1)}, u32[]{:S(2)}) copy-start(bf16[4,24,8,384]{3,2,0,1:T(8,128)(2,1)S(1)} %copy.115) | copy-start | bytes 1769476
  62.9 42.0 %copy-start.7 = (bf16[1536,640]{1,0:T(8,128)(2,1)S(1)}, bf16[1536,640]{1,0:T(8,128)(2,1)}, u32[]{:S(2)}) copy-start(bf16[1536,640]{1,0:T(8,128)(2,1)} %all-gather.17.cloned.1.call-done) | copy-start | bytes 5898244
  101.5 8.3 slice-start
  104.9 4.9 slice-start.1
  139.5 111.3 %all-gather.23.cloned.1.call-start = ((), (), s32[]{:S(2)}) async-start(), calls=%async_computation.15 | async-start | bytes 3538944 | tf_op jit(solution)/shard_map/all_gather | solution.py:338
  151.4 36.1 %copy-start.2 = (bf16[1,384,1536]{2,1,0:T(8,128)(2,1)S(1)}, bf16[1,384,1536]{2,1,0:T(8,128)(2,1)}, u32[]{:S(2)}) copy-start(bf16[1,384,1536]{2,1,0:T(8,128)(2,1)} %param.14) | copy-start | bytes 3538948
  152.7 136.3 %all-gather.19.cloned.1.call-start = ((), (), s32[]{:S(2)}) async-start(), calls=%async_computation.13 | async-start | bytes 5898240 | tf_op jit(solution)/shard_map/all_gather | solution.py:341
  189.4 342.6 %copy-start.15 = (f32[384]{0:T(512)}, f32[384]{0:T(512)S(1)}, u32[]{:S(2)}) copy-start(f32[384]{0:T(512)S(1)} %get-tuple-element.45) | copy-start | bytes 4612
  189.4 342.6 %copy-start.20 = (f32[384]{0:T(512)}, f32[384]{0:T(512)S(1)}, u32[]{:S(2)}) copy-start(f32[384]{0:T(512)S(1)} %get-tuple-element.44) | copy-start | bytes 4612
  190.8 161.5 %all-gather.21.cloned.1.call-start = ((), (), s32[]{:S(2)}) async-start(), calls=%async_computation.14 | async-start | bytes 3538944 | tf_op jit(solution)/shard_map/all_gather | solution.py:338
  191.7 222.7 %all-gather.25.cloned.1.call-start = ((), (), s32[]{:S(2)}) async-start(), calls=%async_computation.16 | async-start | bytes 3538944 | tf_op jit(solution)/shard_map/all_gather | solution.py:338
  193.6 258.6 %all-gather.33.cloned.1.call-start = ((), (), s32[]{:S(2)}) async-start(), calls=%async_computation.27 | async-start | bytes 5898240 | tf_op jit(solution)/shard_map/all_gather | solution.py:341
  194.4 334.6 %reduce-scatter.16.cloned.1.call-start = ((), (), s32[]{:S(2)}) async-start(), calls=%async_computation.18 | async-start | bytes 5898240 | tf_op jit(solution)/shard_map/reduce_scatter | solution.py:344
  452.2 16.2 %copy-start.28 = (bf16[1536,1024]{1,0:T(8,128)(2,1)S(1)}, bf16[1536,1024]{1,0:T(8,128)(2,1)}, u32[]{:S(2)}) copy-start(bf16[1536,1024]{1,0:T(8,128)(2,1)} %all-gather.21.cloned.1.call-done) | copy-start | bytes 9437188
  468.4 5.2 copy-start.29
  468.4 5.2 copy-start.27
  468.4 5.2 copy-start.30
  480.9 125.8 %reduce-scatter.22.cloned.1.call-start = ((), (), s32[]{:S(2)}) async-start(), calls=%async_computation.22 | async-start | bytes 3538944 | tf_op jit(solution)/shard_map/reduce_scatter | solution.py:347
  490.4 193.3 %reduce-scatter.24.cloned.1.call-start = ((), (), s32[]{:S(2)}) async-start(), calls=%async_computation.23 | async-start | bytes 3538944 | tf_op jit(solution)/shard_map/reduce_scatter | solution.py:347
  500.2 260.5 %reduce-scatter.26.cloned.1.call-start = ((), (), s32[]{:S(2)}) async-start(), calls=%async_computation.24 | async-start | bytes 3538944 | tf_op jit(solution)/shard_map/reduce_scatter | solution.py:347
  509.8 289.6 %all-gather.27.cloned.1.call-start = ((), (), s32[]{:S(2)}) async-start(), calls=%async_computation.19 | async-start | bytes 5898240 | tf_op jit(solution)/shard_map/all_gather | solution.py:341
  529.0 3.0 copy-start.4
  532.0 3.4 copy-start.23
  532.0 267.4 %copy-start.6 = (bf16[1536,192]{1,0:T(8,128)(2,1)S(1)}, bf16[1536,192]{1,0:T(8,128)(2,1)}, u32[]{:S(2)}) copy-start(bf16[1536,192]{1,0:T(8,128)(2,1)} %get-tuple-element.18.o) | copy-start | bytes 1769476
  535.3 355.7 %all-gather.35.cloned.1.call-start = ((), (), s32[]{:S(2)}) async-start(), calls=%async_computation.28 | async-start | bytes 1966080 | tf_op jit(solution)/shard_map/all_gather | solution.py:405
  606.7 293.3 %all-gather.37.cloned.1.call-start = ((), (), s32[]{:S(2)}) async-start(), calls=%async_computation.29 | async-start | bytes 1966080 | tf_op jit(solution)/shard_map/all_gather | solution.py:406
  683.7 225.4 %all-gather.29.cloned.1.call-start = ((), (), s32[]{:S(2)}) async-start(), calls=%async_computation.25 | async-start | bytes 1966080 | tf_op jit(solution)/shard_map/all_gather | solution.py:341
  760.7 172.2 %reduce-scatter.20.cloned.1.call-start = ((), (), s32[]{:S(2)}) async-start(), calls=%async_computation.21 | async-start | bytes 663552 | tf_op jit(solution)/shard_map/reduce_scatter | solution.py:347
  821.0 181.5 %reduce-scatter.28.cloned.1.call-start = ((), (), s32[]{:S(2)}) async-start(), calls=%async_computation.30 | async-start | bytes 2211840 | tf_op jit(solution)/shard_map/reduce_scatter | solution.py:347
  860.6 3.1 copy-start.14
  873.5 178.3 %reduce-scatter.18.cloned.1.call-start = ((), (), s32[]{:S(2)}) async-start(), calls=%async_computation.20 | async-start | bytes 5898240 | tf_op jit(solution)/shard_map/reduce_scatter | solution.py:344
  873.8 2.7 copy-start.8
  873.8 2.7 copy-start.10
  881.8 221.2 %reduce-scatter.14.cloned.1.call-start = ((), (), s32[]{:S(2)}) async-start(), calls=%async_computation.17 | async-start | bytes 5898240 | tf_op jit(solution)/shard_map/reduce_scatter | solution.py:344
  909.1 4.0 copy-start.17
  1022.2 29.6 %copy-start.22 = (f32[384]{0:T(512)S(1)}, f32[384]{0:T(512)}, u32[]{:S(2)}) copy-start(f32[384]{0:T(512)} %get-tuple-element.43) | copy-start | bytes 4612
  1026.3 27.6 %copy-start.18 = (f32[1536]{0:T(1024)S(1)}, f32[1536]{0:T(1024)}, u32[]{:S(2)}) copy-start(f32[1536]{0:T(1024)} %get-tuple-element.24) | copy-start | bytes 18436
  1026.3 27.6 %copy-start.19 = (f32[12,32]{1,0:T(8,128)S(1)}, f32[12,32]{1,0:T(8,128)}, u32[]{:S(2)}) copy-start(f32[12,32]{1,0:T(8,128)} %reshape.146) | copy-start | bytes 4612
  1026.3 76.7 %copy-start.16 = (f32[384]{0:T(512)S(1)}, f32[384]{0:T(512)}, u32[]{:S(2)}) copy-start(f32[384]{0:T(512)} %copy-done.15) | copy-start | bytes 4612
  1026.3 76.7 %copy-start.21 = (f32[384]{0:T(512)S(1)}, f32[384]{0:T(512)}, u32[]{:S(2)}) copy-start(f32[384]{0:T(512)} %copy-done.20) | copy-start | bytes 4612
  1026.3 76.7 %copy-start.24 = (f32[384]{0:T(512)S(1)}, f32[384]{0:T(512)}, u32[]{:S(2)}) copy-start(f32[384]{0:T(512)} %copy-done.23) | copy-start | bytes 4612
  1026.3 76.7 %copy-start.26 = (f32[384]{0:T(512)S(1)}, f32[384]{0:T(512)}, u32[]{:S(2)}) copy-start(f32[384]{0:T(512)} %get-tuple-element.42) | copy-start | bytes 4612
  1103.0 4.7 copy-start.1
  (6 other events, 8.3 us)
Sparse Core Ops, SparseCore 0:
  11.0 51.8 all-gather.16
  64.5 36.9 all-gather.30
  139.6 47.8 reduce-scatter.11
  190.4 60.4 all-gather.22
  252.9 36.0 all-gather.18
  291.9 60.4 all-gather.20
  355.3 59.0 all-gather.24
  416.1 36.0 all-gather.32
  481.1 47.8 reduce-scatter.15
  532.4 74.2 reduce-scatter.21
  610.3 73.3 reduce-scatter.23
  687.1 73.5 reduce-scatter.25
  762.8 36.5 all-gather.26
  800.8 24.5 all-gather.34
  826.8 19.6 all-gather.36
  847.9 19.6 all-gather.28
  870.7 62.0 reduce-scatter.19
  936.6 65.8 reduce-scatter.27
  1005.0 46.7 reduce-scatter.17
  1054.4 48.5 reduce-scatter.13

commit v2 on v1

--- a/solution.py
+++ b/solution.py
@@ -11,6 +11,7 @@
 CL = 256
 F32 = jnp.float32
 BF16 = jnp.bfloat16
+MESH = pl.DeviceIdType.MESH
 epsilon = 1e-06
 STRIP = 2 * PROMPT - 128
 FARW = PROMPT - 128 + CL
@@ -23,6 +24,335 @@
 
 def nn(a, b):
     return lax.dot_general(a, b, (((1,), (0,)), ((), ())), preferred_element_type=F32)
+
+
+class Wires:
+    def __init__(self, send, recv):
+        self.send, self.recv, self.used = send, recv, 0
+
+    def copy(self, src, dst, where):
+        i = self.used
+        self.used += 1
+        return pltpu.make_async_remote_copy(
+            src_ref=src,
+            dst_ref=dst,
+            send_sem=self.send.at[i],
+            recv_sem=self.recv.at[i],
+            device_id=where,
+            device_id_type=MESH,
+        )
+
+    def go(self, src, dst, where):
+        c = self.copy(src, dst, where)
+        c.start()
+        return c
+
+
+def seq_places():
+    s = lax.axis_index("seq")
+    near = s + 1 - 2 * lax.rem(s, 2)
+    far = lax.rem(s + 2, 4)
+    cross = lax.rem(near + 2, 4)
+    return s, near, far, cross
+
+
+def meet(places):
+    barrier = pltpu.get_barrier_semaphore()
+    for where in places:
+        pl.semaphore_signal(barrier, inc=1, device_id=where, device_id_type=MESH)
+    pl.semaphore_wait(barrier, len(places))
+
+
+def rows_at(index, rows, offset=0, count=None):
+    return pl.ds(pl.multiple_of(index * rows + offset, 16), rows if count is None else count)
+
+
+class SeqGather:
+    def __init__(self, wires, out_at, chunks):
+        self.wires, self.out_at, self.chunks = wires, out_at, chunks
+        self.s, self.near, self.far, self.cross = seq_places()
+        self.there, self.here, self.onward = [], [], []
+
+    def send(self, c, src):
+        self.there.append(self.wires.go(src, self.out_at(self.s, c), {"seq": self.far}))
+        self.here.append(self.wires.go(src, self.out_at(self.s, c), {"seq": self.near}))
+
+    def forward(self, c):
+        self.there[c].wait_recv()
+        view = self.out_at(self.far, c)
+        self.onward.append(self.wires.go(view, view, {"seq": self.near}))
+
+    def finish(self):
+        for a in self.here + self.onward:
+            a.wait_recv()
+        for a in self.there + self.here + self.onward:
+            a.wait_send()
+
+
+def vm_spec():
+    return pl.BlockSpec(memory_space=pltpu.VMEM)
+
+
+def any_spec():
+    return pl.BlockSpec(memory_space=pl.ANY)
+
+
+def wires_scratch(n):
+    return [pltpu.SemaphoreType.DMA((n,)), pltpu.SemaphoreType.DMA((n,))]
+
+
+def call_params(number, vmem=60):
+    return pltpu.CompilerParams(collective_id=number, has_side_effects=True, vmem_limit_bytes=vmem << 20)
+
+
+def inverse_rms(v):
+    return lax.rsqrt(jnp.mean(v * v, axis=-1, keepdims=True) + epsilon)
+
+
+def norm_back(grad, v, r, gain):
+    scaled = grad * gain
+    return r * scaled - v * (r * r * r) * jnp.mean(v * scaled, axis=-1, keepdims=True)
+
+
+def tokens_gather_kernel(src, out, send, recv, local):
+    rows = src.shape[0]
+    s, near, far, cross = seq_places()
+    meet([{"seq": near}, {"seq": far}])
+    half = rows // 2
+    ring = SeqGather(Wires(send, recv), lambda t, c: out.at[rows_at(t, rows, c * half, half), :], 2)
+    own = pltpu.make_async_copy(src, out.at[rows_at(s, rows), :], local)
+    own.start()
+    for c in range(2):
+        ring.send(c, src.at[pl.ds(c * half, half), :])
+    for c in range(2):
+        ring.forward(c)
+    own.wait()
+    ring.finish()
+
+
+def tokens_gather(tokens, nseq):
+    rows, width = tokens.shape
+    return pl.pallas_call(
+        tokens_gather_kernel,
+        out_shape=jax.ShapeDtypeStruct((nseq * rows, width), BF16),
+        in_specs=[any_spec()],
+        out_specs=any_spec(),
+        scratch_shapes=wires_scratch(6) + [pltpu.SemaphoreType.DMA],
+        compiler_params=call_params(0, 4),
+        name="tokens_gather",
+    )(tokens)
+
+
+def mix_kernel(o, out_w, tok, gain, obuf, resid, n2, send, recv, own, local):
+    rows, width = tok.shape
+    piece = o.shape[1]
+    nseq = obuf.shape[0]
+    s, near, far, cross = seq_places()
+    meet([{"seq": near}, {"seq": far}, {"seq": cross}])
+    wires = Wires(send, recv)
+    trips = [wires.go(o.at[rows_at(t, rows), :], obuf.at[s], {"seq": t}) for t in (far, cross, near)]
+    obuf[s] = o[rows_at(s, rows), :]
+    half = rows // 2
+    for a in trips:
+        a.wait_recv()
+    ring = SeqGather(wires, lambda t, c: n2.at[rows_at(t, rows, c * half, half), :], 2)
+    for c in range(2):
+        part = slice(c * half, (c + 1) * half)
+        cols = out_w.shape[2]
+        for u in range(nseq):
+            acc = tok[part, u * cols : (u + 1) * cols].astype(F32)
+            for t in range(nseq):
+                acc = acc + nn(obuf[t, part, :], out_w[u, t * piece : (t + 1) * piece, :])
+            resid[part, u * cols : (u + 1) * cols] = acc
+        h = resid[part, :]
+        own[part, :] = (h * inverse_rms(h) * gain[...]).astype(BF16)
+        ring.send(c, own.at[pl.ds(c * half, half), :])
+    mineblock = pltpu.make_async_copy(own, n2.at[rows_at(s, rows), :], local)
+    mineblock.start()
+    for c in range(2):
+        ring.forward(c)
+    mineblock.wait()
+    ring.finish()
+    for a in trips:
+        a.wait_send()
+
+
+def mix(o, out_w, tok, gain):
+    nseq = out_w.shape[0]
+    rows, width = tok.shape
+    return pl.pallas_call(
+        mix_kernel,
+        out_shape=(
+            jax.ShapeDtypeStruct((nseq, rows, o.shape[1]), BF16),
+            jax.ShapeDtypeStruct((rows, width), F32),
+            jax.ShapeDtypeStruct((nseq * rows, width), BF16),
+        ),
+        in_specs=[vm_spec()] * 4,
+        out_specs=(vm_spec(), vm_spec(), any_spec()),
+        scratch_shapes=wires_scratch(9) + [pltpu.VMEM((rows, width), BF16), pltpu.SemaphoreType.DMA],
+        compiler_params=call_params(2, 32),
+        name="mix",
+    )(o, out_w, tok, gain)
+
+
+class SeqScatter:
+    def __init__(self, wires, to_near, from_near, to_far, from_far, to_own, from_own):
+        self.s, self.near, self.far, self.cross = seq_places()
+        self.wires = wires
+        self.bufs = (to_near, from_near, to_far, from_far, to_own, from_own)
+        self.first, self.second, self.third = [], [], []
+
+    def cross_chunk(self, c, value):
+        self.bufs[0][c] = value.astype(BF16)
+        self.first.append(self.wires.go(self.bufs[0].at[c], self.bufs[1].at[c], {"seq": self.near}))
+
+    def far_chunk(self, c, value):
+        self.first[c].wait_recv()
+        self.bufs[2][c] = (value + self.bufs[1][c].astype(F32)).astype(BF16)
+        self.second.append(self.wires.go(self.bufs[2].at[c], self.bufs[3].at[c], {"seq": self.far}))
+
+    def near_chunk(self, c, value):
+        self.bufs[4][c] = value.astype(BF16)
+        self.third.append(self.wires.go(self.bufs[4].at[c], self.bufs[5].at[c], {"seq": self.near}))
+
+    def own_chunk(self, c, value):
+        self.third[c].wait_recv()
+        self.second[c].wait_recv()
+        return value + self.bufs[5][c].astype(F32) + self.bufs[3][c].astype(F32)
+
+    def finish(self):
+        for a in self.first + self.second + self.third:
+            a.wait_send()
+
+
+def scatter_scratch(chunks, rows, width):
+    return [pltpu.VMEM((chunks, rows, width), BF16)] * 6
+
+
+def unmix_kernel(
+    chunks, dg, du, gate_w, up_w, resid, gain, cot, out_w, obuf,
+    rgrad, dmix, wgrad, ggrad,
+    send, recv, b0, b1, b2, b3, b4, b5, attn, dob,
+):
+    rows, width = resid.shape
+    nseq, _, piece = obuf.shape
+    s, near, far, cross = seq_places()
+    meet([{"seq": near}, {"seq": far}, {"seq": cross}])
+    wires = Wires(send, recv)
+    sums = SeqScatter(wires, b0, b1, b2, b3, b4, b5)
+    size = rows // chunks
+
+    def part(t, c):
+        at = rows_at(t, rows, c * size, size)
+        return nt(dg[at, :], gate_w[...]) + nt(du[at, :], up_w[...])
+
+    for c in range(chunks):
+        sums.cross_chunk(c, part(cross, c))
+    for c in range(chunks):
+        sums.far_chunk(c, part(far, c))
+    for c in range(chunks):
+        sums.near_chunk(c, part(near, c))
+    for c in range(chunks):
+        rgrad[c * size : (c + 1) * size, :] = part(s, c)
+    total = jnp.zeros((1, width), F32)
+    trips = []
+    for c in range(chunks):
+        at = slice(c * size, (c + 1) * size)
+        dn = sums.own_chunk(c, rgrad[at, :])
+        h = resid[at, :]
+        r = inverse_rms(h)
+        total = total + jnp.sum(dn * h * r, axis=0, keepdims=True)
+        rg = cot[at, :].astype(F32) + norm_back(dn, h, r, gain[...])
+        rgrad[at, :] = rg
+        low = rg.astype(BF16)
+        attn[at, :] = low
+        cols = out_w.shape[2]
+        for t in range(nseq):
+            acc = jnp.zeros((size, piece), F32)
+            for u in range(nseq):
+                acc = acc + nt(low[:, u * cols : (u + 1) * cols], out_w[u, t * piece : (t + 1) * piece, :])
+            dob[t, at, :] = acc.astype(BF16)
+    ggrad[...] = jnp.broadcast_to(total, ggrad.shape)
+    for t in (far, cross, near):
+        trips.append(wires.go(dob.at[t], dmix.at[rows_at(s, rows), :], {"seq": t}))
+    dmix[rows_at(s, rows), :] = dob[s]
+    cols = out_w.shape[2]
+    for t in range(nseq):
+        for u in range(nseq):
+            wgrad[u, t * piece : (t + 1) * piece, :] = lax.dot_general(
+                obuf[t], attn[:, u * cols : (u + 1) * cols], (((0,), (0,)), ((), ())), preferred_element_type=F32
+            ).astype(BF16)
+    for a in trips:
+        a.wait()
+    sums.finish()
+
+
+def unmix(dg, du, gate_w, up_w, resid, gain, cot, out_w, obuf, chunks=2):
+    rows, width = resid.shape
+    nseq, _, piece = obuf.shape
+    return pl.pallas_call(
+        functools.partial(unmix_kernel, chunks),
+        out_shape=(
+            jax.ShapeDtypeStruct((rows, width), F32),
+            jax.ShapeDtypeStruct((nseq * rows, piece), BF16),
+            jax.ShapeDtypeStruct(out_w.shape, BF16),
+            jax.ShapeDtypeStruct((8, width), F32),
+        ),
+        in_specs=[vm_spec()] * 9,
+        out_specs=(vm_spec(),) * 4,
+        scratch_shapes=wires_scratch(3 * chunks + 3)
+        + scatter_scratch(chunks, rows // chunks, width)
+        + [pltpu.VMEM((rows, width), BF16), pltpu.VMEM((nseq, rows, piece), BF16)],
+        compiler_params=call_params(4),
+        name="unmix",
+    )(dg, du, gate_w, up_w, resid, gain, cot, out_w, obuf)
+
+
+def input_kernel(chunks, dqkv, qkv_w, tok, gain, rgrad, in_grad, ggrad, send, recv, b0, b1, b2, b3, b4, b5, hold):
+    rows, width = tok.shape
+    s, near, far, cross = seq_places()
+    meet([{"seq": near}, {"seq": far}])
+    wires = Wires(send, recv)
+    sums = SeqScatter(wires, b0, b1, b2, b3, b4, b5)
+    size = rows // chunks
+    used = dqkv.shape[1]
+
+    def part(t, c):
+        return nt(dqkv[rows_at(t, rows, c * size, size), :], qkv_w[:, :used])
+
+    for c in range(chunks):
+        sums.cross_chunk(c, part(cross, c))
+    for c in range(chunks):
+        sums.far_chunk(c, part(far, c))
+    for c in range(chunks):
+        sums.near_chunk(c, part(near, c))
+    for c in range(chunks):
+        hold[c * size : (c + 1) * size, :] = part(s, c)
+    total = jnp.zeros((1, width), F32)
+    for c in range(chunks):
+        at = slice(c * size, (c + 1) * size)
+        dn = sums.own_chunk(c, hold[at, :])
+        x = tok[at, :].astype(F32)
+        r = inverse_rms(x)
+        total = total + jnp.sum(dn * x * r, axis=0, keepdims=True)
+        in_grad[at, :] = (rgrad[at, :] + norm_back(dn, x, r, gain[...])).astype(BF16)
+    ggrad[...] = jnp.broadcast_to(total, ggrad.shape)
+    sums.finish()
+
+
+def input_grads(dqkv, qkv_w, tok, gain, rgrad, chunks=2):
+    rows, width = tok.shape
+    return pl.pallas_call(
+        functools.partial(input_kernel, chunks),
+        out_shape=(jax.ShapeDtypeStruct((rows, width), BF16), jax.ShapeDtypeStruct((8, width), F32)),
+        in_specs=[vm_spec()] * 5,
+        out_specs=(vm_spec(),) * 2,
+        scratch_shapes=wires_scratch(3 * chunks)
+        + scatter_scratch(chunks, rows // chunks, width)
+        + [pltpu.VMEM((rows, width), F32)],
+        compiler_params=call_params(6, 40),
+        name="input_grads",
+    )(dqkv, qkv_w, tok, gain, rgrad)
 
 
 def build_strips(heads, starts, table, ids, strip, far):
@@ -62,7 +392,25 @@
     return jnp.concatenate(parts, axis=0)
 
 
-def attn_fwd_kernel(heads, starts, table, ids, q, k, v, o, lse, strip, far, kh, vt, ot, s, p):
+def attn_fwd_kernel(
+    heads, starts, table, ids, q, k, v, out_q, cot, o, lse, out_w, cots, strip, far, kh, vt, ot, s, send, recv, local
+):
+    rows = cot.shape[0]
+    mine, near, other, cross = seq_places()
+    meet([{"seq": near}, {"seq": other}])
+    wires = Wires(send, recv)
+    half = rows // 2
+    wring = SeqGather(wires, lambda t, c: out_w.at[t], 1)
+    cring = SeqGather(wires, lambda t, c: cots.at[rows_at(t, rows, c * half, half), :], 2)
+    wring.send(0, out_q)
+    for c in range(2):
+        cring.send(c, cot.at[pl.ds(c * half, half), :])
+    own = [
+        pltpu.make_async_copy(out_q, out_w.at[mine], local.at[0]),
+        pltpu.make_async_copy(cot, cots.at[rows_at(mine, rows), :], local.at[1]),
+    ]
+    for a in own:
+        a.start()
     build_strips(heads, starts, table, ids, strip, far)
     masked_copies(k, kh, heads)
     vt[...] = v[...].astype(F32).T.astype(BF16)
@@ -103,11 +451,18 @@
         block(h, q0, 0, chunks, c)
         return carry
 
+    wring.forward(0)
     lax.fori_loop(0, heads * 2, cont_body, 0)
     o[...] = ot[...].T.astype(BF16)
-
-
-def attn_fwd(starts, table, ids, q, k, v):
+    for c in range(2):
+        cring.forward(c)
+    for a in own:
+        a.wait()
+    wring.finish()
+    cring.finish()
+
+
+def attn_fwd(starts, table, ids, q, k, v, out_q, cot, nseq):
     rows, width = q.shape
     heads = width // HEAD_DIM
     smem = pl.BlockSpec(memory_space=pltpu.SMEM)
@@ -117,9 +472,11 @@
         out_shape=(
             jax.ShapeDtypeStruct((rows, width), BF16),
             jax.ShapeDtypeStruct((8, rows), F32),
+            jax.ShapeDtypeStruct((nseq,) + out_q.shape, BF16),
+            jax.ShapeDtypeStruct((rows, cot.shape[1]), BF16),
         ),
-        in_specs=[smem, smem, vm, vm, vm, vm],
-        out_specs=(vm, vm),
+        in_specs=[smem, smem, vm, vm, vm, vm, any_spec(), any_spec()],
+        out_specs=(vm, vm, any_spec(), any_spec()),
         scratch_shapes=[
             pltpu.VMEM((heads, 128, STRIP), F32),
             pltpu.VMEM((heads, 2, 128, FARW), F32),
@@ -127,22 +484,48 @@
             pltpu.VMEM((width, rows), BF16),
             pltpu.VMEM((width, rows), F32),
             pltpu.VMEM((PROMPT + CL, CL), F32),
-            pltpu.VMEM((PROMPT + CL, CL), BF16),
-        ],
-        compiler_params=pltpu.CompilerParams(vmem_limit_bytes=56 << 20),
+        ]
+        + wires_scratch(9)
+        + [pltpu.SemaphoreType.DMA((2,))],
+        compiler_params=call_params(1, 40),
         name="attend_forward",
-    )(starts, table, ids, q, k, v)
+    )(starts, table, ids, q, k, v, out_q, cot)
 
 
 def attn_bwd_kernel(
-    heads, starts, table, ids, q, k, v, o, do, lse,
-    dq, dk, dv, tgrad,
+    heads, starts, table, ids, q, k, v, o, do, lse, resid, ypart, wpart,
+    dq, dk, dv, tgrad, y, wsum,
     strip, far, kh, vh, qh, doh, kt, delta, dqt, gstrip, gfar,
+    send, recv, local, ybuf, wbuf,
 ):
+    rows = resid.shape[0]
+    mine, near, other, cross = seq_places()
+    meet([{"seq": near}, {"seq": other}])
+    wires = Wires(send, recv)
+
+    def block_of(part, t):
+        return part.at[rows_at(t, rows), :] if part is ypart else part.at[t]
+
+    pairs = ((wpart, wbuf), (ypart, ybuf))
+    hops = [wires.go(block_of(part, cross), buf.at[0], {"seq": near}) for part, buf in pairs]
+    turns = [wires.go(block_of(part, near), buf.at[1], {"seq": near}) for part, buf in pairs]
+    loads = []
+    for n, (part, buf) in enumerate(pairs):
+        loads.append(pltpu.make_async_copy(block_of(part, other), buf.at[2], local.at[2 * n]))
+        loads.append(pltpu.make_async_copy(block_of(part, mine), buf.at[3], local.at[2 * n + 1]))
+    for a in loads:
+        a.start()
     build_strips(heads, starts, table, ids, strip, far)
     for src, dst in ((k, kh), (v, vh), (q, qh), (do, doh)):
         masked_copies(src, dst, heads)
     kt[...] = k[...].astype(F32).T.astype(BF16)
+    far_hops = []
+    for n, (part, buf) in enumerate(pairs):
+        loads[2 * n].wait()
+        hops[n].wait_recv()
+        buf[2] = (buf[2].astype(F32) + buf[0].astype(F32)).astype(BF16)
+    for part, buf in pairs:
+        far_hops.append(wires.go(buf.at[2], buf.at[4], {"seq": other}))
     prod = (o[...].astype(F32) * do[...].astype(F32)).T
     for h in range(heads):
         delta[h : h + 1, :] = jnp.sum(prod[h * HEAD_DIM : (h + 1) * HEAD_DIM, :], axis=0, keepdims=True)
@@ -222,9 +605,19 @@
             total = total + pltpu.roll(piece, PROMPT // 2 + starts[c], 1)
         picked = jnp.where(hot, total[:1, :], 0.0)
         tgrad[h] = jnp.broadcast_to(jnp.sum(picked, axis=1, keepdims=True), tgrad.shape[1:])
-
-
-def attn_bwd(starts, table, ids, q, k, v, o, do, lse):
+    sums = []
+    for n, (part, buf) in enumerate(pairs):
+        loads[2 * n + 1].wait()
+        turns[n].wait_recv()
+        far_hops[n].wait_recv()
+        sums.append(buf[3].astype(F32) + buf[1].astype(F32) + buf[4].astype(F32))
+    wsum[...] = sums[0].astype(BF16)
+    y[...] = (resid[...] + sums[1]).astype(BF16)
+    for a in hops + turns + far_hops:
+        a.wait_send()
+
+
+def attn_bwd(starts, table, ids, q, k, v, o, do, lse, resid, ypart, wpart):
     rows, width = q.shape
     heads = width // HEAD_DIM
     smem = pl.BlockSpec(memory_space=pltpu.SMEM)
@@ -232,9 +625,16 @@
     wide = jax.ShapeDtypeStruct((rows, width), F32)
     return pl.pallas_call(
         functools.partial(attn_bwd_kernel, heads),
-        out_shape=(wide, wide, wide, jax.ShapeDtypeStruct((heads, table.shape[0], 128), F32)),
-        in_specs=[smem, smem] + [vm] * 7,
-        out_specs=(vm,) * 4,
+        out_shape=(
+            wide,
+            wide,
+            wide,
+            jax.ShapeDtypeStruct((heads, table.shape[0], 128), F32),
+            jax.ShapeDtypeStruct(resid.shape, BF16),
+            jax.ShapeDtypeStruct(wpart.shape[1:], BF16),
+        ),
+        in_specs=[smem, smem] + [vm] * 8 + [any_spec()] * 2,
+        out_specs=(vm,) * 6,
         scratch_shapes=[
             pltpu.VMEM((heads, 128, STRIP), F32),
             pltpu.VMEM((heads, 2, 128, FARW), F32),
@@ -246,10 +646,16 @@
             pltpu.VMEM((width, rows), F32),
             pltpu.VMEM((heads, 128, STRIP), F32),
             pltpu.VMEM((heads, 2, 128, FARW), F32),
+        ]
+        + wires_scratch(6)
+        + [
+            pltpu.SemaphoreType.DMA((4,)),
+            pltpu.VMEM((5,) + resid.shape, BF16),
+            pltpu.VMEM((5,) + wpart.shape[1:], BF16),
         ],
-        compiler_params=pltpu.CompilerParams(vmem_limit_bytes=60 << 20),
+        compiler_params=call_params(5),
         name="attend_backward",
-    )(starts, table, ids, q, k, v, o, do, lse)
+    )(starts, table, ids, q, k, v, o, do, lse, resid, ypart, wpart)
 
 
 def reversed_ids(bucket_ids):
@@ -291,21 +697,12 @@
     return lax.dot_general(a, b, (((0,), (0,)), ((), ())), preferred_element_type=F32)
 
 
-def inverse_rms(v):
-    return lax.rsqrt(jnp.mean(v * v, axis=-1, keepdims=True) + epsilon)
-
-
 def gelu_both(u):
     inner = 0.7978845608028654 * (u + 0.044715 * u * u * u)
     t = jnp.tanh(inner)
     value = 0.5 * u * (1.0 + t)
     slope = 0.5 * (1.0 + t) + 0.5 * u * (1.0 - t * t) * 0.7978845608028654 * (1.0 + 3 * 0.044715 * u * u)
     return value, slope
-
-
-def norm_back(grad, v, r, gain):
-    scaled = grad * gain
-    return r * scaled - v * (r * r * r) * jnp.mean(v * scaled, axis=-1, keepdims=True)
 
 
 def body(
@@ -340,9 +737,6 @@
     def gather_s(a):
         return lax.all_gather(a, "seq", axis=0, tiled=True)
 
-    def scatter_s(a):
-        return lax.psum_scatter(a.astype(BF16), "seq", scatter_dimension=0, tiled=True).astype(F32)
-
     def scatter_f(a):
         return lax.psum_scatter(a.astype(BF16), "fsdp", scatter_dimension=0, tiled=True)
 
@@ -354,14 +748,12 @@
     gain_two = first[:, 3 * piece + 1].astype(F32)
     out_cols = width // nseq
     out_local = lax.dynamic_slice_in_dim(w_out, mine * out_cols, out_cols, 1)
-    out_w = lax.all_to_all(gather_f(out_local), "seq", split_axis=0, concat_axis=1, tiled=True)
+    out_q = gather_f(out_local)
     gate_w = gather_f(pack_columns(w_gate, nseq, nfsdp, mine))
     up_w = gather_f(pack_columns(w_up, nseq, nfsdp, mine))
     down_w = gather_f(pack_rows(w_down, nseq, mine))
 
-    block = tokens[0].astype(F32)
-    r_one = inverse_rms(block)
-    group = gather_s(tokens[0]).astype(F32)
+    group = tokens_gather(tokens[0], nseq).astype(F32)
     normed = (group * inverse_rms(group) * gain_one).astype(BF16)
     query = dot32(normed, query_w).astype(BF16)
     keys = dot32(normed, key_w).astype(BF16)
@@ -369,37 +761,30 @@
     table = lax.dynamic_slice_in_dim(rel_table, mine * heads, heads, 1)
     ids = reversed_ids(bucket_ids)
     starts = cont_start[0]
-    mixed, lse = attn_fwd(starts, table, ids, query, keys, values)
-    resid = block + scatter_s(dot32(mixed, out_w))
-    r_two = inverse_rms(resid)
-    normed_two = gather_s((resid * r_two * gain_two).astype(BF16))
+    mixed, lse, out_w, cot = attn_fwd(starts, table, ids, query, keys, values, out_q, out_grad[0], nseq)
+    mixed_rows, resid, normed_two = mix(mixed, out_w, tokens[0], gain_two[None])
     gate = dot32(normed_two, gate_w)
     upward = dot32(normed_two, up_w)
     active, slope = gelu_both(gate)
     hidden = (active * upward).astype(BF16)
-    result = resid + scatter_s(dot32(hidden, down_w))
-    cot = gather_s(out_grad[0])
+    result = dot32(hidden, down_w).astype(BF16)
     down_grad = scatter_f(dot_tn(hidden, cot))
-    hidden_grad = lax.dot_general(cot, down_w, (((1,), (1,)), ((), ())), preferred_element_type=F32)
+    hidden_grad = nt(cot, down_w)
     gate_grad = (hidden_grad * upward * slope).astype(BF16)
     up_grad = (hidden_grad * active).astype(BF16)
-    normed_two_grad = scatter_s(nt(gate_grad, gate_w) + nt(up_grad, up_w))
+    resid_grad, mixed_grad, out_w_grad, gain_two_grad = unmix(
+        gate_grad, up_grad, gate_w, up_w, resid, gain_two[None], out_grad[0], out_w, mixed_rows
+    )
     gate_w_grad = scatter_f(dot_tn(normed_two, gate_grad))
     up_w_grad = scatter_f(dot_tn(normed_two, up_grad))
-    gain_two_grad = jnp.sum(normed_two_grad * resid * r_two, axis=0)
-    resid_grad = out_grad[0].astype(F32) + norm_back(normed_two_grad, resid, r_two, gain_two)
-    attn_grad = gather_s(resid_grad.astype(BF16))
-    out_w_grad = dot_tn(mixed, attn_grad).astype(BF16)
-    mixed_grad = nt(attn_grad, out_w).astype(BF16)
-    dq, dk, dv, tgrad = attn_bwd(starts, table, ids, query, keys, values, mixed, mixed_grad, lse)
-    dq, dk, dv = (a.astype(BF16) for a in (dq, dk, dv))
-    normed_grad = scatter_s(nt(dq, query_w) + nt(dk, key_w) + nt(dv, value_w))
-    qkv_grad = scatter_f(dot_tn(normed, jnp.concatenate([dq, dk, dv], axis=1)))
-    gain_one_grad = jnp.sum(normed_grad * block * r_one, axis=0)
-    in_grad = resid_grad + norm_back(normed_grad, block, r_one, gain_one)
-
-    out_grad_cols = lax.all_to_all(out_w_grad, "seq", split_axis=1, concat_axis=0, tiled=True)
-    out_w_grad = lax.all_gather(scatter_f(out_grad_cols), "seq", axis=1, tiled=True)
+    dq, dk, dv, tgrad, block_out, out_w_grad = attn_bwd(
+        starts, table, ids, query, keys, values, mixed, mixed_grad, lse, resid, result, out_w_grad
+    )
+    dqkv = jnp.concatenate([dq, dk, dv], axis=1).astype(BF16)
+    qkv_grad = scatter_f(dot_tn(normed, dqkv))
+    in_grad, gain_one_grad = input_grads(dqkv, first, tokens[0], gain_one[None], resid_grad)
+
+    out_w_grad = lax.all_gather(scatter_f(out_w_grad), "seq", axis=1, tiled=True)
     qkv_grad = lax.all_gather(qkv_grad, "seq", axis=0).reshape(nseq, -1, 3, piece)
     qkv_grad = qkv_grad.transpose(1, 2, 0, 3).reshape(-1, 3, inner).astype(F32)
     gate_w_grad = unpack_columns(lax.all_gather(gate_w_grad, "seq", axis=0), hidden_all, nfsdp)
@@ -409,13 +794,15 @@
     buckets = rel_table.shape[0]
     table_full = jnp.zeros((nseq, heads, buckets), F32)
     table_full = lax.dynamic_update_slice(table_full, tgrad[None, :, :, 0], (mine, jnp.int32(0), jnp.int32(0)))
-    table_grad, gain_one_all, gain_two_all = lax.psum((table_full, gain_one_grad, gain_two_grad), ("seq", "fsdp"))
+    table_grad, gain_one_all, gain_two_all = lax.psum(
+        (table_full, gain_one_grad[0], gain_two_grad[0]), ("seq", "fsdp")
+    )
     share = width // nfsdp
     gain_one_share = lax.dynamic_slice_in_dim(gain_one_all, where * share, share)
     gain_two_share = lax.dynamic_slice_in_dim(gain_two_all, where * share, share)
     return (
-        result.astype(BF16)[None],
-        in_grad.astype(BF16)[None],
+        block_out[None],
+        in_grad[None],
         gain_one_share,
         qkv_grad[:, 0],
         qkv_grad[:, 1],

time: 1130 us -> 721 us (0.64)
  waiting for transfers between devices: 715 us -> 176 us
  Pallas kernels: 53.4 us -> 258 us
  matrix products: 124 us -> 88.3 us
  blocking collectives: 111 us -> 92.1 us
  other arithmetic: 34.9 us -> 18.5 us
    reduce_scatter x5, waiting for transfers between devices: 307 us -> 125 us  [scatter_f(): lax.psum_scatter(a.astype(BF16), 'fsdp', scatter_dimension=0, tiled=True)]
    pallas_call x0 -> x4, Pallas kernels: none -> 162 us  [the longest x1 55.8 us: unmix(): pl.pallas_call(functools.partial(unmix_kernel, chunks), out_shape=(jax.Sh...]
    all_gather x5 -> x1, waiting for transfers between devices: 151 us -> 12.2 us  [gather_s(): return lax.all_gather(a, 'seq', axis=0, tiled=True)]
    all_gather x4, waiting for transfers between devices: 163 us -> 26.8 us  [gather_f(): return lax.all_gather(a, 'fsdp', axis=0, tiled=True)]
    reduce_scatter x4 -> x0, waiting for transfers between devices: 84.3 us -> none  [scatter_s(): lax.psum_scatter(a.astype(BF16), 'seq', scatter_dimension=0, tiled=True)]
    pallas_call x1, Pallas kernels: 19.3 us -> 42.7 us  [attn_fwd(): pl.pallas_call(functools.partial(attn_fwd_kernel, heads), out_shape=(jax....]
    pallas_call x1, Pallas kernels: 34.2 us -> 53.3 us  [attn_bwd(): pl.pallas_call(functools.partial(attn_bwd_kernel, heads), out_shape=(wide...]
    all_to_all x1 -> x0, blocking collectives: 18 us -> none  [body(): lax.all_to_all(out_w_grad, 'seq', split_axis=1, concat_axis=0, tiled=True)]
  transfers between devices with their start and end apart: 21 -> 12, of which waited for: 18 -> 6; matrix products, arithmetic and copies ran while one was open for 14% -> 17% of each run, Pallas kernels for 3% -> 36%
where the time goes in v2:
time: 721 us; the launch traced here: 715 us
  Pallas kernels  258 us (36%)
  waiting for transfers between devices  176 us (24%)
  blocking collectives  92.1 us (13%)
  matrix products  88.3 us (12%)
  local copies, waits for them, and re-layouts  65.7 us (9%)
  other arithmetic  18.5 us (3%)
  between operations  15.1 us (2%)
    reduce_scatter x5, waiting for transfers between devices, scatter_f(): lax.psum_scatter(a.astype(BF16), 'fsdp', scatter_dimension=0, tiled=True)  125 us
    pallas_call x1, Pallas kernels, unmix(): pl.pallas_call(functools.partial(unmix_kernel, chunks), out_shape=(jax.Sh...  55.8 us
    pallas_call x1, Pallas kernels, attn_bwd(): pl.pallas_call(functools.partial(attn_bwd_kernel, heads), out_shape=(wide...  53.3 us
    dot_general x6, matrix products, dot32(): return jnp.dot(a, b, preferred_element_type=F32)  42.8 us
    pallas_call x1, Pallas kernels, attn_fwd(): pl.pallas_call(functools.partial(attn_fwd_kernel, heads), out_shape=(jax....  42.7 us
    pallas_call x1, Pallas kernels, mix(): pl.pallas_call(mix_kernel, out_shape=(jax.ShapeDtypeStruct((nseq, rows, o...  42 us
    psum x1, blocking collectives, body(): lax.psum((table_full, gain_one_grad[0], gain_two_grad[0]), ('seq', 'fsdp'))  39.7 us
    dot_general x4, matrix products, dot_tn(): lax.dot_general(a, b, (((0,), (0,)), ((), ())), preferred_element_type=F32)  35.6 us
  transfers between devices with their start and end apart: 12, of which 6 were waited for; matrix products, arithmetic and copies ran while one was open for 17% of the time, Pallas kernels for 36%

profile of v2, /device:TPU:0, one launch (start us, length us, event | category | flops | bytes accessed | tf_op | source)
XLA Modules:
  0.0 715.4 jit_solution(2267749816005345681)
XLA Ops:
  10.9 5.3 reshape.110
  16.2 4.5 reshape.107
  20.8 1.8 pad_bitcast_fusion
  26.1 31.6 %tokens_gather.1 = bf16[1536,1536]{1,0:T(8,128)(2,1)S(1)} custom-call(bf16[384,1536]{1,0:T(8,128)(2,1)S(1)} %bitcast.76), custom_call_target="tpu_custom_call" | custom-call | tf_op jit(solution)/shard_map/tokens_gather/pallas_call | solution.py:135
  57.7 2.1 copy-done.2
  61.7 3.3 fusion
  65.1 35.4 %all_gather.40.out_q = bf16[768,384]{1,0:T(8,128)(2,1)} all-gather(bf16[96,384]{1,0:T(8,128)(2,1)S(1)} %constant_dynamic-slice_fusion.2), channel_id=1, replica_groups=mesh['seq'=4,'fsdp'=8] {'fsdp'}, dimensions={0}, use_global_device_ids=true | all-gather | bytes 663552 | tf_op jit(solution)/shard_map/all_gather | solution.py:735
  100.5 1.8 convert_reduce_fusion
  102.4 4.2 convolution_convert_fusion.5.v
  106.7 1.7 convolution_convert_fusion.6.k
  108.4 1.6 convolution_convert_fusion.7.q
  110.1 42.7 %attend_forward.1 = (bf16[1536,192]{1,0:T(8,128)(2,1)S(1)}, f32[8,1536]{1,0:T(8,128)S(1)}, bf16[4,768,384]{2,1,0:T(8,128)(2,1)S(1)}, bf16[1536,1536]{1,0:T(8,128)(2,1)S(1)}) custom-call(s32[2]{0:T(128)S(1)} %bitcast.83, f32[32,3]{1,0:T(8,128)S(1)} %copy.90.table, s32[8,3072]{1,0:T(8,128)S(1)} %broadcast_in_dim.8.ids, ...), custom_call_target="tpu_custom_call" | custom-call | tf_op jit(solution)/shard_map/attend_forward/pallas_call | solution.py:470
  153.5 2.2 copy-done.23
  155.6 42.0 %mix.1 = (bf16[4,384,192]{2,1,0:T(8,128)(2,1)S(1)}, f32[384,1536]{1,0:T(8,128)S(1)}, bf16[1536,1536]{1,0:T(8,128)(2,1)S(1)}) custom-call(bf16[1536,192]{1,0:T(8,128)(2,1)S(1)} %get-tuple-element.31.o, bf16[4,768,384]{2,1,0:T(8,128)(2,1)S(1)} %get-tuple-element.33.out_w, bf16[384,1536]{1,0:T(8,128)(2,1)S(1)} %bitcast.77, f32[1,1536]{1,0:T(1,128)S(1)} %reshape.119.gain), custom_call_target="tpu_custom_call" | custom-call | tf_op jit(solution)/shard_map/mix/pallas_call | solution.py:183
  202.2 2.2 copy-done.24
  204.4 9.8 %fusion.20 = f32[1536,1024]{1,0:T(8,128)} fusion(bf16[1536,1536]{1,0:T(8,128)(2,1)} %copy-done.24, bf16[1536,1024]{1,0:T(8,128)(2,1)} %all-gather.17.cloned.1.call-done.gate_w), kind=kOutput, calls=%fused_computation.62 | convolution fusion | flops 4831838208 | bytes 14155776 | tf_op jit(solution)/shard_map/dot_general | solution.py:693
  214.3 9.9 %fusion.19 = f32[1536,1024]{1,0:T(8,128)} fusion(bf16[1536,1536]{1,0:T(8,128)(2,1)} %copy-done.23, bf16[1024,1536]{1,0:T(8,128)(2,1)} %all-gather.13.cloned.1.call-done), kind=kOutput, calls=%fused_computation.61 | convolution fusion | flops 4831838208 | bytes 14155776 | tf_op jit(solution)/shard_map/dot_general | solution.py:22
  224.1 26.8 %all-gather.15.cloned.1.call-done.up_w = bf16[1536,1024]{1,0:T(8,128)(2,1)} async-done(((bf16[192,1024]{1,0:T(8,128)(2,1)}), bf16[1536,1024]{1,0:T(8,128)(2,1)}) %all-gather.15.cloned.1.call-update) | async-done | bytes 3145744 | tf_op jit(solution)/shard_map/all_gather | solution.py:735
  250.9 16.3 %multiply_convert_fusion = (bf16[1536,1024]{1,0:T(8,128)(2,1)}, bf16[1536,1024]{1,0:T(8,128)(2,1)S(1)}, bf16[1536,1024]{1,0:T(8,128)(2,1)}) fusion(f32[1536,1024]{1,0:T(8,128)} %fusion.20, f32[1536,1024]{1,0:T(8,128)} %fusion.19, bf16[1536,1536]{1,0:T(8,128)(2,1)} %copy-done.24, bf16[1536,1024]{1,0:T(8,128)(2,1)} %all-gather.15.cloned.1.call-done.up_w), kind=kOutput, calls=%fused_computation.15 | convolution fusion | flops 4871159808 | bytes 29884416 | tf_op jit(solution)/shard_map/dot_general | solution.py:693
  267.2 1.6 copy-done.25
  268.9 8.9 %convolution_convert_fusion.3 = bf16[1536,1024]{1,0:T(8,128)(2,1)} fusion(bf16[1536,1536]{1,0:T(8,128)(2,1)} %copy-done.24, bf16[1536,1024]{1,0:T(8,128)(2,1)S(1)} %get-tuple-element.56.dg), kind=kOutput, calls=%fused_computation.20 | convolution fusion | flops 4833411072 | bytes 11010048 | tf_op jit(solution)/shard_map/dot_general | solution.py:697
  277.8 9.4 %convolution_convert_fusion.2 = bf16[1536,1024]{1,0:T(8,128)(2,1)} fusion(bf16[1536,1536]{1,0:T(8,128)(2,1)} %copy-done.24, bf16[1536,1024]{1,0:T(8,128)(2,1)} %get-tuple-element.57.du), kind=kOutput, calls=%fused_computation.19 | convolution fusion | flops 4833411072 | bytes 11010048 | tf_op jit(solution)/shard_map/dot_general | solution.py:697
  287.3 9.4 %convolution_convert_fusion.1 = bf16[1024,1536]{1,0:T(8,128)(2,1)} fusion(bf16[1536,1024]{1,0:T(8,128)(2,1)} %get-tuple-element.55, bf16[1536,1536]{1,0:T(8,128)(2,1)} %copy-done.23), kind=kOutput, calls=%fused_computation.18 | convolution fusion | flops 4833411072 | bytes 11010048 | tf_op jit(solution)/shard_map/dot_general | solution.py:697
  297.0 55.8 %unmix.1 = (f32[384,1536]{1,0:T(8,128)}, bf16[1536,192]{1,0:T(8,128)(2,1)}, bf16[4,768,384]{2,1,0:T(8,128)(2,1)}, f32[8,1536]{1,0:T(8,128)}) custom-call(bf16[1536,1024]{1,0:T(8,128)(2,1)} %copy-done.25, bf16[1536,1024]{1,0:T(8,128)(2,1)} %get-tuple-element.57.du, bf16[1536,1024]{1,0:T(8,128)(2,1)} %all-gather.17.cloned.1.call-done.gate_w, ...), custom_call_target="tpu_custom_call" | custom-call | tf_op jit(solution)/shard_map/unmix/pallas_call | solution.py:293
  352.8 9.2 %convolution_convert_fusion.ypart = bf16[1536,1536]{1,0:T(8,128)(2,1)} fusion(bf16[1536,1024]{1,0:T(8,128)(2,1)} %get-tuple-element.55, bf16[1024,1536]{1,0:T(8,128)(2,1)} %all-gather.13.cloned.1.call-done), kind=kOutput, calls=%fused_computation.7 | convolution fusion | flops 4834197504 | bytes 11010048 | tf_op jit(solution)/shard_map/dot_general | solution.py:693
  362.0 53.3 %attend_backward.1 = (f32[1536,192]{1,0:T(8,128)}, f32[1536,192]{1,0:T(8,128)}, f32[1536,192]{1,0:T(8,128)}, f32[3,32,128]{2,1,0:T(8,128)}, bf16[384,1536]{1,0:T(8,128)(2,1)}, /*index=5*/bf16[768,384]{1,0:T(8,128)(2,1)}) custom-call(s32[2]{0:T(128)} %bitcast.82, f32[32,3]{1,0:T(8,128)} %copy-done.19, s32[8,3072]{1,0:T(8,128)} %copy-done.17, ...), custom_call_target="tpu_custom_call" | custom-call | tf_op jit(solution)/shard_map/attend_backward/pallas_call | solution.py:626
  415.4 1.6 convert.17
  419.3 7.9 %convolution_convert_fusion.4 = bf16[1536,576]{1,0:T(8,128)(2,1)} fusion(bf16[1536,576]{1,0:T(8,128)(2,1)S(1)} %pad_maximum_fusion.dqkv, bf16[1536,1536]{1,0:T(8,128)(2,1)} %copy-done.2, f32[1536]{0:T(1024)S(1)} %get-tuple-element.51, f32[1536]{0:T(1024)S(1)} %add_rsqrt_fusion), kind=kOutput, calls=%fused_computation.21 | convolution fusion | flops 2728230912 | bytes 8269824 | tf_op jit(solution)/shard_map/dot_general | solution.py:697
  429.0 76.6 %reduce-scatter.14.cloned.1.call-done = bf16[128,1536]{1,0:T(8,128)(2,1)} async-done(((bf16[1024,1536]{1,0:T(8,128)(2,1)}), bf16[128,1536]{1,0:T(8,128)(2,1)}) %reduce-scatter.14.cloned.1.call-update) | async-done | bytes 393232 | tf_op jit(solution)/shard_map/reduce_scatter | solution.py:741
  505.6 1.5 copy-done.8
  507.2 1.7 copy-done.14
  508.8 33.0 %input_grads.1 = (bf16[384,1536]{1,0:T(8,128)(2,1)S(1)}, f32[8,1536]{1,0:T(8,128)S(1)}) custom-call(bf16[1536,576]{1,0:T(8,128)(2,1)S(1)} %pad_maximum_fusion.dqkv, bf16[1536,640]{1,0:T(8,128)(2,1)S(1)} %copy-done.8, bf16[384,1536]{1,0:T(8,128)(2,1)S(1)} %bitcast.78, f32[1,1536]{1,0:T(1,128)S(1)} %reshape.120.gain, f32[384,1536]{1,0:T(8,128)S(1)} %copy-done.14), custom_call_target="tpu_custom_call" | custom-call | tf_op jit(solution)/shard_map/input_grads/pallas_call | solution.py:345
  543.8 39.7 %all-reduce.4 = (f32[1536]{0:T(1024)S(1)}, f32[1536]{0:T(1024)S(1)}, f32[32,12]{0,1:T(8,128)}) all-reduce(f32[1536]{0:T(1024)S(1)} %slice_reduce_fusion.2, f32[1536]{0:T(1024)S(1)} %slice_reduce_fusion.1, f32[32,12]{0,1:T(8,128)S(1)} %bitcast.94), channel_id=1, replica_groups=mesh['seq'=4,'fsdp'=8] {'seq','fsdp'}, use_global_device_ids=true, to_apply=%region_1.2 | all-reduce | flops 3456 | bytes 27648 | tf_op jit(solution)/shard_map/psum | solution.py:797
  584.7 6.9 all_gather.46
  592.5 47.9 %reduce-scatter.16.cloned.1.call-done = bf16[192,576]{1,0:T(8,128)(2,1)} async-done(((bf16[1536,576]{1,0:T(8,128)(2,1)}), bf16[192,576]{1,0:T(8,128)(2,1)}) %reduce-scatter.16.cloned.1.call-update) | async-done | bytes 221200 | tf_op jit(solution)/shard_map/reduce_scatter | solution.py:741
  640.4 10.1 %all-gather = bf16[768,576]{1,0:T(8,128)(2,1)S(1)} all-gather(bf16[192,576]{1,0:T(8,128)(2,1)} %reduce-scatter.16.cloned.1.call-done), channel_id=2, replica_groups=mesh['seq'=4,'fsdp'=8] {'seq'}, dimensions={0}, use_global_device_ids=true | all-gather | bytes 1105920 | tf_op jit(solution)/shard_map/all_gather | solution.py:788
  651.8 2.9 reshape.124
  654.6 2.5 copy.81
  657.1 2.8 reshape.121
  661.2 1.8 copy.93
  663.2 2.1 slice_convert_fusion.1
  665.3 4.8 reshape.122
  670.1 11.5 %all-gather.23.cloned.1.call-done = bf16[768,1024]{1,0:T(8,128)(2,1)} async-done(((bf16[192,1024]{1,0:T(8,128)(2,1)}), bf16[768,1024]{1,0:T(8,128)(2,1)}) %all-gather.23.cloned.1.call-update) | async-done | bytes 1572880 | tf_op jit(solution)/shard_map/all_gather | solution.py:791
  681.6 1.8 copy.94
  683.7 2.1 slice_convert_fusion
  685.7 4.8 reshape.123
  690.6 12.2 %all-gather.19.cloned.1.call-done = bf16[512,1536]{1,0:T(8,128)(2,1)} async-done(((bf16[128,1536]{1,0:T(8,128)(2,1)}), bf16[512,1536]{1,0:T(8,128)(2,1)}) %all-gather.19.cloned.1.call-update) | async-done | bytes 1572880 | tf_op jit(solution)/shard_map/all_gather | solution.py:738
  702.7 3.5 slice_convert_fusion.2
  (132 shorter events, 27.7 us)
Async XLA Ops:
  7.2 1.6 copy-start
  7.2 93.3 %all-gather.11.cloned.1.call-start = ((), (), s32[]{:S(2)}) async-start(), calls=%async_computation.5 | async-start | bytes 2211840 | tf_op jit(solution)/shard_map/all_gather | solution.py:735
  10.9 193.6 %all-gather.17.cloned.1.call-start = ((), (), s32[]{:S(2)}) async-start(), calls=%async_computation.8 | async-start | bytes 3538944 | tf_op jit(solution)/shard_map/all_gather | solution.py:735
  22.8 1.5 copy-start.27
  22.8 3.3 copy-start.3
  23.8 190.5 %all-gather.13.cloned.1.call-start = ((), (), s32[]{:S(2)}) async-start(), calls=%async_computation.6 | async-start | bytes 3538944 | tf_op jit(solution)/shard_map/all_gather | solution.py:735
  25.1 225.8 %all-gather.15.cloned.1.call-start = ((), (), s32[]{:S(2)}) async-start(), calls=%async_computation.7 | async-start | bytes 3538944 | tf_op jit(solution)/shard_map/all_gather | solution.py:735
  26.0 34.6 %copy-start.30 = (s32[3071]{0:T(1024)S(1)}, s32[3071]{0:T(1024)}, u32[]{:S(2)}) copy-start(s32[3071]{0:T(1024)} %param.26) | copy-start | bytes 36856
  26.0 401.3 %reduce-scatter.10.cloned.1.call-start = ((), (), s32[]{:S(2)}) async-start(), calls=%async_computation.10 | async-start | bytes 3538944 | tf_op jit(solution)/shard_map/reduce_scatter | solution.py:741
  57.7 2.1 copy-start.2
  60.6 49.5 %copy-start.19 = (f32[32,3]{1,0:T(8,128)}, f32[32,3]{1,0:T(8,128)S(1)}, u32[]{:S(2)}) copy-start(f32[32,3]{1,0:T(8,128)S(1)} %copy.90.table) | copy-start | bytes 1156
  100.5 6.1 slice-start
  102.3 53.3 %copy-start.20 = (f32[1,1536]{1,0:T(1,128)}, f32[1,1536]{1,0:T(1,128)S(1)}, u32[]{:S(2)}) copy-start(f32[1,1536]{1,0:T(1,128)S(1)} %reshape.119.gain) | copy-start | bytes 18436
  102.3 4.3 slice-start.1
  102.4 4.3 copy-start.7
  106.6 3.5 copy-start.9
  108.4 1.7 copy-start.10
  108.4 1.7 copy-start.6
  108.4 1.7 copy-start.13
  108.4 1.7 copy-start.22
  110.0 87.6 %copy-start.11 = (bf16[1536,192]{1,0:T(8,128)(2,1)}, bf16[1536,192]{1,0:T(8,128)(2,1)S(1)}, u32[]{:S(2)}) copy-start(bf16[1536,192]{1,0:T(8,128)(2,1)S(1)} %convolution_convert_fusion.7.q) | copy-start | bytes 1769476
  110.1 45.6 %copy-start.17 = (s32[8,3072]{1,0:T(8,128)}, s32[8,3072]{1,0:T(8,128)S(1)}, u32[]{:S(2)}) copy-start(s32[8,3072]{1,0:T(8,128)S(1)} %broadcast_in_dim.8.ids) | copy-start | bytes 294916
  152.9 0.6 copy-start.21
  153.5 2.2 copy-start.23
  197.6 1.4 copy-start.4
  199.0 1.4 copy-start.5
  200.4 0.9 copy-start.12
  201.3 0.9 copy-start.18
  202.2 2.2 copy-start.24
  267.2 1.6 copy-start.25
  277.8 150.6 %reduce-scatter.12.cloned.1.call-start = ((), (), s32[]{:S(2)}) async-start(), calls=%async_computation.11 | async-start | bytes 3538944 | tf_op jit(solution)/shard_map/reduce_scatter | solution.py:741
  287.2 218.3 %reduce-scatter.14.cloned.1.call-start = ((), (), s32[]{:S(2)}) async-start(), calls=%async_computation.12 | async-start | bytes 3538944 | tf_op jit(solution)/shard_map/reduce_scatter | solution.py:741
  296.7 288.0 %reduce-scatter.8.cloned.1.call-start = ((), (), s32[]{:S(2)}) async-start(), calls=%async_computation.9 | async-start | bytes 663552 | tf_op jit(solution)/shard_map/reduce_scatter | solution.py:741
  415.3 3.2 copy-start.26
  415.3 225.1 %reduce-scatter.16.cloned.1.call-start = ((), (), s32[]{:S(2)}) async-start(), calls=%async_computation.16 | async-start | bytes 2211840 | tf_op jit(solution)/shard_map/reduce_scatter | solution.py:741
  419.3 9.6 %copy-start.29 = (f32[3,32,128]{2,1,0:T(8,128)S(1)}, f32[3,32,128]{2,1,0:T(8,128)}, u32[]{:S(2)}) copy-start(f32[3,32,128]{2,1,0:T(8,128)} %get-tuple-element.49) | copy-start | bytes 147460
  427.3 233.9 %all-gather.21.cloned.1.call-start = ((), (), s32[]{:S(2)}) async-start(), calls=%async_computation.14 | async-start | bytes 1966080 | tf_op jit(solution)/shard_map/all_gather | solution.py:790
  427.9 253.7 %all-gather.23.cloned.1.call-start = ((), (), s32[]{:S(2)}) async-start(), calls=%async_computation.15 | async-start | bytes 1966080 | tf_op jit(solution)/shard_map/all_gather | solution.py:791
  428.6 274.1 %all-gather.19.cloned.1.call-start = ((), (), s32[]{:S(2)}) async-start(), calls=%async_computation.13 | async-start | bytes 1966080 | tf_op jit(solution)/shard_map/all_gather | solution.py:738
  505.6 1.5 copy-start.8
  507.2 1.7 copy-start.14
  541.9 1.0 copy-start.15
  690.6 15.6 %copy-start.28 = (bf16[384,1536]{1,0:T(8,128)(2,1)S(1)}, bf16[384,1536]{1,0:T(8,128)(2,1)}, u32[]{:S(2)}) copy-start(bf16[384,1536]{1,0:T(8,128)(2,1)} %get-tuple-element.40) | copy-start | bytes 3538948
  690.6 16.6 %copy-start.16 = (bf16[384,1536]{1,0:T(8,128)(2,1)S(1)}, bf16[384,1536]{1,0:T(8,128)(2,1)}, u32[]{:S(2)}) copy-start(bf16[384,1536]{1,0:T(8,128)(2,1)} %copy-done.15) | copy-start | bytes 3538948
  702.7 5.5 copy-start.1
Sparse Core Ops, SparseCore 0:
  11.0 50.2 all-gather.10
  64.0 62.8 all-gather.16
  129.7 59.5 all-gather.12
  191.8 59.0 all-gather.14
  277.9 73.1 reduce-scatter.9
  354.6 73.7 reduce-scatter.11
  432.0 73.5 reduce-scatter.13
  508.9 61.3 reduce-scatter.7
  574.7 65.6 reduce-scatter.15
  641.8 18.5 all-gather.20
  661.9 19.6 all-gather.22
  683.0 19.6 all-gather.18

commit v3 on v2

--- a/solution.py
+++ b/solution.py
@@ -30,9 +30,11 @@
     def __init__(self, send, recv):
         self.send, self.recv, self.used = send, recv, 0
 
-    def copy(self, src, dst, where):
-        i = self.used
-        self.used += 1
+    def take(self, count):
+        self.used += count
+        return self.used - count
+
+    def at(self, i, src, dst, where):
         return pltpu.make_async_remote_copy(
             src_ref=src,
             dst_ref=dst,
@@ -43,7 +45,7 @@
         )
 
     def go(self, src, dst, where):
-        c = self.copy(src, dst, where)
+        c = self.at(self.take(1), src, dst, where)
         c.start()
         return c
 
@@ -71,22 +73,140 @@
     def __init__(self, wires, out_at, chunks):
         self.wires, self.out_at, self.chunks = wires, out_at, chunks
         self.s, self.near, self.far, self.cross = seq_places()
-        self.there, self.here, self.onward = [], [], []
+        self.base = wires.take(3 * chunks)
+
+    def trip(self, kind, c, src=None):
+        view = self.out_at(self.far if kind == 2 else self.s, c)
+        where = {"seq": self.far if kind == 0 else self.near}
+        return self.wires.at(self.base + 3 * c + kind, view if src is None else src, view, where)
 
     def send(self, c, src):
-        self.there.append(self.wires.go(src, self.out_at(self.s, c), {"seq": self.far}))
-        self.here.append(self.wires.go(src, self.out_at(self.s, c), {"seq": self.near}))
+        self.trip(0, c, src).start()
+        self.trip(1, c, src).start()
 
     def forward(self, c):
-        self.there[c].wait_recv()
-        view = self.out_at(self.far, c)
-        self.onward.append(self.wires.go(view, view, {"seq": self.near}))
+        self.trip(0, c).wait_recv()
+        self.trip(2, c).start()
 
     def finish(self):
-        for a in self.here + self.onward:
-            a.wait_recv()
-        for a in self.there + self.here + self.onward:
-            a.wait_send()
+        for c in range(self.chunks):
+            self.trip(1, c).wait_recv()
+            self.trip(2, c).wait_recv()
+            for kind in range(3):
+                self.trip(kind, c).wait_send()
+
+
+def fsdp_places():
+    f = lax.axis_index("fsdp")
+    return f // 2, lax.rem(f, 2), lax.axis_size("fsdp") // 2
+
+
+def fsdp_peers():
+    pair, side, pairs = fsdp_places()
+    peers = [{"fsdp": lax.rem(pair + d, pairs) * 2 + side} for d in range(1, pairs)]
+    return peers + [{"fsdp": pair * 2 + 1 - side}]
+
+
+class FsdpGather:
+    def __init__(self, wires, shard, full, local):
+        self.wires, self.shard, self.full, self.local = wires, shard, full, local
+        self.pair, self.side, self.pairs = fsdp_places()
+        self.base = wires.take(2 * self.pairs)
+
+    def view(self, d, side):
+        return self.full.at[lax.rem(self.pair + d, self.pairs) * 2 + side]
+
+    def out(self, d):
+        own = self.view(0, self.side)
+        if d == 0:
+            return self.wires.at(self.base, self.shard, own, {"fsdp": self.pair * 2 + 1 - self.side})
+        where = {"fsdp": lax.rem(self.pair + d, self.pairs) * 2 + self.side}
+        return self.wires.at(self.base + d, self.shard, own, where)
+
+    def onward(self, d):
+        view = self.view(self.pairs - d, self.side)
+        return self.wires.at(self.base + self.pairs + d, view, view, {"fsdp": self.pair * 2 + 1 - self.side})
+
+    def keep(self):
+        return pltpu.make_async_copy(self.shard, self.view(0, self.side), self.local)
+
+    def start(self):
+        self.out(0).start()
+        for d in range(1, self.pairs):
+            self.out(d).start()
+        self.keep().start()
+
+    def forward(self, d):
+        self.out(d).wait_recv()
+        self.onward(d).start()
+
+    def finish(self):
+        self.keep().wait()
+        self.out(0).wait_recv()
+        for d in range(1, self.pairs):
+            self.onward(d).wait_recv()
+        for d in range(self.pairs):
+            self.out(d).wait_send()
+        for d in range(1, self.pairs):
+            self.onward(d).wait_send()
+
+
+class FsdpScatter:
+    def __init__(self, wires, parts, bufs, local, result):
+        self.wires, self.parts, self.local, self.result = wires, parts, local, result
+        self.mine, self.got, self.passed, self.landed = bufs
+        self.pair, self.side, self.pairs = fsdp_places()
+        self.base = wires.take(2 * self.pairs)
+
+    def owner(self, d):
+        return lax.rem(self.pair + d, self.pairs) * 2
+
+    def load(self, d):
+        return pltpu.make_async_copy(self.parts.at[self.owner(d) + self.side], self.mine.at[d], self.local.at[d])
+
+    def swap(self, d):
+        src = self.parts.at[self.owner(d) + 1 - self.side]
+        return self.wires.at(self.base + d, src, self.got.at[d], {"fsdp": self.pair * 2 + 1 - self.side})
+
+    def onward(self, d):
+        where = {"fsdp": self.owner(d) + self.side}
+        return self.wires.at(self.base + self.pairs + d, self.passed.at[d], self.landed.at[d], where)
+
+    def order(self):
+        return list(range(1, self.pairs)) + [0]
+
+    def start(self):
+        for d in self.order():
+            self.swap(d).start()
+            self.load(d).start()
+
+    def step(self, d):
+        self.load(d).wait()
+        self.swap(d).wait_recv()
+        self.passed[d] = (self.mine[d].astype(F32) + self.got[d].astype(F32)).astype(BF16)
+        self.onward(d).start()
+
+    def finish(self):
+        self.load(0).wait()
+        self.swap(0).wait_recv()
+        total = self.mine[0].astype(F32) + self.got[0].astype(F32)
+        for d in range(1, self.pairs):
+            self.onward(d).wait_recv()
+            total = total + self.landed[d].astype(F32)
+        self.result[...] = total.astype(BF16)
+        for d in range(self.pairs):
+            self.swap(d).wait_send()
+        for d in range(1, self.pairs):
+            self.onward(d).wait_send()
+
+
+def fsdp_scatter_scratch(parts):
+    shape = (parts.shape[0] // 2,) + parts.shape[1:]
+    return [pltpu.VMEM(shape, BF16)] * 4 + [pltpu.SemaphoreType.DMA((shape[0],))]
+
+
+def blocks(a, count):
+    return a.reshape((count, a.shape[0] // count) + a.shape[1:])
 
 
 def vm_spec():
@@ -114,42 +234,61 @@
     return r * scaled - v * (r * r * r) * jnp.mean(v * scaled, axis=-1, keepdims=True)
 
 
-def tokens_gather_kernel(src, out, send, recv, local):
+def tokens_gather_kernel(src, first_q, out_q, out, first, out_w, send, recv, local):
     rows = src.shape[0]
     s, near, far, cross = seq_places()
-    meet([{"seq": near}, {"seq": far}])
+    meet([{"seq": near}, {"seq": far}] + fsdp_peers())
     half = rows // 2
-    ring = SeqGather(Wires(send, recv), lambda t, c: out.at[rows_at(t, rows, c * half, half), :], 2)
-    own = pltpu.make_async_copy(src, out.at[rows_at(s, rows), :], local)
-    own.start()
+    wires = Wires(send, recv)
+    ring = SeqGather(wires, lambda t, c: out.at[rows_at(t, rows, c * half, half), :], 2)
+    lead = FsdpGather(wires, first_q, first, local.at[1])
+    late = FsdpGather(wires, out_q, out_w, local.at[2])
+    own = pltpu.make_async_copy(src, out.at[rows_at(s, rows), :], local.at[0])
+    lead.start()
     for c in range(2):
         ring.send(c, src.at[pl.ds(c * half, half), :])
-    for c in range(2):
-        ring.forward(c)
+    late.start()
+    own.start()
+    for d in range(1, lead.pairs):
+        lead.forward(d)
+        if d == lead.pairs // 2:
+            ring.forward(0)
+    for d in range(1, late.pairs):
+        late.forward(d)
+    ring.forward(1)
     own.wait()
+    lead.finish()
+    late.finish()
     ring.finish()
 
 
-def tokens_gather(tokens, nseq):
+def tokens_gather(tokens, first_q, out_q, nseq, nfsdp):
     rows, width = tokens.shape
     return pl.pallas_call(
         tokens_gather_kernel,
-        out_shape=jax.ShapeDtypeStruct((nseq * rows, width), BF16),
-        in_specs=[any_spec()],
-        out_specs=any_spec(),
-        scratch_shapes=wires_scratch(6) + [pltpu.SemaphoreType.DMA],
+        out_shape=(
+            jax.ShapeDtypeStruct((nseq * rows, width), BF16),
+            jax.ShapeDtypeStruct((nfsdp,) + first_q.shape, BF16),
+            jax.ShapeDtypeStruct((nfsdp,) + out_q.shape, BF16),
+        ),
+        in_specs=[any_spec()] * 3,
+        out_specs=(any_spec(),) * 3,
+        scratch_shapes=wires_scratch(6 + 2 * nfsdp) + [pltpu.SemaphoreType.DMA((3,))],
         compiler_params=call_params(0, 4),
         name="tokens_gather",
-    )(tokens)
-
-
-def mix_kernel(o, out_w, tok, gain, obuf, resid, n2, send, recv, own, local):
+    )(tokens, first_q, out_q)
+
+
+def mix_kernel(o, out_w, tok, gain, up_q, down_q, obuf, resid, n2, up_w, down_w, send, recv, own, local):
     rows, width = tok.shape
     piece = o.shape[1]
     nseq = obuf.shape[0]
     s, near, far, cross = seq_places()
-    meet([{"seq": near}, {"seq": far}, {"seq": cross}])
+    meet([{"seq": near}, {"seq": far}, {"seq": cross}] + fsdp_peers())
     wires = Wires(send, recv)
+    weights = [FsdpGather(wires, up_q, up_w, local.at[1]), FsdpGather(wires, down_q, down_w, local.at[2])]
+    for a in weights:
+        a.start()
     trips = [wires.go(o.at[rows_at(t, rows), :], obuf.at[s], {"seq": t}) for t in (far, cross, near)]
     obuf[s] = o[rows_at(s, rows), :]
     half = rows // 2
@@ -167,17 +306,25 @@
         h = resid[part, :]
         own[part, :] = (h * inverse_rms(h) * gain[...]).astype(BF16)
         ring.send(c, own.at[pl.ds(c * half, half), :])
-    mineblock = pltpu.make_async_copy(own, n2.at[rows_at(s, rows), :], local)
+    mineblock = pltpu.make_async_copy(own, n2.at[rows_at(s, rows), :], local.at[0])
     mineblock.start()
-    for c in range(2):
-        ring.forward(c)
+    pairs = weights[0].pairs
+    weights[0].forward(1)
+    ring.forward(0)
+    for d in range(2, pairs):
+        weights[0].forward(d)
+    ring.forward(1)
+    for d in range(1, pairs):
+        weights[1].forward(d)
+    for a in weights:
+        a.finish()
     mineblock.wait()
     ring.finish()
     for a in trips:
         a.wait_send()
 
 
-def mix(o, out_w, tok, gain):
+def mix(o, out_w, tok, gain, up_q, down_q, nfsdp):
     nseq = out_w.shape[0]
     rows, width = tok.shape
     return pl.pallas_call(
@@ -186,43 +333,51 @@
             jax.ShapeDtypeStruct((nseq, rows, o.shape[1]), BF16),
             jax.ShapeDtypeStruct((rows, width), F32),
             jax.ShapeDtypeStruct((nseq * rows, width), BF16),
+            jax.ShapeDtypeStruct((nfsdp,) + up_q.shape, BF16),
+            jax.ShapeDtypeStruct((nfsdp,) + down_q.shape, BF16),
         ),
-        in_specs=[vm_spec()] * 4,
-        out_specs=(vm_spec(), vm_spec(), any_spec()),
-        scratch_shapes=wires_scratch(9) + [pltpu.VMEM((rows, width), BF16), pltpu.SemaphoreType.DMA],
+        in_specs=[vm_spec()] * 4 + [any_spec()] * 2,
+        out_specs=(vm_spec(), vm_spec()) + (any_spec(),) * 3,
+        scratch_shapes=wires_scratch(9 + 2 * nfsdp)
+        + [pltpu.VMEM((rows, width), BF16), pltpu.SemaphoreType.DMA((3,))],
         compiler_params=call_params(2, 32),
         name="mix",
-    )(o, out_w, tok, gain)
+    )(o, out_w, tok, gain, up_q, down_q)
 
 
 class SeqScatter:
-    def __init__(self, wires, to_near, from_near, to_far, from_far, to_own, from_own):
+    def __init__(self, wires, chunks, *bufs):
         self.s, self.near, self.far, self.cross = seq_places()
-        self.wires = wires
-        self.bufs = (to_near, from_near, to_far, from_far, to_own, from_own)
-        self.first, self.second, self.third = [], [], []
+        self.wires, self.chunks, self.bufs = wires, chunks, bufs
+        self.base = wires.take(3 * chunks)
+
+    def trip(self, kind, c):
+        where = {"seq": self.far if kind == 1 else self.near}
+        src, dst = self.bufs[2 * kind].at[c], self.bufs[2 * kind + 1].at[c]
+        return self.wires.at(self.base + 3 * c + kind, src, dst, where)
 
     def cross_chunk(self, c, value):
         self.bufs[0][c] = value.astype(BF16)
-        self.first.append(self.wires.go(self.bufs[0].at[c], self.bufs[1].at[c], {"seq": self.near}))
+        self.trip(0, c).start()
 
     def far_chunk(self, c, value):
-        self.first[c].wait_recv()
+        self.trip(0, c).wait_recv()
         self.bufs[2][c] = (value + self.bufs[1][c].astype(F32)).astype(BF16)
-        self.second.append(self.wires.go(self.bufs[2].at[c], self.bufs[3].at[c], {"seq": self.far}))
+        self.trip(1, c).start()
 
     def near_chunk(self, c, value):
         self.bufs[4][c] = value.astype(BF16)
-        self.third.append(self.wires.go(self.bufs[4].at[c], self.bufs[5].at[c], {"seq": self.near}))
+        self.trip(2, c).start()
 
     def own_chunk(self, c, value):
-        self.third[c].wait_recv()
-        self.second[c].wait_recv()
+        self.trip(2, c).wait_recv()
+        self.trip(1, c).wait_recv()
         return value + self.bufs[5][c].astype(F32) + self.bufs[3][c].astype(F32)
 
     def finish(self):
-        for a in self.first + self.second + self.third:
-            a.wait_send()
+        for c in range(self.chunks):
+            for kind in range(3):
+                self.trip(kind, c).wait_send()
 
 
 def scatter_scratch(chunks, rows, width):
@@ -230,16 +385,18 @@
 
 
 def unmix_kernel(
-    chunks, dg, du, gate_w, up_w, resid, gain, cot, out_w, obuf,
-    rgrad, dmix, wgrad, ggrad,
-    send, recv, b0, b1, b2, b3, b4, b5, attn, dob,
+    chunks, dg, du, gate_w, up_w, resid, gain, cot, out_w, obuf, parts,
+    rgrad, dmix, wgrad, ggrad, shard,
+    send, recv, b0, b1, b2, b3, b4, b5, attn, dob, p0, p1, p2, p3, local,
 ):
     rows, width = resid.shape
     nseq, _, piece = obuf.shape
     s, near, far, cross = seq_places()
-    meet([{"seq": near}, {"seq": far}, {"seq": cross}])
+    meet([{"seq": near}, {"seq": far}, {"seq": cross}] + fsdp_peers())
     wires = Wires(send, recv)
-    sums = SeqScatter(wires, b0, b1, b2, b3, b4, b5)
+    grads = FsdpScatter(wires, parts, (p0, p1, p2, p3), local, shard)
+    grads.start()
+    sums = SeqScatter(wires, chunks, b0, b1, b2, b3, b4, b5)
     size = rows // chunks
 
     def part(t, c):
@@ -256,6 +413,7 @@
         rgrad[c * size : (c + 1) * size, :] = part(s, c)
     total = jnp.zeros((1, width), F32)
     trips = []
+    grads.step(1)
     for c in range(chunks):
         at = slice(c * size, (c + 1) * size)
         dn = sums.own_chunk(c, rgrad[at, :])
@@ -272,6 +430,9 @@
             for u in range(nseq):
                 acc = acc + nt(low[:, u * cols : (u + 1) * cols], out_w[u, t * piece : (t + 1) * piece, :])
             dob[t, at, :] = acc.astype(BF16)
+        if c == 0:
+            for d in range(2, grads.pairs):
+                grads.step(d)
     ggrad[...] = jnp.broadcast_to(total, ggrad.shape)
     for t in (far, cross, near):
         trips.append(wires.go(dob.at[t], dmix.at[rows_at(s, rows), :], {"seq": t}))
@@ -285,9 +446,10 @@
     for a in trips:
         a.wait()
     sums.finish()
-
-
-def unmix(dg, du, gate_w, up_w, resid, gain, cot, out_w, obuf, chunks=2):
+    grads.finish()
+
+
+def unmix(dg, du, gate_w, up_w, resid, gain, cot, out_w, obuf, parts, chunks=2):
     rows, width = resid.shape
     nseq, _, piece = obuf.shape
     return pl.pallas_call(
@@ -297,23 +459,31 @@
             jax.ShapeDtypeStruct((nseq * rows, piece), BF16),
             jax.ShapeDtypeStruct(out_w.shape, BF16),
             jax.ShapeDtypeStruct((8, width), F32),
+            jax.ShapeDtypeStruct(parts.shape[1:], BF16),
         ),
-        in_specs=[vm_spec()] * 9,
-        out_specs=(vm_spec(),) * 4,
-        scratch_shapes=wires_scratch(3 * chunks + 3)
+        in_specs=[vm_spec()] * 9 + [any_spec()],
+        out_specs=(vm_spec(),) * 5,
+        scratch_shapes=wires_scratch(3 * chunks + 3 + parts.shape[0])
         + scatter_scratch(chunks, rows // chunks, width)
-        + [pltpu.VMEM((rows, width), BF16), pltpu.VMEM((nseq, rows, piece), BF16)],
+        + [pltpu.VMEM((rows, width), BF16), pltpu.VMEM((nseq, rows, piece), BF16)]
+        + fsdp_scatter_scratch(parts),
         compiler_params=call_params(4),
         name="unmix",
-    )(dg, du, gate_w, up_w, resid, gain, cot, out_w, obuf)
-
-
-def input_kernel(chunks, dqkv, qkv_w, tok, gain, rgrad, in_grad, ggrad, send, recv, b0, b1, b2, b3, b4, b5, hold):
+    )(dg, du, gate_w, up_w, resid, gain, cot, out_w, obuf, parts)
+
+
+def input_kernel(
+    chunks, dqkv, qkv_w, tok, gain, rgrad, parts, done0, done1,
+    in_grad, ggrad, shard, full0, full1,
+    send, recv, b0, b1, b2, b3, b4, b5, hold, p0, p1, p2, p3, plocal, local,
+):
     rows, width = tok.shape
     s, near, far, cross = seq_places()
-    meet([{"seq": near}, {"seq": far}])
+    meet([{"seq": near}, {"seq": far}] + fsdp_peers())
     wires = Wires(send, recv)
-    sums = SeqScatter(wires, b0, b1, b2, b3, b4, b5)
+    grads = FsdpScatter(wires, parts, (p0, p1, p2, p3), plocal, shard)
+    grads.start()
+    sums = SeqScatter(wires, chunks, b0, b1, b2, b3, b4, b5)
     size = rows // chunks
     used = dqkv.shape[1]
 
@@ -329,6 +499,13 @@
     for c in range(chunks):
         hold[c * size : (c + 1) * size, :] = part(s, c)
     total = jnp.zeros((1, width), F32)
+    rings = []
+    for n, (done, full) in enumerate(((done0, full0), (done1, full1))):
+        ring = SeqGather(wires, lambda t, c, full=full: full.at[t], 1)
+        ring.send(0, done)
+        pltpu.make_async_copy(done, full.at[s], local.at[n]).start()
+        rings.append(ring)
+    grads.step(1)
     for c in range(chunks):
         at = slice(c * size, (c + 1) * size)
         dn = sums.own_chunk(c, hold[at, :])
@@ -336,23 +513,138 @@
         r = inverse_rms(x)
         total = total + jnp.sum(dn * x * r, axis=0, keepdims=True)
         in_grad[at, :] = (rgrad[at, :] + norm_back(dn, x, r, gain[...])).astype(BF16)
+        if c == 0:
+            for d in range(2, grads.pairs):
+                grads.step(d)
     ggrad[...] = jnp.broadcast_to(total, ggrad.shape)
+    for ring in rings:
+        ring.forward(0)
     sums.finish()
-
-
-def input_grads(dqkv, qkv_w, tok, gain, rgrad, chunks=2):
+    grads.finish()
+    for n, (done, full) in enumerate(((done0, full0), (done1, full1))):
+        rings[n].finish()
+        pltpu.make_async_copy(done, full.at[s], local.at[n]).wait()
+
+
+def input_grads(dqkv, qkv_w, tok, gain, rgrad, parts, done0, done1, nseq, chunks=2):
     rows, width = tok.shape
     return pl.pallas_call(
         functools.partial(input_kernel, chunks),
-        out_shape=(jax.ShapeDtypeStruct((rows, width), BF16), jax.ShapeDtypeStruct((8, width), F32)),
-        in_specs=[vm_spec()] * 5,
-        out_specs=(vm_spec(),) * 2,
-        scratch_shapes=wires_scratch(3 * chunks)
+        out_shape=(
+            jax.ShapeDtypeStruct((rows, width), BF16),
+            jax.ShapeDtypeStruct((8, width), F32),
+            jax.ShapeDtypeStruct(parts.shape[1:], BF16),
+            jax.ShapeDtypeStruct((nseq,) + done0.shape, BF16),
+            jax.ShapeDtypeStruct((nseq,) + done1.shape, BF16),
+        ),
+        in_specs=[vm_spec()] * 5 + [any_spec()] * 3,
+        out_specs=(vm_spec(),) * 3 + (any_spec(),) * 2,
+        scratch_shapes=wires_scratch(3 * chunks + parts.shape[0] + 6)
         + scatter_scratch(chunks, rows // chunks, width)
-        + [pltpu.VMEM((rows, width), F32)],
-        compiler_params=call_params(6, 40),
+        + [pltpu.VMEM((rows, width), F32)]
+        + fsdp_scatter_scratch(parts)
+        + [pltpu.SemaphoreType.DMA((2,))],
+        compiler_params=call_params(6, 48),
         name="input_grads",
-    )(dqkv, qkv_w, tok, gain, rgrad)
+    )(dqkv, qkv_w, tok, gain, rgrad, parts, done0, done1)
+
+
+def last_kernel(
+    qkv_p, out_p, done, gain_a, gain_b, table,
+    qkv_f, out_f, full, small,
+    send, recv, local, qkv_s, out_s, held, stage, one, two, three, *bufs,
+):
+    s, near, far, cross = seq_places()
+    pair, side, pairs = fsdp_places()
+    meet([{"seq": near}, {"seq": far}, {"seq": cross}] + fsdp_peers())
+    wires = Wires(send, recv)
+    scatters = [
+        FsdpScatter(wires, qkv_p, bufs[:4], bufs[4], qkv_s),
+        FsdpScatter(wires, out_p, bufs[5:9], bufs[9], out_s),
+    ]
+    for a in scatters:
+        a.start()
+    ring = SeqGather(wires, lambda t, c: full.at[t], 1)
+    ring.send(0, done)
+    keep = pltpu.make_async_copy(done, full.at[s], local.at[0])
+    keep.start()
+    held[...] = jnp.zeros(held.shape, F32)
+    lanes = held.shape[1]
+    lines = gain_a.shape[1] // lanes
+    for n in range(lines):
+        held[n : n + 1, :] = gain_a[:1, n * lanes : (n + 1) * lanes]
+        held[lines + n : lines + n + 1, :] = gain_b[:1, n * lanes : (n + 1) * lanes]
+    heads = table.shape[0]
+    held[pl.ds(2 * lines + s * 8, heads), :] = table[...]
+    trips = [wires.go(held, one.at[n], {"seq": t}) for n, t in enumerate((near, far, cross))]
+    scatters[0].step(1)
+    for a in trips:
+        a.wait_recv()
+    stage[0] = held[...] + one[0] + one[1] + one[2]
+    trips.append(wires.go(stage.at[0], two, {"fsdp": pair * 2 + 1 - side}))
+    for d in range(2, pairs):
+        scatters[0].step(d)
+    trips[-1].wait_recv()
+    stage[1] = stage[0] + two[...]
+    zs = [
+        wires.go(stage.at[1], three.at[d - 1], {"fsdp": lax.rem(pair + d, pairs) * 2 + side})
+        for d in range(1, pairs)
+    ]
+    for d in range(1, pairs):
+        scatters[1].step(d)
+    ring.forward(0)
+    scatters[0].finish()
+    more = [SeqGather(wires, lambda t, c: qkv_f.at[t], 1), SeqGather(wires, lambda t, c: out_f.at[t], 1)]
+    copies = [pltpu.make_async_copy(qkv_s, qkv_f.at[s], local.at[1]), pltpu.make_async_copy(out_s, out_f.at[s], local.at[2])]
+    more[0].send(0, qkv_s)
+    scatters[1].finish()
+    more[1].send(0, out_s)
+    total = stage[1]
+    for d, a in enumerate(zs):
+        a.wait_recv()
+        total = total + three[d]
+    small[...] = total
+    for n in range(2):
+        copies[n].start()
+        more[n].forward(0)
+    for n in range(2):
+        more[n].finish()
+        copies[n].wait()
+    ring.finish()
+    keep.wait()
+    for a in trips + zs:
+        a.wait_send()
+
+
+def last_sums(qkv_p, out_p, done, gain_a, gain_b, table, nseq):
+    nfsdp = qkv_p.shape[0]
+    lines = -(-(2 * gain_a.shape[1] // 128 + 8 * nseq) // 8) * 8
+    return pl.pallas_call(
+        last_kernel,
+        out_shape=(
+            jax.ShapeDtypeStruct((nseq,) + qkv_p.shape[1:], BF16),
+            jax.ShapeDtypeStruct((nseq,) + out_p.shape[1:], BF16),
+            jax.ShapeDtypeStruct((nseq,) + done.shape, BF16),
+            jax.ShapeDtypeStruct((lines, 128), F32),
+        ),
+        in_specs=[any_spec()] * 3 + [vm_spec()] * 3,
+        out_specs=(any_spec(),) * 3 + (vm_spec(),),
+        scratch_shapes=wires_scratch(2 * nfsdp + 9 + 4 + nfsdp // 2)
+        + [
+            pltpu.SemaphoreType.DMA((3,)),
+            pltpu.VMEM(qkv_p.shape[1:], BF16),
+            pltpu.VMEM(out_p.shape[1:], BF16),
+            pltpu.VMEM((lines, 128), F32),
+            pltpu.VMEM((2, lines, 128), F32),
+            pltpu.VMEM((3, lines, 128), F32),
+            pltpu.VMEM((lines, 128), F32),
+            pltpu.VMEM((nfsdp // 2 - 1, lines, 128), F32),
+        ]
+        + fsdp_scatter_scratch(qkv_p)
+        + fsdp_scatter_scratch(out_p),
+        compiler_params=call_params(7, 32),
+        name="last_sums",
+    )(qkv_p, out_p, done, gain_a, gain_b, table)
 
 
 def build_strips(heads, starts, table, ids, strip, far):
@@ -393,13 +685,17 @@
 
 
 def attn_fwd_kernel(
-    heads, starts, table, ids, q, k, v, out_q, cot, o, lse, out_w, cots, strip, far, kh, vt, ot, s, send, recv, local
+    heads, starts, table, ids, q, k, v, out_q, cot, gate_q,
+    o, lse, out_w, cots, gate_w,
+    strip, far, kh, vt, ot, s, send, recv, local,
 ):
     rows = cot.shape[0]
     mine, near, other, cross = seq_places()
-    meet([{"seq": near}, {"seq": other}])
+    meet([{"seq": near}, {"seq": other}] + fsdp_peers())
     wires = Wires(send, recv)
     half = rows // 2
+    weight = FsdpGather(wires, gate_q, gate_w, local.at[2])
+    weight.start()
     wring = SeqGather(wires, lambda t, c: out_w.at[t], 1)
     cring = SeqGather(wires, lambda t, c: cots.at[rows_at(t, rows, c * half, half), :], 2)
     wring.send(0, out_q)
@@ -439,6 +735,11 @@
         h, blk = i // nblk, i % nblk
         q0 = pl.multiple_of(blk * CL, CL)
         block(h, q0, q0, [(j * KC, "strip", j * KC) for j in range(PROMPT // KC)], None)
+
+        @pl.when(i == 6)
+        def _():
+            weight.forward(1)
+
         return carry
 
     lax.fori_loop(0, heads * nblk, prompt_body, 0)
@@ -454,15 +755,18 @@
     wring.forward(0)
     lax.fori_loop(0, heads * 2, cont_body, 0)
     o[...] = ot[...].T.astype(BF16)
-    for c in range(2):
-        cring.forward(c)
+    cring.forward(0)
+    for d in range(2, weight.pairs):
+        weight.forward(d)
+    cring.forward(1)
     for a in own:
         a.wait()
+    weight.finish()
     wring.finish()
     cring.finish()
 
 
-def attn_fwd(starts, table, ids, q, k, v, out_q, cot, nseq):
+def attn_fwd(starts, table, ids, q, k, v, out_q, cot, gate_q, nseq, nfsdp):
     rows, width = q.shape
     heads = width // HEAD_DIM
     smem = pl.BlockSpec(memory_space=pltpu.SMEM)
@@ -474,9 +778,10 @@
             jax.ShapeDtypeStruct((8, rows), F32),
             jax.ShapeDtypeStruct((nseq,) + out_q.shape, BF16),
             jax.ShapeDtypeStruct((rows, cot.shape[1]), BF16),
+            jax.ShapeDtypeStruct((nfsdp,) + gate_q.shape, BF16),
         ),
-        in_specs=[smem, smem, vm, vm, vm, vm, any_spec(), any_spec()],
-        out_specs=(vm, vm, any_spec(), any_spec()),
+        in_specs=[smem, smem, vm, vm, vm, vm] + [any_spec()] * 3,
+        out_specs=(vm, vm) + (any_spec(),) * 3,
         scratch_shapes=[
             pltpu.VMEM((heads, 128, STRIP), F32),
             pltpu.VMEM((heads, 2, 128, FARW), F32),
@@ -485,23 +790,25 @@
             pltpu.VMEM((width, rows), F32),
             pltpu.VMEM((PROMPT + CL, CL), F32),
         ]
-        + wires_scratch(9)
-        + [pltpu.SemaphoreType.DMA((2,))],
+        + wires_scratch(9 + nfsdp)
+        + [pltpu.SemaphoreType.DMA((3,))],
         compiler_params=call_params(1, 40),
         name="attend_forward",
-    )(starts, table, ids, q, k, v, out_q, cot)
+    )(starts, table, ids, q, k, v, out_q, cot, gate_q)
 
 
 def attn_bwd_kernel(
-    heads, starts, table, ids, q, k, v, o, do, lse, resid, ypart, wpart,
-    dq, dk, dv, tgrad, y, wsum,
+    heads, starts, table, ids, q, k, v, o, do, lse, resid, ypart, wpart, parts,
+    dq, dk, dv, tgrad, y, wsum, shard,
     strip, far, kh, vh, qh, doh, kt, delta, dqt, gstrip, gfar,
-    send, recv, local, ybuf, wbuf,
+    send, recv, local, ybuf, wbuf, p0, p1, p2, p3, plocal,
 ):
     rows = resid.shape[0]
     mine, near, other, cross = seq_places()
-    meet([{"seq": near}, {"seq": other}])
+    meet([{"seq": near}, {"seq": other}] + fsdp_peers())
     wires = Wires(send, recv)
+    grads = FsdpScatter(wires, parts, (p0, p1, p2, p3), plocal, shard)
+    grads.start()
 
     def block_of(part, t):
         return part.at[rows_at(t, rows), :] if part is ypart else part.at[t]
@@ -568,9 +875,17 @@
         h, blk = i // nblk, i % nblk
         q0 = pl.multiple_of(blk * CL, CL)
         block(h, q0, q0, [(j * KC, "strip", j * KC) for j in range(PROMPT // KC)], None)
+
+        @pl.when(i == 3)
+        def _():
+            grads.step(1)
+
         return carry
 
     lax.fori_loop(0, heads * nblk, prompt_body, 0)
+
+    for d in range(2, grads.pairs - 1):
+        grads.step(d)
 
     def cont_body(i, carry):
         h, c = i // 2, i % 2
@@ -581,6 +896,8 @@
         return carry
 
     lax.fori_loop(0, heads * 2, cont_body, 0)
+    if grads.pairs > 2:
+        grads.step(grads.pairs - 1)
     dq[...] = dqt[...].T
 
     length = ids.shape[1]
@@ -615,9 +932,10 @@
     y[...] = (resid[...] + sums[1]).astype(BF16)
     for a in hops + turns + far_hops:
         a.wait_send()
-
-
-def attn_bwd(starts, table, ids, q, k, v, o, do, lse, resid, ypart, wpart):
+    grads.finish()
+
+
+def attn_bwd(starts, table, ids, q, k, v, o, do, lse, resid, ypart, wpart, parts):
     rows, width = q.shape
     heads = width // HEAD_DIM
     smem = pl.BlockSpec(memory_space=pltpu.SMEM)
@@ -632,9 +950,10 @@
             jax.ShapeDtypeStruct((heads, table.shape[0], 128), F32),
             jax.ShapeDtypeStruct(resid.shape, BF16),
             jax.ShapeDtypeStruct(wpart.shape[1:], BF16),
+            jax.ShapeDtypeStruct(parts.shape[1:], BF16),
         ),
-        in_specs=[smem, smem] + [vm] * 8 + [any_spec()] * 2,
-        out_specs=(vm,) * 6,
+        in_specs=[smem, smem] + [vm] * 8 + [any_spec()] * 3,
+        out_specs=(vm,) * 7,
         scratch_shapes=[
             pltpu.VMEM((heads, 128, STRIP), F32),
             pltpu.VMEM((heads, 2, 128, FARW), F32),
@@ -647,15 +966,16 @@
             pltpu.VMEM((heads, 128, STRIP), F32),
             pltpu.VMEM((heads, 2, 128, FARW), F32),
         ]
-        + wires_scratch(6)
+        + wires_scratch(6 + parts.shape[0])
         + [
             pltpu.SemaphoreType.DMA((4,)),
             pltpu.VMEM((5,) + resid.shape, BF16),
             pltpu.VMEM((5,) + wpart.shape[1:], BF16),
-        ],
+        ]
+        + fsdp_scatter_scratch(parts),
         compiler_params=call_params(5),
         name="attend_backward",
-    )(starts, table, ids, q, k, v, o, do, lse, resid, ypart, wpart)
+    )(starts, table, ids, q, k, v, o, do, lse, resid, ypart, wpart, parts)
 
 
 def reversed_ids(bucket_ids):
@@ -731,29 +1051,19 @@
     heads = piece // HEAD_DIM
     hidden_all = w_gate.shape[1]
 
-    def gather_f(a):
-        return lax.all_gather(a, "fsdp", axis=0, tiled=True)
-
-    def gather_s(a):
-        return lax.all_gather(a, "seq", axis=0, tiled=True)
-
-    def scatter_f(a):
-        return lax.psum_scatter(a.astype(BF16), "fsdp", scatter_dimension=0, tiled=True)
-
     local = [lax.dynamic_slice_in_dim(w, mine * piece, piece, 1) for w in (w_query, w_key, w_value)]
     gains = jnp.pad(jnp.stack([attn_gain, mix_gain], axis=1), ((0, 0), (0, 62)))
-    first = gather_f(jnp.concatenate(local + [gains], axis=1))
+    out_cols = width // nseq
+    out_local = lax.dynamic_slice_in_dim(w_out, mine * out_cols, out_cols, 1)
+    group, first, out_q = tokens_gather(
+        tokens[0], jnp.concatenate(local + [gains], axis=1), out_local, nseq, nfsdp
+    )
+    first = first.reshape(width, -1)
+    out_q = out_q.reshape(inner, out_cols)
     query_w, key_w, value_w = (first[:, i * piece : (i + 1) * piece] for i in range(3))
     gain_one = first[:, 3 * piece].astype(F32)
     gain_two = first[:, 3 * piece + 1].astype(F32)
-    out_cols = width // nseq
-    out_local = lax.dynamic_slice_in_dim(w_out, mine * out_cols, out_cols, 1)
-    out_q = gather_f(out_local)
-    gate_w = gather_f(pack_columns(w_gate, nseq, nfsdp, mine))
-    up_w = gather_f(pack_columns(w_up, nseq, nfsdp, mine))
-    down_w = gather_f(pack_rows(w_down, nseq, mine))
-
-    group = tokens_gather(tokens[0], nseq).astype(F32)
+    group = group.astype(F32)
     normed = (group * inverse_rms(group) * gain_one).astype(BF16)
     query = dot32(normed, query_w).astype(BF16)
     keys = dot32(normed, key_w).astype(BF16)
@@ -761,45 +1071,91 @@
     table = lax.dynamic_slice_in_dim(rel_table, mine * heads, heads, 1)
     ids = reversed_ids(bucket_ids)
     starts = cont_start[0]
-    mixed, lse, out_w, cot = attn_fwd(starts, table, ids, query, keys, values, out_q, out_grad[0], nseq)
-    mixed_rows, resid, normed_two = mix(mixed, out_w, tokens[0], gain_two[None])
+    gate_q = pack_columns(w_gate, nseq, nfsdp, mine)
+    up_q = pack_columns(w_up, nseq, nfsdp, mine)
+    down_q = pack_rows(w_down, nseq, mine)
+    mixed, lse, out_w, cot, gate_w = attn_fwd(
+        starts, table, ids, query, keys, values, out_q, out_grad[0], gate_q, nseq, nfsdp
+    )
+    mixed_rows, resid, normed_two, up_w, down_w = mix(
+        mixed, out_w, tokens[0], gain_two[None], up_q, down_q, nfsdp
+    )
+    gate_w = gate_w.reshape(width, -1)
+    up_w = up_w.reshape(width, -1)
+    down_w = down_w.reshape(-1, width)
     gate = dot32(normed_two, gate_w)
     upward = dot32(normed_two, up_w)
     active, slope = gelu_both(gate)
     hidden = (active * upward).astype(BF16)
     result = dot32(hidden, down_w).astype(BF16)
-    down_grad = scatter_f(dot_tn(hidden, cot))
+    down_grad = dot_tn(hidden, cot).astype(BF16)
     hidden_grad = nt(cot, down_w)
     gate_grad = (hidden_grad * upward * slope).astype(BF16)
     up_grad = (hidden_grad * active).astype(BF16)
-    resid_grad, mixed_grad, out_w_grad, gain_two_grad = unmix(
-        gate_grad, up_grad, gate_w, up_w, resid, gain_two[None], out_grad[0], out_w, mixed_rows
+    resid_grad, mixed_grad, out_w_grad, gain_two_grad, down_grad = unmix(
+        gate_grad,
+        up_grad,
+        gate_w,
+        up_w,
+        resid,
+        gain_two[None],
+        out_grad[0],
+        out_w,
+        mixed_rows,
+        blocks(down_grad, nfsdp),
     )
-    gate_w_grad = scatter_f(dot_tn(normed_two, gate_grad))
-    up_w_grad = scatter_f(dot_tn(normed_two, up_grad))
-    dq, dk, dv, tgrad, block_out, out_w_grad = attn_bwd(
-        starts, table, ids, query, keys, values, mixed, mixed_grad, lse, resid, result, out_w_grad
+    gate_w_grad = dot_tn(normed_two, gate_grad).astype(BF16)
+    up_w_grad = dot_tn(normed_two, up_grad).astype(BF16)
+    dq, dk, dv, tgrad, block_out, out_w_grad, gate_w_grad = attn_bwd(
+        starts,
+        table,
+        ids,
+        query,
+        keys,
+        values,
+        mixed,
+        mixed_grad,
+        lse,
+        resid,
+        result,
+        out_w_grad,
+        blocks(gate_w_grad, nfsdp),
     )
     dqkv = jnp.concatenate([dq, dk, dv], axis=1).astype(BF16)
-    qkv_grad = scatter_f(dot_tn(normed, dqkv))
-    in_grad, gain_one_grad = input_grads(dqkv, first, tokens[0], gain_one[None], resid_grad)
-
-    out_w_grad = lax.all_gather(scatter_f(out_w_grad), "seq", axis=1, tiled=True)
-    qkv_grad = lax.all_gather(qkv_grad, "seq", axis=0).reshape(nseq, -1, 3, piece)
-    qkv_grad = qkv_grad.transpose(1, 2, 0, 3).reshape(-1, 3, inner).astype(F32)
-    gate_w_grad = unpack_columns(lax.all_gather(gate_w_grad, "seq", axis=0), hidden_all, nfsdp)
-    up_w_grad = unpack_columns(lax.all_gather(up_w_grad, "seq", axis=0), hidden_all, nfsdp)
-    down_grad = gather_s(down_grad)[: w_down.shape[0]]
-
+    qkv_grad = dot_tn(normed, dqkv).astype(BF16)
+    in_grad, gain_one_grad, up_w_grad, down_grad, gate_w_grad = input_grads(
+        dqkv,
+        first,
+        tokens[0],
+        gain_one[None],
+        resid_grad,
+        blocks(up_w_grad, nfsdp),
+        down_grad,
+        gate_w_grad,
+        nseq,
+    )
     buckets = rel_table.shape[0]
-    table_full = jnp.zeros((nseq, heads, buckets), F32)
-    table_full = lax.dynamic_update_slice(table_full, tgrad[None, :, :, 0], (mine, jnp.int32(0), jnp.int32(0)))
-    table_grad, gain_one_all, gain_two_all = lax.psum(
-        (table_full, gain_one_grad[0], gain_two_grad[0]), ("seq", "fsdp")
+    tpad = jnp.pad(tgrad[:, :, 0], ((0, 0), (0, 128 - buckets)))
+    qkv_grad, out_w_grad, up_w_grad, small = last_sums(
+        blocks(qkv_grad, nfsdp),
+        blocks(out_w_grad, nfsdp),
+        up_w_grad,
+        gain_one_grad,
+        gain_two_grad,
+        tpad,
+        nseq,
     )
+    qkv_grad = qkv_grad.reshape(nseq, -1, 3, piece).transpose(1, 2, 0, 3).reshape(-1, 3, inner).astype(F32)
+    out_w_grad = out_w_grad.transpose(1, 0, 2).reshape(-1, width)
+    gate_w_grad = unpack_columns(gate_w_grad, hidden_all, nfsdp)
+    up_w_grad = unpack_columns(up_w_grad, hidden_all, nfsdp)
+    down_grad = down_grad.reshape(-1, width)[: w_down.shape[0]]
+    lines = width // 128
     share = width // nfsdp
-    gain_one_share = lax.dynamic_slice_in_dim(gain_one_all, where * share, share)
-    gain_two_share = lax.dynamic_slice_in_dim(gain_two_all, where * share, share)
+    gain_one_share = lax.dynamic_slice_in_dim(small[:lines].reshape(-1), where * share, share)
+    gain_two_share = lax.dynamic_slice_in_dim(small[lines : 2 * lines].reshape(-1), where * share, share)
+    tables = small[2 * lines : 2 * lines + 8 * nseq].reshape(nseq, 8, 128)[:, :heads, :buckets]
+    table_grad = tables.reshape(nseq * heads, buckets).T
     return (
         block_out[None],
         in_grad[None],
@@ -812,7 +1168,7 @@
         gate_w_grad.astype(F32),
         up_w_grad.astype(F32),
         down_grad.astype(F32),
-        table_grad.reshape(nseq * heads, buckets).T,
+        table_grad,
     )
 
 

time: 721 us -> 566 us (0.79)
  waiting for transfers between devices: 176 us -> 0 us
  Pallas kernels: 258 us -> 407 us
  blocking collectives: 92.1 us -> 0 us
  matrix products: 88.3 us -> 73.6 us
  between operations: 15.1 us -> 1.69 us
    reduce_scatter x5 -> x0, waiting for transfers between devices: 125 us -> none  [scatter_f(): lax.psum_scatter(a.astype(BF16), 'fsdp', scatter_dimension=0, tiled=True)]
    pallas_call x1 -> x2, Pallas kernels: 31.6 us -> 84.7 us  [the longest x1 45.6 us: last_sums(): pl.pallas_call(last_kernel, out_shape=(jax.ShapeDtypeStruct((nseq,) + qkv...]
    all_gather x3 -> x0, blocking collectives: 52.4 us -> none  [the longest x1 35.4 us: gather_f(): return lax.all_gather(a, 'fsdp', axis=0, tiled=True)]
    all_gather x7 -> x0, waiting for transfers between devices: 50.5 us -> none  [the longest x4 26.8 us: gather_f(): return lax.all_gather(a, 'fsdp', axis=0, tiled=True)]
    pallas_call x1, Pallas kernels: 42 us -> 89.8 us  [mix(): pl.pallas_call(mix_kernel, out_shape=(jax.ShapeDtypeStruct((nseq, rows, o...]
    psum x1 -> x0, blocking collectives: 39.7 us -> none  [body(): lax.psum((table_full, gain_one_grad[0], gain_two_grad[0]), ('seq', 'fsdp'))]
    pallas_call x1, Pallas kernels: 33 us -> 54.7 us  [input_grads(): pl.pallas_call(functools.partial(input_kernel, chunks), out_shape=(jax.Sh...]
    pallas_call x1, Pallas kernels: 53.3 us -> 62.9 us  [attn_bwd(): pl.pallas_call(functools.partial(attn_bwd_kernel, heads), out_shape=(wide...]
  transfers between devices with their start and end apart: 12 -> 0, of which waited for: 6 -> 0; matrix products, arithmetic and copies ran while one was open for 17% -> 0% of each run, Pallas kernels for 36% -> 0%
where the time goes in v3:
time: 566 us; the launch traced here: 556 us
  Pallas kernels  407 us (72%)
  matrix products  73.6 us (13%)
  local copies, waits for them, and re-layouts  61.7 us (11%)
  other arithmetic  12.7 us (2%)
    pallas_call x1, Pallas kernels, mix(): pl.pallas_call(mix_kernel, out_shape=(jax.ShapeDtypeStruct((nseq, rows, o...  89.8 us
    pallas_call x1, Pallas kernels, unmix(): pl.pallas_call(functools.partial(unmix_kernel, chunks), out_shape=(jax.Sh...  63.6 us
    pallas_call x1, Pallas kernels, attn_bwd(): pl.pallas_call(functools.partial(attn_bwd_kernel, heads), out_shape=(wide...  62.9 us
    pallas_call x1, Pallas kernels, input_grads(): pl.pallas_call(functools.partial(input_kernel, chunks), out_shape=(jax.Sh...  54.7 us
    pallas_call x1, Pallas kernels, attn_fwd(): pl.pallas_call(functools.partial(attn_fwd_kernel, heads), out_shape=(jax....  50.9 us
    pallas_call x1, Pallas kernels, last_sums(): pl.pallas_call(last_kernel, out_shape=(jax.ShapeDtypeStruct((nseq,) + qkv...  45.6 us
    pallas_call x1, Pallas kernels, tokens_gather(): pl.pallas_call(tokens_gather_kernel, out_shape=(jax.ShapeDtypeStruct((nse...  39.1 us
    dot_general x6, matrix products, dot32(): return jnp.dot(a, b, preferred_element_type=F32)  34.4 us

profile of v3, /device:TPU:0, one launch (start us, length us, event | category | flops | bytes accessed | tf_op | source)
XLA Modules:
  0.0 556.5 jit_solution(4805216152062053462)
XLA Ops:
  0.7 1.2 constant_dynamic-slice_fusion.3
  4.5 1.3 copy-done.2
  5.7 39.1 %tokens_gather.1 = (bf16[1536,1536]{1,0:T(8,128)(2,1)S(1)}, bf16[8,192,640]{2,1,0:T(8,128)(2,1)S(1)}, bf16[8,96,384]{2,1,0:T(8,128)(2,1)S(1)}) custom-call(bf16[384,1536]{1,0:T(8,128)(2,1)S(1)} %bitcast.94, bf16[192,640]{1,0:T(8,128)(2,1)S(1)} %fusion.14.first_q, bf16[96,384]{1,0:T(8,128)(2,1)S(1)} %constant_dynamic-slice_fusion.2.out_q), custom_call_target="tpu_custom_call" | custom-call | tf_op jit(solution)/shard_map/tokens_gather/pallas_call | solution.py:267
  45.7 1.3 convert_reduce_fusion
  47.0 1.0 fusion
  48.0 2.5 convolution_convert_fusion.5.v
  50.6 2.6 convolution_convert_fusion.6.k
  53.2 2.5 convolution_convert_fusion.7.q
  56.5 3.4 reshape.157
  60.2 4.6 reshape.154
  67.7 1.3 copy-done.6
  69.0 1.1 copy-done.9
  70.1 1.1 copy-done.10
  71.3 1.1 copy-done.11
  72.4 1.0 copy-done.17
  73.4 1.1 copy-done.25
  75.1 50.9 %attend_forward.1 = (bf16[1536,192]{1,0:T(8,128)(2,1)S(1)}, f32[8,1536]{1,0:T(8,128)S(1)}, bf16[4,768,384]{2,1,0:T(8,128)(2,1)S(1)}, bf16[1536,1536]{1,0:T(8,128)(2,1)}, bf16[8,192,1024]{2,1,0:T(8,128)(2,1)S(1)}) custom-call(s32[2]{0:T(128)S(1)} %bitcast.117, f32[32,3]{1,0:T(8,128)S(1)} %copy.69.table, s32[8,3072]{1,0:T(8,128)S(1)} %broadcast_in_dim.6.ids, ...), custom_call_target="tpu_custom_call" | custom-call | tf_op jit(solution)/shard_map/attend_forward/pallas_call | solution.py:774
  127.0 1.6 copy-done.14
  130.0 1.2 pad_dynamic-slice_fusion.down_q
  131.1 1.2 copy.79
  132.4 89.8 %mix.1 = (bf16[4,384,192]{2,1,0:T(8,128)(2,1)S(1)}, f32[384,1536]{1,0:T(8,128)S(1)}, bf16[1536,1536]{1,0:T(8,128)(2,1)S(1)}, bf16[8,192,1024]{2,1,0:T(8,128)(2,1)S(1)}, bf16[8,128,1536]{2,1,0:T(8,128)(2,1)S(1)}) custom-call(bf16[1536,192]{1,0:T(8,128)(2,1)S(1)} %copy-done.13, bf16[4,768,384]{2,1,0:T(8,128)(2,1)S(1)} %get-tuple-element.51.out_w, ...), custom_call_target="tpu_custom_call" | custom-call | tf_op jit(solution)/shard_map/mix/pallas_call | solution.py:330
  222.3 7.1 %fusion.19 = f32[1536,1024]{1,0:T(8,128)} fusion(bf16[1536,1536]{1,0:T(8,128)(2,1)S(1)} %copy-done.46, bf16[1024,1536]{1,0:T(8,128)(2,1)S(1)} %bitcast.118), kind=kOutput, calls=%fused_computation.62 | convolution fusion | flops 4831838208 | bytes 14155776 | tf_op jit(solution)/shard_map/dot_general | solution.py:22
  229.3 6.9 %fusion.20 = f32[1536,1024]{1,0:T(8,128)} fusion(bf16[1536,1536]{1,0:T(8,128)(2,1)S(1)} %get-tuple-element.53, bf16[1536,1024]{1,0:T(8,128)(2,1)S(1)} %bitcast.106), kind=kOutput, calls=%fused_computation.63 | convolution fusion | flops 4831838208 | bytes 14155776 | tf_op jit(solution)/shard_map/dot_general | solution.py:1013
  236.2 13.0 %multiply_convert_fusion = (bf16[1536,1024]{1,0:T(8,128)(2,1)}, bf16[1536,1024]{1,0:T(8,128)(2,1)S(1)}, bf16[1536,1024]{1,0:T(8,128)(2,1)}) fusion(f32[1536,1024]{1,0:T(8,128)} %fusion.20, f32[1536,1024]{1,0:T(8,128)} %fusion.19, bf16[1536,1536]{1,0:T(8,128)(2,1)S(1)} %get-tuple-element.53, bf16[1536,1024]{1,0:T(8,128)(2,1)S(1)} %bitcast.107), kind=kOutput, calls=%fused_computation.15 | convolution fusion | flops 4871159808 | bytes 29884416 | tf_op jit(solution)/shard_map/dot_general | solution.py:1013
  249.3 6.6 %convolution_convert_fusion.2 = bf16[1536,1024]{1,0:T(8,128)(2,1)} fusion(bf16[1536,1536]{1,0:T(8,128)(2,1)S(1)} %get-tuple-element.53, bf16[1536,1024]{1,0:T(8,128)(2,1)S(1)} %get-tuple-element.83.dg), kind=kOutput, calls=%fused_computation.19 | convolution fusion | flops 4833411072 | bytes 11010048 | tf_op jit(solution)/shard_map/dot_general | solution.py:1017
  255.9 6.8 %convolution_convert_fusion.ypart = bf16[1536,1536]{1,0:T(8,128)(2,1)} fusion(bf16[1536,1024]{1,0:T(8,128)(2,1)S(1)} %copy-done.47, bf16[1024,1536]{1,0:T(8,128)(2,1)S(1)} %bitcast.119), kind=kOutput, calls=%fused_computation.7 | convolution fusion | flops 4834197504 | bytes 11010048 | tf_op jit(solution)/shard_map/dot_general | solution.py:1013
  262.7 9.0 %convolution_convert_fusion.3 = bf16[1024,1536]{1,0:T(8,128)(2,1)} fusion(bf16[1536,1024]{1,0:T(8,128)(2,1)S(1)} %copy-done.47, bf16[1536,1536]{1,0:T(8,128)(2,1)} %get-tuple-element.50), kind=kOutput, calls=%fused_computation.20 | convolution fusion | flops 4833411072 | bytes 11010048 | tf_op jit(solution)/shard_map/dot_general | solution.py:1017
  271.7 63.6 %unmix.1 = (f32[384,1536]{1,0:T(8,128)}, bf16[1536,192]{1,0:T(8,128)(2,1)}, bf16[4,768,384]{2,1,0:T(8,128)(2,1)}, f32[8,1536]{1,0:T(8,128)}, bf16[128,1536]{1,0:T(8,128)(2,1)}) custom-call(bf16[1536,1024]{1,0:T(8,128)(2,1)} %copy-done.36, bf16[1536,1024]{1,0:T(8,128)(2,1)} %get-tuple-element.84.du, bf16[1536,1024]{1,0:T(8,128)(2,1)} %bitcast.105, ...), custom_call_target="tpu_custom_call" | custom-call | tf_op jit(solution)/shard_map/unmix/pallas_call | solution.py:455
  335.3 62.9 %attend_backward.1 = (f32[1536,192]{1,0:T(8,128)}, f32[1536,192]{1,0:T(8,128)}, f32[1536,192]{1,0:T(8,128)}, f32[3,32,128]{2,1,0:T(8,128)}, bf16[384,1536]{1,0:T...) custom-call(s32[2]{0:T(128)} %bitcast.116, f32[32,3]{1,0:T(8,128)} %copy-done.29, ...), custom_call_target="tpu_custom_call" | custom-call | tf_op jit(solution)/shard_map/attend_backward/pallas_call | solution.py:944
  398.3 1.6 convert.19
  399.9 1.5 convert.20
  402.3 1.3 copy-done.35
  403.5 7.0 %convolution_convert_fusion.4 = bf16[1536,576]{0,1:T(8,128)(2,1)} fusion(bf16[1536,576]{1,0:T(8,128)(2,1)S(1)} %pad_maximum_fusion.dqkv, bf16[1536,1536]{1,0:T(8,128)(2,1)} %copy-done.7, f32[1536]{0:T(1024)S(1)} %copy-done.43, f32[1536]{0:T(1024)S(1)} %copy-done.45), kind=kOutput, calls=%fused_computation.21 | convolution fusion | flops 2728230912 | bytes 8269824 | tf_op jit(solution)/shard_map/dot_general | solution.py:1017
  410.5 2.7 copy.60
  413.3 9.6 %convolution_convert_fusion.1 = bf16[1536,1024]{1,0:T(8,128)(2,1)} fusion(bf16[1536,1536]{1,0:T(8,128)(2,1)} %copy-done.34, bf16[1536,1024]{1,0:T(8,128)(2,1)} %get-tuple-element.84.du), kind=kOutput, calls=%fused_computation.18 | convolution fusion | flops 4833411072 | bytes 11010048 | tf_op jit(solution)/shard_map/dot_general | solution.py:1017
  422.9 54.7 %input_grads.1 = (bf16[384,1536]{1,0:T(8,128)(2,1)S(1)}, f32[8,1536]{1,0:T(8,128)S(1)}, bf16[192,1024]{1,0:T(8,128)(2,1)S(1)}, bf16[4,128,1536]{2,1,0:T(8,128)(2,1)S(1)}, bf16[4,192,1024]{2,1,0:T(8,128)(2,1)}) custom-call(bf16[1536,576]{1,0:T(8,128)(2,1)} %copy-done.35, bf16[1536,640]{1,0:T(8,128)(2,1)} %bitcast.104, bf16[384,1536]{1,0:T(8,128)(2,1)S(1)} %bitcast.96, ...), custom_call_target="tpu_custom_call" | custom-call | tf_op jit(solution)/shard_map/input_grads/pallas_call | solution.py:531
  477.8 45.6 %last_sums.1 = (bf16[4,192,576]{2,1,0:T(8,128)(2,1)S(1)}, bf16[4,96,384]{2,1,0:T(8,128)(2,1)S(1)}, bf16[4,192,1024]{2,1,0:T(8,128)(2,1)S(1)}, f32[56,128]{1,0:T(8,128)S(1)}) custom-call(bf16[8,192,576]{2,1,0:T(8,128)(2,1)S(1)} %bitcast.97, bf16[8,96,384]{2,1,0:T(8,128)(2,1)S(1)} %bitcast.115, bf16[192,1024]{1,0:T(8,128)(2,1)S(1)} %get-tuple-element.70.done, ...), custom_call_target="tpu_custom_call" | custom-call | tf_op jit(solution)/shard_map/last_sums/pallas_call | solution.py:622
  524.1 2.1 slice_convert_fusion
  526.1 5.0 reshape.183
  531.2 1.7 copy.61
  532.9 3.0 copy.62
  536.0 2.8 reshape.180
  538.7 2.8 slice_bitcast_fusion
  542.2 2.1 slice_convert_fusion.1
  544.2 4.9 reshape.182
  552.0 2.0 slice_convert_fusion.2
  554.0 1.0 copy.83
  555.0 1.0 copy.84
  (123 shorter events, 15.5 us)
Async XLA Ops:
  0.6 1.2 copy-start
  4.5 1.3 copy-start.2
  44.9 0.8 copy-start.24
  45.7 7.5 %copy-start.7 = (bf16[1536,1536]{1,0:T(8,128)(2,1)}, bf16[1536,1536]{1,0:T(8,128)(2,1)S(1)}, u32[]{:S(2)}) copy-start(bf16[1536,1536]{1,0:T(8,128)(2,1)S(1)} %get-tuple-element.46) | copy-start | bytes 14155780
  45.7 7.5 %copy-start.8 = (bf16[8,192,640]{2,1,0:T(8,128)(2,1)}, bf16[8,192,640]{2,1,0:T(8,128)(2,1)S(1)}, u32[]{:S(2)}) copy-start(bf16[8,192,640]{2,1,0:T(8,128)(2,1)S(1)} %get-tuple-element.47) | copy-start | bytes 5898244
  47.0 6.2 %copy-start.42 = (f32[1536]{0:T(1024)}, f32[1536]{0:T(1024)S(1)}, u32[]{:S(2)}) copy-start(f32[1536]{0:T(1024)S(1)} %get-tuple-element.81) | copy-start | bytes 18436
  48.0 5.2 copy-start.44
  53.2 3.3 copy-start.39
  56.5 11.2 %copy-start.29 = (f32[32,3]{1,0:T(8,128)}, f32[32,3]{1,0:T(8,128)S(1)}, u32[]{:S(2)}) copy-start(f32[32,3]{1,0:T(8,128)S(1)} %copy.69.table) | copy-start | bytes 1156
  67.7 58.4 %copy-start.22 = (s32[8,3072]{1,0:T(8,128)}, s32[8,3072]{1,0:T(8,128)S(1)}, u32[]{:S(2)}) copy-start(s32[8,3072]{1,0:T(8,128)S(1)} %broadcast_in_dim.6.ids) | copy-start | bytes 294916
  67.7 1.3 copy-start.6
  69.0 1.1 copy-start.9
  70.1 1.1 copy-start.10
  71.3 1.1 copy-start.11
  72.4 1.0 copy-start.17
  73.4 1.1 copy-start.25
  74.5 0.7 copy-start.33
  75.1 57.2 %copy-start.3 = (bf16[1,384,1536]{2,1,0:T(8,128)(2,1)S(1)}, bf16[1,384,1536]{2,1,0:T(8,128)(2,1)}, u32[]{:S(2)}) copy-start(bf16[1,384,1536]{2,1,0:T(8,128)(2,1)} %param.14) | copy-start | bytes 3538948
  126.1 0.9 copy-start.12
  127.0 1.6 copy-start.14
  128.6 0.6 copy-start.31
  129.3 92.9 %copy-start.5 = (bf16[4,768,384]{2,1,0:T(8,128)(2,1)}, bf16[4,768,384]{2,1,0:T(8,128)(2,1)S(1)}, u32[]{:S(2)}) copy-start(bf16[4,768,384]{2,1,0:T(8,128)(2,1)S(1)} %get-tuple-element.51.out_w) | copy-start | bytes 7077892
  130.0 92.3 %copy-start.30 = (f32[1,1536]{1,0:T(1,128)}, f32[1,1536]{1,0:T(1,128)S(1)}, u32[]{:S(2)}) copy-start(f32[1,1536]{1,0:T(1,128)S(1)} %reshape.178.gain) | copy-start | bytes 18436
  130.0 2.4 copy-start.13
  131.1 91.1 %copy-start.46 = (bf16[1536,1536]{1,0:T(8,128)(2,1)S(1)}, bf16[1536,1536]{1,0:T(8,128)(2,1)}, u32[]{:S(2)}) copy-start(bf16[1536,1536]{1,0:T(8,128)(2,1)} %get-tuple-element.50) | copy-start | bytes 14155780
  222.2 7.1 %copy-start.4 = (f32[384,1536]{1,0:T(8,128)}, f32[384,1536]{1,0:T(8,128)S(1)}, u32[]{:S(2)}) copy-start(f32[384,1536]{1,0:T(8,128)S(1)} %get-tuple-element.56.resid) | copy-start | bytes 7077892
  222.2 7.1 %copy-start.23 = (bf16[4,384,192]{2,1,0:T(8,128)(2,1)}, bf16[4,384,192]{2,1,0:T(8,128)(2,1)S(1)}, u32[]{:S(2)}) copy-start(bf16[4,384,192]{2,1,0:T(8,128)(2,1)S(1)} %get-tuple-element.57.obuf) | copy-start | bytes 1769476
  222.2 14.0 %copy-start.16 = (bf16[8,192,1024]{2,1,0:T(8,128)(2,1)}, bf16[8,192,1024]{2,1,0:T(8,128)(2,1)S(1)}, u32[]{:S(2)}) copy-start(bf16[8,192,1024]{2,1,0:T(8,128)(2,1)S(1)} %get-tuple-element.54) | copy-start | bytes 9437188
  222.2 27.0 %copy-start.34 = (bf16[1536,1536]{1,0:T(8,128)(2,1)}, bf16[1536,1536]{1,0:T(8,128)(2,1)S(1)}, u32[]{:S(2)}) copy-start(bf16[1536,1536]{1,0:T(8,128)(2,1)S(1)} %get-tuple-element.53) | copy-start | bytes 14155780
  222.3 7.1 %copy-start.15 = (bf16[8,192,1024]{2,1,0:T(8,128)(2,1)S(1)}, bf16[8,192,1024]{2,1,0:T(8,128)(2,1)}, u32[]{:S(2)}) copy-start(bf16[8,192,1024]{2,1,0:T(8,128)(2,1)} %copy-done.14) | copy-start | bytes 9437188
  249.3 6.6 %copy-start.36 = (bf16[1536,1024]{1,0:T(8,128)(2,1)}, bf16[1536,1024]{1,0:T(8,128)(2,1)S(1)}, u32[]{:S(2)}) copy-start(bf16[1536,1024]{1,0:T(8,128)(2,1)S(1)} %get-tuple-element.83.dg) | copy-start | bytes 9437188
  249.3 6.6 %copy-start.47 = (bf16[1536,1024]{1,0:T(8,128)(2,1)S(1)}, bf16[1536,1024]{1,0:T(8,128)(2,1)}, u32[]{:S(2)}) copy-start(bf16[1536,1024]{1,0:T(8,128)(2,1)} %get-tuple-element.82) | copy-start | bytes 9437188
  398.3 3.1 copy-start.38
  401.4 2.2 copy-start.43
  401.4 2.1 copy-start.45
  402.3 1.3 copy-start.35
  413.3 9.6 %copy-start.27 = (bf16[128,1536]{1,0:T(8,128)(2,1)S(1)}, bf16[128,1536]{1,0:T(8,128)(2,1)}, u32[]{:S(2)}) copy-start(bf16[128,1536]{1,0:T(8,128)(2,1)} %get-tuple-element.66.done0) | copy-start | bytes 1179652
  413.3 9.6 %copy-start.28 = (bf16[192,1024]{1,0:T(8,128)(2,1)S(1)}, bf16[192,1024]{1,0:T(8,128)(2,1)}, u32[]{:S(2)}) copy-start(bf16[192,1024]{1,0:T(8,128)(2,1)} %get-tuple-element.67.done1) | copy-start | bytes 1179652
  422.9 54.8 %copy-start.41 = (f32[3,32,128]{2,1,0:T(8,128)S(1)}, f32[3,32,128]{2,1,0:T(8,128)}, u32[]{:S(2)}) copy-start(f32[3,32,128]{2,1,0:T(8,128)} %get-tuple-element.73) | copy-start | bytes 147460
  422.9 54.9 %copy-start.26 = (bf16[768,384]{1,0:T(8,128)(2,1)S(1)}, bf16[768,384]{1,0:T(8,128)(2,1)}, u32[]{:S(2)}) copy-start(bf16[768,384]{1,0:T(8,128)(2,1)} %get-tuple-element.69) | copy-start | bytes 1769476
  422.9 54.9 %copy-start.32 = (f32[8,1536]{1,0:T(8,128)S(1)}, f32[8,1536]{1,0:T(8,128)}, u32[]{:S(2)}) copy-start(f32[8,1536]{1,0:T(8,128)} %get-tuple-element.72.gain_b) | copy-start | bytes 147460
  477.6 46.4 %copy-start.18 = (bf16[4,128,1536]{2,1,0:T(8,128)(2,1)}, bf16[4,128,1536]{2,1,0:T(8,128)(2,1)S(1)}, u32[]{:S(2)}) copy-start(bf16[4,128,1536]{2,1,0:T(8,128)(2,1)S(1)} %get-tuple-element.79) | copy-start | bytes 4718596
  477.6 46.4 %copy-start.20 = (bf16[384,1536]{1,0:T(8,128)(2,1)}, bf16[384,1536]{1,0:T(8,128)(2,1)S(1)}, u32[]{:S(2)}) copy-start(bf16[384,1536]{1,0:T(8,128)(2,1)S(1)} %get-tuple-element.68) | copy-start | bytes 3538948
  538.7 2.8 copy-start.37
  544.2 7.7 %copy-start.19 = (bf16[4,128,1536]{2,1,0:T(8,128)(2,1)S(1)}, bf16[4,128,1536]{2,1,0:T(8,128)(2,1)}, u32[]{:S(2)}) copy-start(bf16[4,128,1536]{2,1,0:T(8,128)(2,1)} %copy-done.18) | copy-start | bytes 4718596
  550.1 3.9 copy-start.40
  552.0 3.1 copy-start.21
  552.0 4.1 copy-start.1

commit v4 on v3

--- a/solution.py
+++ b/solution.py
@@ -88,12 +88,22 @@
         self.trip(0, c).wait_recv()
         self.trip(2, c).start()
 
+    def got_near(self, c):
+        self.trip(1, c).wait_recv()
+
+    def got_cross(self, c):
+        self.trip(2, c).wait_recv()
+
+    def drain(self):
+        for c in range(self.chunks):
+            for kind in range(3):
+                self.trip(kind, c).wait_send()
+
     def finish(self):
         for c in range(self.chunks):
-            self.trip(1, c).wait_recv()
-            self.trip(2, c).wait_recv()
-            for kind in range(3):
-                self.trip(kind, c).wait_send()
+            self.got_near(c)
+            self.got_cross(c)
+        self.drain()
 
 
 def fsdp_places():
@@ -108,27 +118,27 @@
 
 
 class FsdpGather:
-    def __init__(self, wires, shard, full, local):
-        self.wires, self.shard, self.full, self.local = wires, shard, full, local
+    def __init__(self, wires, shard, full_at, local):
+        self.wires, self.shard, self.full_at, self.local = wires, shard, full_at, local
         self.pair, self.side, self.pairs = fsdp_places()
         self.base = wires.take(2 * self.pairs)
 
-    def view(self, d, side):
-        return self.full.at[lax.rem(self.pair + d, self.pairs) * 2 + side]
+    def source(self, d):
+        return lax.rem(self.pair + self.pairs - d, self.pairs)
 
     def out(self, d):
-        own = self.view(0, self.side)
+        own = self.full_at(self.pair * 2 + self.side)
         if d == 0:
             return self.wires.at(self.base, self.shard, own, {"fsdp": self.pair * 2 + 1 - self.side})
         where = {"fsdp": lax.rem(self.pair + d, self.pairs) * 2 + self.side}
         return self.wires.at(self.base + d, self.shard, own, where)
 
     def onward(self, d):
-        view = self.view(self.pairs - d, self.side)
+        view = self.full_at(self.source(d) * 2 + self.side)
         return self.wires.at(self.base + self.pairs + d, view, view, {"fsdp": self.pair * 2 + 1 - self.side})
 
     def keep(self):
-        return pltpu.make_async_copy(self.shard, self.view(0, self.side), self.local)
+        return pltpu.make_async_copy(self.shard, self.full_at(self.pair * 2 + self.side), self.local)
 
     def start(self):
         self.out(0).start()
@@ -140,15 +150,23 @@
         self.out(d).wait_recv()
         self.onward(d).start()
 
-    def finish(self):
-        self.keep().wait()
-        self.out(0).wait_recv()
-        for d in range(1, self.pairs):
+    def complete(self, d):
+        if d == 0:
+            self.keep().wait()
+            self.out(0).wait_recv()
+        else:
             self.onward(d).wait_recv()
+
+    def drain(self):
         for d in range(self.pairs):
             self.out(d).wait_send()
         for d in range(1, self.pairs):
             self.onward(d).wait_send()
+
+    def finish(self):
+        for d in range(self.pairs):
+            self.complete(d)
+        self.drain()
 
 
 class FsdpScatter:
@@ -209,6 +227,10 @@
     return a.reshape((count, a.shape[0] // count) + a.shape[1:])
 
 
+def shard_rows(f, size):
+    return pl.ds(pl.multiple_of(f * size, 16 if size % 16 == 0 else 8 if size % 8 == 0 else size), size)
+
+
 def vm_spec():
     return pl.BlockSpec(memory_space=pltpu.VMEM)
 
@@ -234,115 +256,175 @@
     return r * scaled - v * (r * r * r) * jnp.mean(v * scaled, axis=-1, keepdims=True)
 
 
-def tokens_gather_kernel(src, first_q, out_q, out, first, out_w, send, recv, local):
-    rows = src.shape[0]
-    s, near, far, cross = seq_places()
-    meet([{"seq": near}, {"seq": far}] + fsdp_peers())
-    half = rows // 2
-    wires = Wires(send, recv)
-    ring = SeqGather(wires, lambda t, c: out.at[rows_at(t, rows, c * half, half), :], 2)
-    lead = FsdpGather(wires, first_q, first, local.at[1])
-    late = FsdpGather(wires, out_q, out_w, local.at[2])
-    own = pltpu.make_async_copy(src, out.at[rows_at(s, rows), :], local.at[0])
-    lead.start()
-    for c in range(2):
-        ring.send(c, src.at[pl.ds(c * half, half), :])
-    late.start()
-    own.start()
-    for d in range(1, lead.pairs):
-        lead.forward(d)
-        if d == lead.pairs // 2:
-            ring.forward(0)
-    for d in range(1, late.pairs):
-        late.forward(d)
-    ring.forward(1)
-    own.wait()
-    lead.finish()
-    late.finish()
-    ring.finish()
-
-
-def tokens_gather(tokens, first_q, out_q, nseq, nfsdp):
-    rows, width = tokens.shape
-    return pl.pallas_call(
-        tokens_gather_kernel,
-        out_shape=(
-            jax.ShapeDtypeStruct((nseq * rows, width), BF16),
-            jax.ShapeDtypeStruct((nfsdp,) + first_q.shape, BF16),
-            jax.ShapeDtypeStruct((nfsdp,) + out_q.shape, BF16),
-        ),
-        in_specs=[any_spec()] * 3,
-        out_specs=(any_spec(),) * 3,
-        scratch_shapes=wires_scratch(6 + 2 * nfsdp) + [pltpu.SemaphoreType.DMA((3,))],
-        compiler_params=call_params(0, 4),
-        name="tokens_gather",
-    )(tokens, first_q, out_q)
-
-
-def mix_kernel(o, out_w, tok, gain, up_q, down_q, obuf, resid, n2, up_w, down_w, send, recv, own, local):
+def middle_kernel(
+    o, out_w, tok, gains, up_q, down_q, gate_h, cot_h,
+    obuf, resid, n2_h, hid_h, dg_h, du_h, up_h, down_h, parts_h,
+    send, recv, local, own, n2, cot, gate_w, up_w, down_w, ga, ub, hid, dg, du, parts,
+):
     rows, width = tok.shape
     piece = o.shape[1]
     nseq = obuf.shape[0]
+    units = gate_w.shape[1]
+    nfsdp = parts.shape[0]
     s, near, far, cross = seq_places()
+    loads = [pltpu.make_async_copy(gate_h, gate_w, local.at[0]), pltpu.make_async_copy(cot_h, cot, local.at[1])]
+    for a in loads:
+        a.start()
     meet([{"seq": near}, {"seq": far}, {"seq": cross}] + fsdp_peers())
     wires = Wires(send, recv)
-    weights = [FsdpGather(wires, up_q, up_w, local.at[1]), FsdpGather(wires, down_q, down_w, local.at[2])]
-    for a in weights:
-        a.start()
     trips = [wires.go(o.at[rows_at(t, rows), :], obuf.at[s], {"seq": t}) for t in (far, cross, near)]
+    up_size, down_size = up_q.shape[0], down_q.shape[0]
+    ups = FsdpGather(wires, up_q, lambda f: up_w.at[shard_rows(f, up_size), :], local.at[2])
+    downs = FsdpGather(wires, down_q, lambda f: down_w.at[shard_rows(f, down_size), :], local.at[3])
+    ups.start()
+    downs.start()
     obuf[s] = o[rows_at(s, rows), :]
     half = rows // 2
     for a in trips:
         a.wait_recv()
     ring = SeqGather(wires, lambda t, c: n2.at[rows_at(t, rows, c * half, half), :], 2)
+    cols = out_w.shape[2]
     for c in range(2):
         part = slice(c * half, (c + 1) * half)
-        cols = out_w.shape[2]
         for u in range(nseq):
             acc = tok[part, u * cols : (u + 1) * cols].astype(F32)
             for t in range(nseq):
                 acc = acc + nn(obuf[t, part, :], out_w[u, t * piece : (t + 1) * piece, :])
             resid[part, u * cols : (u + 1) * cols] = acc
         h = resid[part, :]
-        own[part, :] = (h * inverse_rms(h) * gain[...]).astype(BF16)
+        low = (h * inverse_rms(h) * gains[1:2, :]).astype(BF16)
+        own[part, :] = low
+        n2[rows_at(s, rows, c * half, half), :] = low
         ring.send(c, own.at[pl.ds(c * half, half), :])
-    mineblock = pltpu.make_async_copy(own, n2.at[rows_at(s, rows), :], local.at[0])
-    mineblock.start()
-    pairs = weights[0].pairs
-    weights[0].forward(1)
-    ring.forward(0)
+    loads[0].wait()
+
+    def gate_rows(t):
+        ga[rows_at(t, rows), :] = nn(n2[rows_at(t, rows), :], gate_w[...])
+
+    def act_rows(t):
+        up = nn(n2[rows_at(t, rows), :], up_w[...])
+        active, slope = gelu_both(ga[rows_at(t, rows), :])
+        hid[rows_at(t, rows), :] = (active * up).astype(BF16)
+        ga[rows_at(t, rows), :] = slope * up
+        ub[rows_at(t, rows), :] = active
+
+    pairs = ups.pairs
+    ups.forward(1)
+    gate_rows(s)
+    ring.got_near(0)
+    ring.got_near(1)
+    gate_rows(near)
     for d in range(2, pairs):
-        weights[0].forward(d)
+        ups.forward(d)
+        if d == 2:
+            ring.forward(0)
     ring.forward(1)
-    for d in range(1, pairs):
-        weights[1].forward(d)
-    for a in weights:
-        a.finish()
-    mineblock.wait()
-    ring.finish()
+    downs.forward(1)
+    gate_rows(far)
+    for c in range(2):
+        ring.got_cross(c)
+    gate_rows(cross)
+    saves = [pltpu.make_async_copy(n2, n2_h, local.at[4])]
+    saves[0].start()
+    for d in range(pairs):
+        ups.complete(d)
+    saves.append(pltpu.make_async_copy(up_w, up_h, local.at[5]))
+    saves[1].start()
+    for t in (s, near):
+        act_rows(t)
+    downs.forward(2) if pairs > 2 else None
+    for t in (far, cross):
+        act_rows(t)
+    saves.append(pltpu.make_async_copy(hid, hid_h, local.at[6]))
+    saves[2].start()
+    loads[1].wait()
+    width_f = units // nfsdp
+    wide = max(256 // width_f, 1)
+
+    def down_part(n):
+        got = dot_tn(hid[:, n * wide * width_f : (n + 1) * wide * width_f], cot[...]).astype(BF16)
+        for m in range(wide):
+            parts[n * wide + m] = got[m * width_f : (m + 1) * width_f, :]
+
+    for n in range(nfsdp // wide):
+        down_part(n)
+        if n == 1:
+            for d in range(3, pairs):
+                downs.forward(d)
+    saves.append(pltpu.make_async_copy(parts, parts_h, local.at[7]))
+    saves[3].start()
+
+    def back_cols(at, units_at):
+        for t in range(nseq):
+            band = slice(t * rows, (t + 1) * rows)
+            dh = nt(cot[band, :], down_w[units_at, :])
+            dg[band, at] = (dh * ga[band, at]).astype(BF16)
+            du[band, at] = (dh * ub[band, at]).astype(BF16)
+
+    if (2 * width_f) % 128 == 0:
+        for d in range(pairs):
+            downs.complete(d)
+            at = pl.ds(pl.multiple_of(downs.source(d) * 2 * width_f, 2 * width_f), 2 * width_f)
+            back_cols(at, at)
+    else:
+        for d in range(pairs):
+            downs.complete(d)
+        for n in range(units // 256):
+            at = slice(n * 256, (n + 1) * 256)
+            back_cols(at, at)
+    saves.append(pltpu.make_async_copy(down_w, down_h, local.at[8]))
+    saves.append(pltpu.make_async_copy(dg, dg_h, local.at[9]))
+    saves.append(pltpu.make_async_copy(du, du_h, local.at[10]))
+    for a in saves[4:]:
+        a.start()
+    ring.drain()
+    ups.drain()
+    downs.drain()
     for a in trips:
         a.wait_send()
-
-
-def mix(o, out_w, tok, gain, up_q, down_q, nfsdp):
+    for a in saves:
+        a.wait()
+
+
+def middle(o, out_w, tok, gains, up_q, down_q, gate_w, cot, nfsdp):
     nseq = out_w.shape[0]
     rows, width = tok.shape
+    units = gate_w.shape[1]
+    tall = nseq * rows
     return pl.pallas_call(
-        mix_kernel,
+        middle_kernel,
         out_shape=(
             jax.ShapeDtypeStruct((nseq, rows, o.shape[1]), BF16),
             jax.ShapeDtypeStruct((rows, width), F32),
-            jax.ShapeDtypeStruct((nseq * rows, width), BF16),
-            jax.ShapeDtypeStruct((nfsdp,) + up_q.shape, BF16),
-            jax.ShapeDtypeStruct((nfsdp,) + down_q.shape, BF16),
+            jax.ShapeDtypeStruct((tall, width), BF16),
+            jax.ShapeDtypeStruct((tall, units), BF16),
+            jax.ShapeDtypeStruct((tall, units), BF16),
+            jax.ShapeDtypeStruct((tall, units), BF16),
+            jax.ShapeDtypeStruct((width, units), BF16),
+            jax.ShapeDtypeStruct((units, width), BF16),
+            jax.ShapeDtypeStruct((nfsdp, units // nfsdp, width), BF16),
         ),
-        in_specs=[vm_spec()] * 4 + [any_spec()] * 2,
-        out_specs=(vm_spec(), vm_spec()) + (any_spec(),) * 3,
+        in_specs=[vm_spec()] * 4 + [any_spec()] * 4,
+        out_specs=(vm_spec(), vm_spec()) + (any_spec(),) * 7,
         scratch_shapes=wires_scratch(9 + 2 * nfsdp)
-        + [pltpu.VMEM((rows, width), BF16), pltpu.SemaphoreType.DMA((3,))],
-        compiler_params=call_params(2, 32),
-        name="mix",
-    )(o, out_w, tok, gain, up_q, down_q)
+        + [
+            pltpu.SemaphoreType.DMA((11,)),
+            pltpu.VMEM((rows, width), BF16),
+            pltpu.VMEM((tall, width), BF16),
+            pltpu.VMEM((tall, width), BF16),
+            pltpu.VMEM((width, units), BF16),
+            pltpu.VMEM((width, units), BF16),
+            pltpu.VMEM((units, width), BF16),
+            pltpu.VMEM((tall, units), F32),
+            pltpu.VMEM((tall, units), F32),
+            pltpu.VMEM((tall, units), BF16),
+            pltpu.VMEM((tall, units), BF16),
+            pltpu.VMEM((tall, units), BF16),
+            pltpu.VMEM((nfsdp, units // nfsdp, width), BF16),
+        ],
+        compiler_params=call_params(2, 63),
+        name="middle",
+    )(o, out_w, tok, gains, up_q, down_q, gate_w, cot)
 
 
 class SeqScatter:
@@ -684,33 +766,161 @@
     return jnp.concatenate(parts, axis=0)
 
 
-def attn_fwd_kernel(
-    heads, starts, table, ids, q, k, v, out_q, cot, gate_q,
-    o, lse, out_w, cots, gate_w,
-    strip, far, kh, vt, ot, s, send, recv, local,
+def pack_piece(units, nfsdp, nseq):
+    block = units // nfsdp
+    return block, -(-block // (16 * nseq)) * 16
+
+
+def pack_front(t, raw, first_q, out_q, gains):
+    r_q, r_k, r_v, r_o = raw
+    piece = first_q.shape[1] * 3 // 10
+    depth = first_q.shape[0]
+    cut = slice(t * piece, (t + 1) * piece)
+    first_q[...] = jnp.concatenate(
+        [r_q[:, cut], r_k[:, cut], r_v[:, cut], gains, jnp.zeros((depth, first_q.shape[1] - 3 * piece - 8), BF16)], axis=1
+    )
+    cols = out_q.shape[1]
+    out_q[...] = r_o[:, t * cols : (t + 1) * cols]
+
+
+def pack_cols(t, nseq, nfsdp, raw, packed):
+    block, piece = pack_piece(raw.shape[1], nfsdp, nseq)
+    pieces = []
+    for f in range(nfsdp):
+        begin = f * block + t * piece
+        end = min(begin + piece, (f + 1) * block)
+        pieces.append(raw[:, begin:end])
+        if end - begin < piece:
+            pieces.append(jnp.zeros((raw.shape[0], piece - end + begin), BF16))
+    packed[...] = jnp.concatenate(pieces, axis=1)
+
+
+def pack_down(t, raw, packed):
+    piece = packed.shape[0]
+    begin = t * piece
+    end = min(begin + piece, raw.shape[0])
+    packed[: end - begin, :] = raw[begin:end, :]
+    if end - begin < piece:
+        packed[end - begin :, :] = jnp.zeros((piece - end + begin, raw.shape[1]), BF16)
+
+
+def front_kernel(
+    heads, nseq, starts, table, ids, gain_a, gain_b, tok, w_q, w_k, w_v, w_o, w_g, w_u, w_d, cot,
+    q, k, v, o, lse, gains, n1_h, first_h, out_w, cots, gate_w, up_q, down_q,
+    send, recv, local, r_q, r_k, r_v, r_o, r_g, r_u, r_d, first_q, out_q, gate_q, up_s, down_s,
+    group, n1, first, strip, far, kh, vt, ot, s,
 ):
-    rows = cot.shape[0]
+    rows, width = tok.shape
     mine, near, other, cross = seq_places()
+    pair, side, pairs = fsdp_places()
+    nfsdp = 2 * pairs
+    loads = [
+        pltpu.make_async_copy(src, dst, local.at[n])
+        for n, (src, dst) in enumerate(
+            ((w_q, r_q), (w_k, r_k), (w_v, r_v), (w_o, r_o), (w_g, r_g), (w_u, r_u), (w_d, r_d))
+        )
+    ]
+    for a in loads:
+        a.start()
     meet([{"seq": near}, {"seq": other}] + fsdp_peers())
     wires = Wires(send, recv)
     half = rows // 2
-    weight = FsdpGather(wires, gate_q, gate_w, local.at[2])
-    weight.start()
+    ring = SeqGather(wires, lambda t, c: group.at[rows_at(t, rows, c * half, half), :], 2)
+    size = first_q.shape[0]
+    lead = FsdpGather(wires, first_q, lambda f: first.at[shard_rows(f, size), :], local.at[7])
+    late = FsdpGather(wires, out_q, lambda f: out_w.at[mine, f], local.at[8])
+    gate_size = gate_q.shape[0]
+    weight = FsdpGather(wires, gate_q, lambda f: gate_w.at[shard_rows(f, gate_size), :], local.at[9])
     wring = SeqGather(wires, lambda t, c: out_w.at[t], 1)
     cring = SeqGather(wires, lambda t, c: cots.at[rows_at(t, rows, c * half, half), :], 2)
-    wring.send(0, out_q)
+    own = [
+        pltpu.make_async_copy(tok, group.at[rows_at(mine, rows), :], local.at[10]),
+        pltpu.make_async_copy(cot, cots.at[rows_at(mine, rows), :], local.at[11]),
+    ]
+    for c in range(2):
+        ring.send(c, tok.at[pl.ds(c * half, half), :])
+    for a in own:
+        a.start()
+    for a in loads[:4]:
+        a.wait()
+    both = jnp.concatenate([gain_a[...], gain_b[...], jnp.zeros((6, gain_a.shape[1]), BF16)], axis=0)
+    both = both.astype(F32).T.astype(BF16)
+    for t in range(nseq):
+
+        @pl.when(mine == t)
+        def _():
+            pack_front(t, (r_q, r_k, r_v, r_o), first_q, out_q, both)
+
+    for a in loads[4:]:
+        a.wait()
+    lead.start()
+    for t in range(nseq):
+
+        @pl.when(mine == t)
+        def _():
+            pack_cols(t, nseq, nfsdp, r_g, gate_q)
+
+    late.start()
+    for t in range(nseq):
+
+        @pl.when(mine == t)
+        def _():
+            pack_cols(t, nseq, nfsdp, r_u, up_s)
+            pack_down(t, r_d, down_s)
+
+    weight.start()
     for c in range(2):
         cring.send(c, cot.at[pl.ds(c * half, half), :])
-    own = [
-        pltpu.make_async_copy(out_q, out_w.at[mine], local.at[0]),
-        pltpu.make_async_copy(cot, cots.at[rows_at(mine, rows), :], local.at[1]),
-    ]
-    for a in own:
+    saves = [pltpu.make_async_copy(up_s, up_q, local.at[12]), pltpu.make_async_copy(down_s, down_q, local.at[13])]
+    for a in saves:
         a.start()
     build_strips(heads, starts, table, ids, strip, far)
+    lse[...] = jnp.zeros(lse.shape, F32)
+    for d in range(1, pairs):
+        lead.forward(d)
+        if d == pairs // 2:
+            ring.forward(0)
+    for d in range(1, pairs):
+        late.forward(d)
+    ring.forward(1)
+    lead.finish()
+    saves.append(pltpu.make_async_copy(first, first_h, local.at[14]))
+    saves[2].start()
+    piece = q.shape[1]
+    column = 3 * piece
+    gains[...] = jnp.zeros(gains.shape, F32)
+    for b in range(width // 256):
+        band = first[b * 256 : (b + 1) * 256, column // 128 * 128 : column // 128 * 128 + 128].astype(F32).T
+        for n in range(2):
+            line = column % 128 + n
+            gains[n : n + 1, b * 256 : (b + 1) * 256] = band[line : line + 1, :]
+
+    def project(t):
+        at = rows_at(t, rows)
+        x = group[at, :].astype(F32)
+        low = (x * inverse_rms(x) * gains[0:1, :]).astype(BF16)
+        n1[at, :] = low
+        r = nn(low, first[:, :column])
+        q[at, :] = r[:, :piece].astype(BF16)
+        k[at, :] = r[:, piece : 2 * piece].astype(BF16)
+        v[at, :] = r[:, 2 * piece :].astype(BF16)
+
+    own[0].wait()
+    project(mine)
+    for c in range(2):
+        ring.got_near(c)
+    project(near)
+    project(other)
+    for c in range(2):
+        ring.got_cross(c)
+    project(cross)
+    saves.append(pltpu.make_async_copy(n1, n1_h, local.at[15]))
+    saves[3].start()
+    for d in range(pairs):
+        late.complete(d)
+    wring.send(0, out_w.at[mine])
     masked_copies(k, kh, heads)
     vt[...] = v[...].astype(F32).T.astype(BF16)
-    lse[...] = jnp.zeros(lse.shape, F32)
 
     def block(h, q0, bias_q0, chunks, c):
         qb = q[pl.ds(q0, CL), :]
@@ -735,10 +945,11 @@
         h, blk = i // nblk, i % nblk
         q0 = pl.multiple_of(blk * CL, CL)
         block(h, q0, q0, [(j * KC, "strip", j * KC) for j in range(PROMPT // KC)], None)
-
-        @pl.when(i == 6)
-        def _():
-            weight.forward(1)
+        for d in range(1, pairs - 1):
+
+            @pl.when(i == heads * nblk * d // pairs)
+            def _():
+                weight.forward(d)
 
         return carry
 
@@ -752,49 +963,79 @@
         block(h, q0, 0, chunks, c)
         return carry
 
-    wring.forward(0)
+    cring.forward(0)
     lax.fori_loop(0, heads * 2, cont_body, 0)
     o[...] = ot[...].T.astype(BF16)
-    cring.forward(0)
-    for d in range(2, weight.pairs):
-        weight.forward(d)
+    weight.forward(pairs - 1)
     cring.forward(1)
-    for a in own:
+    wring.forward(0)
+    for a in own[1:] + saves:
         a.wait()
     weight.finish()
+    late.drain()
     wring.finish()
     cring.finish()
-
-
-def attn_fwd(starts, table, ids, q, k, v, out_q, cot, gate_q, nseq, nfsdp):
-    rows, width = q.shape
-    heads = width // HEAD_DIM
+    ring.drain()
+
+
+def front(starts, table, ids, gain_a, gain_b, tok, w_q, w_k, w_v, w_o, w_g, w_u, w_d, cot, nseq, nfsdp):
+    rows, width = tok.shape
+    inner = w_q.shape[1]
+    piece = inner // nseq
+    heads = piece // HEAD_DIM
+    tall = nseq * rows
+    size = w_q.shape[0]
+    units = pack_piece(w_g.shape[1], nfsdp, nseq)[1]
+    cols = width // nseq
+    lead = piece * 10 // 3
     smem = pl.BlockSpec(memory_space=pltpu.SMEM)
-    vm = pl.BlockSpec(memory_space=pltpu.VMEM)
     return pl.pallas_call(
-        functools.partial(attn_fwd_kernel, heads),
+        functools.partial(front_kernel, heads, nseq),
         out_shape=(
-            jax.ShapeDtypeStruct((rows, width), BF16),
-            jax.ShapeDtypeStruct((8, rows), F32),
-            jax.ShapeDtypeStruct((nseq,) + out_q.shape, BF16),
-            jax.ShapeDtypeStruct((rows, cot.shape[1]), BF16),
-            jax.ShapeDtypeStruct((nfsdp,) + gate_q.shape, BF16),
+            jax.ShapeDtypeStruct((tall, piece), BF16),
+            jax.ShapeDtypeStruct((tall, piece), BF16),
+            jax.ShapeDtypeStruct((tall, piece), BF16),
+            jax.ShapeDtypeStruct((tall, piece), BF16),
+            jax.ShapeDtypeStruct((8, tall), F32),
+            jax.ShapeDtypeStruct((8, width), F32),
+            jax.ShapeDtypeStruct((tall, width), BF16),
+            jax.ShapeDtypeStruct((width, lead), BF16),
+            jax.ShapeDtypeStruct((nseq, nfsdp, w_o.shape[0], cols), BF16),
+            jax.ShapeDtypeStruct((tall, width), BF16),
+            jax.ShapeDtypeStruct((width, nfsdp * units), BF16),
+            jax.ShapeDtypeStruct((size, nfsdp * units), BF16),
+            jax.ShapeDtypeStruct((nseq * units // nseq, width), BF16),
         ),
-        in_specs=[smem, smem, vm, vm, vm, vm] + [any_spec()] * 3,
-        out_specs=(vm, vm) + (any_spec(),) * 3,
-        scratch_shapes=[
+        in_specs=[smem, smem, vm_spec(), vm_spec(), vm_spec()] + [any_spec()] * 9,
+        out_specs=(vm_spec(),) * 6 + (any_spec(),) * 7,
+        scratch_shapes=wires_scratch(15 + 3 * nfsdp)
+        + [
+            pltpu.SemaphoreType.DMA((16,)),
+            pltpu.VMEM(w_q.shape, BF16),
+            pltpu.VMEM(w_k.shape, BF16),
+            pltpu.VMEM(w_v.shape, BF16),
+            pltpu.VMEM(w_o.shape, BF16),
+            pltpu.VMEM(w_g.shape, BF16),
+            pltpu.VMEM(w_u.shape, BF16),
+            pltpu.VMEM(w_d.shape, BF16),
+            pltpu.VMEM((size, lead), BF16),
+            pltpu.VMEM((w_o.shape[0], cols), BF16),
+            pltpu.VMEM((size, nfsdp * units), BF16),
+            pltpu.VMEM((size, nfsdp * units), BF16),
+            pltpu.VMEM((units, width), BF16),
+            pltpu.VMEM((tall, width), BF16),
+            pltpu.VMEM((tall, width), BF16),
+            pltpu.VMEM((width, lead), BF16),
             pltpu.VMEM((heads, 128, STRIP), F32),
             pltpu.VMEM((heads, 2, 128, FARW), F32),
-            pltpu.VMEM((heads, rows, width), BF16),
-            pltpu.VMEM((width, rows), BF16),
-            pltpu.VMEM((width, rows), F32),
+            pltpu.VMEM((heads, tall, piece), BF16),
+            pltpu.VMEM((piece, tall), BF16),
+            pltpu.VMEM((piece, tall), F32),
             pltpu.VMEM((PROMPT + CL, CL), F32),
-        ]
-        + wires_scratch(9 + nfsdp)
-        + [pltpu.SemaphoreType.DMA((3,))],
-        compiler_params=call_params(1, 40),
-        name="attend_forward",
-    )(starts, table, ids, q, k, v, out_q, cot, gate_q)
+        ],
+        compiler_params=call_params(1, 60),
+        name="front",
+    )(starts, table, ids, gain_a, gain_b, tok, w_q, w_k, w_v, w_o, w_g, w_u, w_d, cot)
 
 
 def attn_bwd_kernel(
@@ -984,29 +1225,12 @@
     return jnp.broadcast_to(ids[None, :], (8, span + 1))
 
 
-def pack_columns(w, nseq, nfsdp, mine):
-    depth, total = w.shape
-    block = total // nfsdp
-    piece = -(-block // (16 * nseq)) * 16
-    w = jnp.pad(w.reshape(depth, nfsdp, block), ((0, 0), (0, 0), (0, nseq * piece - block)))
-    w = w.reshape(depth, nfsdp, nseq, piece)
-    w = lax.dynamic_index_in_dim(w, mine, 2, keepdims=False)
-    return w.reshape(depth, nfsdp * piece)
-
-
 def unpack_columns(parts, total, nfsdp):
     nseq, depth, width = parts.shape
     piece = width // nfsdp
     block = total // nfsdp
     w = parts.reshape(nseq, depth, nfsdp, piece).transpose(1, 2, 0, 3)
     return w.reshape(depth, nfsdp, nseq * piece)[:, :, :block].reshape(depth, total)
-
-
-def pack_rows(w, nseq, mine):
-    block, depth = w.shape
-    piece = -(-block // (16 * nseq)) * 16
-    w = jnp.pad(w, ((0, nseq * piece - block), (0, 0)))
-    return lax.dynamic_slice_in_dim(w, mine * piece, piece, 0)
 
 
 def dot32(a, b):
@@ -1051,47 +1275,33 @@
     heads = piece // HEAD_DIM
     hidden_all = w_gate.shape[1]
 
-    local = [lax.dynamic_slice_in_dim(w, mine * piece, piece, 1) for w in (w_query, w_key, w_value)]
-    gains = jnp.pad(jnp.stack([attn_gain, mix_gain], axis=1), ((0, 0), (0, 62)))
-    out_cols = width // nseq
-    out_local = lax.dynamic_slice_in_dim(w_out, mine * out_cols, out_cols, 1)
-    group, first, out_q = tokens_gather(
-        tokens[0], jnp.concatenate(local + [gains], axis=1), out_local, nseq, nfsdp
-    )
-    first = first.reshape(width, -1)
-    out_q = out_q.reshape(inner, out_cols)
-    query_w, key_w, value_w = (first[:, i * piece : (i + 1) * piece] for i in range(3))
-    gain_one = first[:, 3 * piece].astype(F32)
-    gain_two = first[:, 3 * piece + 1].astype(F32)
-    group = group.astype(F32)
-    normed = (group * inverse_rms(group) * gain_one).astype(BF16)
-    query = dot32(normed, query_w).astype(BF16)
-    keys = dot32(normed, key_w).astype(BF16)
-    values = dot32(normed, value_w).astype(BF16)
     table = lax.dynamic_slice_in_dim(rel_table, mine * heads, heads, 1)
     ids = reversed_ids(bucket_ids)
     starts = cont_start[0]
-    gate_q = pack_columns(w_gate, nseq, nfsdp, mine)
-    up_q = pack_columns(w_up, nseq, nfsdp, mine)
-    down_q = pack_rows(w_down, nseq, mine)
-    mixed, lse, out_w, cot, gate_w = attn_fwd(
-        starts, table, ids, query, keys, values, out_q, out_grad[0], gate_q, nseq, nfsdp
+    query, keys, values, mixed, lse, gains, normed, first, out_w, cot, gate_w, up_q, down_q = front(
+        starts,
+        table,
+        ids,
+        attn_gain[None],
+        mix_gain[None],
+        tokens[0],
+        w_query,
+        w_key,
+        w_value,
+        w_out,
+        w_gate,
+        w_up,
+        w_down,
+        out_grad[0],
+        nseq,
+        nfsdp,
     )
-    mixed_rows, resid, normed_two, up_w, down_w = mix(
-        mixed, out_w, tokens[0], gain_two[None], up_q, down_q, nfsdp
+    out_w = out_w.reshape(nseq, inner, -1)
+    mixed_rows, resid, normed_two, hidden, gate_grad, up_grad, up_w, down_w, down_grad = middle(
+        mixed, out_w, tokens[0], gains, up_q, down_q, gate_w, cot, nfsdp
     )
-    gate_w = gate_w.reshape(width, -1)
-    up_w = up_w.reshape(width, -1)
-    down_w = down_w.reshape(-1, width)
-    gate = dot32(normed_two, gate_w)
-    upward = dot32(normed_two, up_w)
-    active, slope = gelu_both(gate)
-    hidden = (active * upward).astype(BF16)
+    gain_one, gain_two = gains[0], gains[1]
     result = dot32(hidden, down_w).astype(BF16)
-    down_grad = dot_tn(hidden, cot).astype(BF16)
-    hidden_grad = nt(cot, down_w)
-    gate_grad = (hidden_grad * upward * slope).astype(BF16)
-    up_grad = (hidden_grad * active).astype(BF16)
     resid_grad, mixed_grad, out_w_grad, gain_two_grad, down_grad = unmix(
         gate_grad,
         up_grad,
@@ -1102,7 +1312,7 @@
         out_grad[0],
         out_w,
         mixed_rows,
-        blocks(down_grad, nfsdp),
+        down_grad,
     )
     gate_w_grad = dot_tn(normed_two, gate_grad).astype(BF16)
     up_w_grad = dot_tn(normed_two, up_grad).astype(BF16)

time: 566 us -> 510 us (0.901)
  matrix products: 73.6 us -> 26.7 us
  local copies, waits for them, and re-layouts: 61.7 us -> 41.9 us
  Pallas kernels: 407 us -> 421 us
    dot_general x6 -> x1, matrix products: 34.4 us -> 6.8 us  [dot32(): return jnp.dot(a, b, preferred_element_type=F32)]
    pallas_call x1, Pallas kernels: 63.6 us -> 79.6 us  [unmix(): pl.pallas_call(functools.partial(unmix_kernel, chunks), out_shape=(jax.Sh...]
    dot_general x4 -> x3, matrix products: 32.2 us -> 19.9 us  [dot_tn(): lax.dot_general(a, b, (((0,), (0,)), ((), ())), preferred_element_type=F32)]
    unnamed x105 -> x61, local copies, waits for them, and re-layouts: 20 us -> 11.3 us
    reshape x4 -> x0, local copies, waits for them, and re-layouts: 8.5 us -> none  [the longest x2 7.94 us: pack_columns(): w.reshape(depth, nfsdp, block)]
    dot_general x1 -> x0, matrix products: 7.06 us -> none  [nt(): lax.dot_general(a, b, (((1,), (1,)), ((), ())), preferred_element_type=F32)]
    pallas_call x3 -> x2, Pallas kernels: 180 us -> 178 us  [the longest x1 90.1 us: front(): pl.pallas_call(functools.partial(front_kernel, heads, nseq), out_shape=(j...]
where the time goes in v4:
time: 510 us; the launch traced here: 502 us
  Pallas kernels  421 us (83%)
  local copies, waits for them, and re-layouts  41.9 us (8%)
  matrix products  26.7 us (5%)
  other arithmetic  10.7 us (2%)
    pallas_call x1, Pallas kernels, front(): pl.pallas_call(functools.partial(front_kernel, heads, nseq), out_shape=(j...  90.1 us
    pallas_call x1, Pallas kernels, middle(): pl.pallas_call(middle_kernel, out_shape=(jax.ShapeDtypeStruct((nseq, rows...  88.2 us
    pallas_call x1, Pallas kernels, unmix(): pl.pallas_call(functools.partial(unmix_kernel, chunks), out_shape=(jax.Sh...  79.6 us
    pallas_call x1, Pallas kernels, attn_bwd(): pl.pallas_call(functools.partial(attn_bwd_kernel, heads), out_shape=(wide...  61.8 us
    pallas_call x1, Pallas kernels, input_grads(): pl.pallas_call(functools.partial(input_kernel, chunks), out_shape=(jax.Sh...  55.1 us
    pallas_call x1, Pallas kernels, last_sums(): pl.pallas_call(last_kernel, out_shape=(jax.ShapeDtypeStruct((nseq,) + qkv...  46.3 us
    dot_general x3, matrix products, dot_tn(): lax.dot_general(a, b, (((0,), (0,)), ((), ())), preferred_element_type=F32)  19.9 us
    unnamed x61, local copies, waits for them, and re-layouts  11.3 us

profile of v4, /device:TPU:0, one launch (start us, length us, event | category | flops | bytes accessed | tf_op | source)
XLA Modules:
  0.0 501.6 jit_solution(12538786391174381438)
XLA Ops:
  0.7 1.2 broadcast_in_dim.19.gain_a
  1.9 1.2 broadcast_in_dim.20.gain_b
  3.1 0.8 reverse
  4.1 0.7 copy.42.table
  4.7 0.6 broadcast_in_dim.18.ids
  5.4 90.1 %front.1 = (bf16[1536,192]{1,0:T(8,128)(2,1)}, bf16[1536,192]{1,0:T(8,128)(2,1)}, bf16[1536,192]{1,0:T(8,128)(2,1)}, bf16[1536,192]{1,0:T(8,128)(2,1)}, f32[8,15...) custom-call(s32[2]{0:T(128)} %bitcast.88, ...), custom_call_target="tpu_custom_call" | custom-call | tf_op jit(solution)/shard_map/front/pallas_call | solution.py:992
  95.5 1.5 fusion
  96.9 88.2 %middle.1 = (bf16[4,384,192]{2,1,0:T(8,128)(2,1)}, f32[384,1536]{1,0:T(8,128)}, bf16[1536,1536]{1,0:T(8,128)(2,1)}, bf16[1536,1024]{1,0:T(8,128)(2,1)}, bf16[153...) custom-call(bf16[1536,192]{1,0:T(8,128)(2,1)} %get-tuple-element.58., ...), custom_call_target="tpu_custom_call" | custom-call | tf_op jit(solution)/shard_map/middle/pallas_call | solution.py:394
  185.2 79.6 %unmix.1 = (f32[384,1536]{1,0:T(8,128)}, bf16[1536,192]{1,0:T(8,128)(2,1)}, bf16[4,768,384]{2,1,0:T(8,128)(2,1)}, f32[8,1536]{1,0:T(8,128)}, bf16[128,1536]{1,0:T(8,128)(2,1)}) custom-call(bf16[1536,1024]{1,0:T(8,128)(2,1)} %get-tuple-element.65.dg, bf16[1536,1024]{1,0:T(8,128)(2,1)} %get-tuple-element.66.du, ...), custom_call_target="tpu_custom_call" | custom-call | tf_op jit(solution)/shard_map/unmix/pallas_call | solution.py:537
  264.8 9.0 %convolution_convert_fusion.1 = bf16[1536,1024]{1,0:T(8,128)(2,1)} fusion(bf16[1536,1536]{1,0:T(8,128)(2,1)} %get-tuple-element.76, bf16[1536,1024]{1,0:T(8,128)(2,1)S(1)} %copy-done.19), kind=kOutput, calls=%fused_computation.1 | convolution fusion | flops 4833411072 | bytes 11010048 | tf_op jit(solution)/shard_map/dot_general | solution.py:1241
  273.8 6.7 %convolution_convert_fusion.2 = bf16[1536,1024]{1,0:T(8,128)(2,1)} fusion(bf16[1536,1536]{1,0:T(8,128)(2,1)S(1)} %copy-done.22, bf16[1536,1024]{1,0:T(8,128)(2,1)S(1)} %copy-done.18), kind=kOutput, calls=%fused_computation.2 | convolution fusion | flops 4833411072 | bytes 11010048 | tf_op jit(solution)/shard_map/dot_general | solution.py:1241
  280.4 6.8 %convolution_convert_fusion.ypart = bf16[1536,1536]{1,0:T(8,128)(2,1)} fusion(bf16[1536,1024]{1,0:T(8,128)(2,1)S(1)} %copy-done.23, bf16[1024,1536]{1,0:T(8,128)(2,1)S(1)} %copy-done.24), kind=kOutput, calls=%fused_computation | convolution fusion | flops 4834197504 | bytes 11010048 | tf_op jit(solution)/shard_map/dot_general | solution.py:1237
  287.2 61.8 %attend_backward.1 = (f32[1536,192]{1,0:T(8,128)}, f32[1536,192]{1,0:T(8,128)}, f32[1536,192]{1,0:T(8,128)}, f32[3,32,128]{2,1,0:T(8,128)}, bf16[384,1536]{1,0:T...) custom-call(s32[2]{0:T(128)} %bitcast.89, f32[32,3]{1,0:T(8,128)} %copy.42.table, ...), custom_call_target="tpu_custom_call" | custom-call | tf_op jit(solution)/shard_map/attend_backward/pallas_call | solution.py:1185
  349.1 1.0 slice_reduce_fusion
  350.1 1.5 convert.16
  351.6 1.5 convert.17
  353.1 0.1 convert.18
  353.2 2.1 pad_maximum_fusion.dqkv
  355.3 55.1 %input_grads.1 = (bf16[384,1536]{1,0:T(8,128)(2,1)S(1)}, f32[8,1536]{1,0:T(8,128)S(1)}, bf16[192,1024]{1,0:T(8,128)(2,1)S(1)}, bf16[4,128,1536]{2,1,0:T(8,128)(2,1)S(1)}, bf16[4,192,1024]{2,1,0:T(8,128)(2,1)}) custom-call(bf16[1536,576]{1,0:T(8,128)(2,1)} %pad_maximum_fusion.dqkv, bf16[1536,640]{1,0:T(8,128)(2,1)} %get-tuple-element.81.qkv_w, ...), custom_call_target="tpu_custom_call" | custom-call | tf_op jit(solution)/shard_map/input_grads/pallas_call | solution.py:613
  410.4 4.3 convolution_convert_fusion.3
  414.7 2.8 copy.36
  417.5 1.1 copy-done.8
  418.6 1.0 copy-done.12
  419.6 0.8 copy-done.14
  420.4 0.8 copy-done.16
  421.2 46.3 %last_sums.1 = (bf16[4,192,576]{2,1,0:T(8,128)(2,1)S(1)}, bf16[4,96,384]{2,1,0:T(8,128)(2,1)S(1)}, bf16[4,192,1024]{2,1,0:T(8,128)(2,1)S(1)}, f32[56,128]{1,0:T(8,128)S(1)}) custom-call(bf16[8,192,576]{2,1,0:T(8,128)(2,1)S(1)} %bitcast.69, bf16[8,96,384]{2,1,0:T(8,128)(2,1)S(1)} %bitcast.73, bf16[192,1024]{1,0:T(8,128)(2,1)S(1)} %copy-done.12, ...), custom_call_target="tpu_custom_call" | custom-call | tf_op jit(solution)/shard_map/last_sums/pallas_call | solution.py:704
  467.5 0.9 copy-done.7
  468.5 0.7 copy-done.13
  469.2 0.6 reshape.95
  469.8 0.6 dynamic_slice.11
  470.4 0.6 dynamic_slice.10
  471.1 1.0 convert_bitcast_fusion
  472.1 0.9 copy.43
  472.9 2.7 copy.37
  475.6 4.4 copy.38
  480.0 2.8 reshape.96
  482.8 1.2 slice_bitcast_fusion
  484.0 0.4 copy.45
  484.5 0.2 copy_bitcast_fusion
  484.6 0.4 slice_convert_fusion
  485.1 3.2 reshape.99
  488.3 1.8 copy.44
  490.1 0.2 copy_bitcast_fusion.1
  490.3 2.1 slice_convert_fusion.1
  492.4 4.9 reshape.98
  497.3 2.0 slice_convert_fusion.2
  499.4 1.0 copy.50
  500.4 1.0 copy.51
  (56 shorter events, 0.3 us)
Async XLA Ops:
  0.6 2.5 copy-start
  185.1 79.6 %copy-start.19 = (bf16[1536,1024]{1,0:T(8,128)(2,1)S(1)}, bf16[1536,1024]{1,0:T(8,128)(2,1)}, u32[]{:S(2)}) copy-start(bf16[1536,1024]{1,0:T(8,128)(2,1)} %get-tuple-element.66.du) | copy-start | bytes 9437188
  264.8 9.0 %copy-start.18 = (bf16[1536,1024]{1,0:T(8,128)(2,1)S(1)}, bf16[1536,1024]{1,0:T(8,128)(2,1)}, u32[]{:S(2)}) copy-start(bf16[1536,1024]{1,0:T(8,128)(2,1)} %get-tuple-element.65.dg) | copy-start | bytes 9437188
  264.8 9.0 %copy-start.22 = (bf16[1536,1536]{1,0:T(8,128)(2,1)S(1)}, bf16[1536,1536]{1,0:T(8,128)(2,1)}, u32[]{:S(2)}) copy-start(bf16[1536,1536]{1,0:T(8,128)(2,1)} %get-tuple-element.76) | copy-start | bytes 14155780
  273.8 6.7 %copy-start.23 = (bf16[1536,1024]{1,0:T(8,128)(2,1)S(1)}, bf16[1536,1024]{1,0:T(8,128)(2,1)}, u32[]{:S(2)}) copy-start(bf16[1536,1024]{1,0:T(8,128)(2,1)} %get-tuple-element.73) | copy-start | bytes 9437188
  273.8 6.7 %copy-start.24 = (bf16[1024,1536]{1,0:T(8,128)(2,1)S(1)}, bf16[1024,1536]{1,0:T(8,128)(2,1)}, u32[]{:S(2)}) copy-start(bf16[1024,1536]{1,0:T(8,128)(2,1)} %get-tuple-element.74) | copy-start | bytes 9437188
  349.0 4.0 copy-start.20
  353.1 2.2 copy-start.2
  353.1 2.2 copy-start.9
  353.1 2.2 copy-start.10
  353.2 57.2 %slice-start = ((s8[4718592]{0:T(1024)(128)(4,1)}), s8[4194304]{0:T(1024)(128)(4,1)S(1)}, s32[]{:S(2)}) async-start(s8[4718592]{0:T(1024)(128)(4,1)} %bitcast.90), calls=%async_computation | async-start | bytes 8388608
  355.3 55.1 %copy-start.17 = (bf16[1536,576]{1,0:T(8,128)(2,1)S(1)}, bf16[1536,576]{1,0:T(8,128)(2,1)}, u32[]{:S(2)}) copy-start(bf16[1536,576]{1,0:T(8,128)(2,1)} %pad_maximum_fusion.dqkv) | copy-start | bytes 5308420
  355.3 55.1 %slice-start.1 = ((s8[4718592]{0:T(1024)(128)(4,1)}), s8[524288]{0:T(1024)(128)(4,1)S(1)}, s32[]{:S(2)}) async-start(s8[4718592]{0:T(1024)(128)(4,1)} %bitcast.90), calls=%async_computation.1 | async-start | bytes 1048576
  410.4 4.3 copy-start.3
  410.4 4.3 copy-start.5
  410.4 4.3 copy-start.11
  410.4 4.3 copy-start.15
  417.5 1.1 copy-start.8
  418.6 1.0 copy-start.12
  419.6 0.8 copy-start.14
  420.4 0.8 copy-start.16
  467.5 0.9 copy-start.7
  468.5 0.7 copy-start.13
  492.4 4.9 copy-start.4
  497.3 2.1 copy-start.21
  497.3 3.1 copy-start.6
  497.3 4.1 copy-start.1
